TPU v7x, 32 devices: a whole 2x2x4 slice. The times are simulated.
32 devices in a mesh: dp: 8 (over z, y), chan: 4 (over x, core).
Axes of the slice: x: 2, y: 2, z: 4, core: 2. Of those that a mesh axis runs over, the one named last changes fastest.
Arguments:
- block_input: bfloat16 [112, 6, 4, 128], P(None, None, None, 'dp'), may hold values from -8 to 8
- cotangent: bfloat16 [112, 6, 4, 128], P('chan', None, None, 'dp'), may hold values from -8 to 8
- expand_weight: float32 [672, 112], P('chan'), may hold values from -0.5 to 0.5
- expand_weight_first: float32 [672, 112], P('chan'), may hold values from -0.0024414062 to 0.0024414062
- expand_weight_second: float32 [672, 112], P('chan'), may hold values from 2.6e-09 to 1e-08
- expand_gains: float32 [2, 672], P(None, 'chan'), may hold values from 0.5 to 1.5
- expand_gains_first: float32 [2, 672], P(None, 'chan'), may hold values from -0.0024414062 to 0.0024414062
- expand_gains_second: float32 [2, 672], P(None, 'chan'), may hold values from 2.6e-09 to 1e-08
- depth_weight: float32 [25, 672], P(None, 'chan'), may hold values from -1.25 to 1.25
- depth_weight_first: float32 [25, 672], P(None, 'chan'), may hold values from -0.001953125 to 0.001953125
- depth_weight_second: float32 [25, 672], P(None, 'chan'), may hold values from 2e-09 to 7.8e-09
- depth_gains: float32 [2, 672], P(None, 'chan'), may hold values from 0.5 to 1.5
- depth_gains_first: float32 [2, 672], P(None, 'chan'), may hold values from -0.0024414062 to 0.0024414062
- depth_gains_second: float32 [2, 672], P(None, 'chan'), may hold values from 2.6e-09 to 1e-08
- squeeze_weight: float32 [28, 672], P(None, 'chan'), may hold values from -0.25 to 0.25
- squeeze_weight_first: float32 [28, 672], P(None, 'chan'), may hold values from -0.0007324219 to 0.0007324219
- squeeze_weight_second: float32 [28, 672], P(None, 'chan'), may hold values from 2.3e-10 to 9.2e-10
- squeeze_bias: float32 [28], replicated, may hold values from -3 to 3
- squeeze_bias_first: float32 [28], replicated, may hold values from -0.0024414062 to 0.0024414062
- squeeze_bias_second: float32 [28], replicated, may hold values from 2.6e-09 to 1e-08
- excite_weight: float32 [28, 672], P(None, 'chan'), may hold values from -1 to 1
- excite_weight_first: float32 [28, 672], P(None, 'chan'), may hold values from -0.00024414062 to 0.00024414062
- excite_weight_second: float32 [28, 672], P(None, 'chan'), may hold values from 2.6e-11 to 1e-10
- excite_bias: float32 [672], P('chan'), may hold values from -3 to 3
- excite_bias_first: float32 [672], P('chan'), may hold values from -0.0008544922 to 0.0008544922
- excite_bias_second: float32 [672], P('chan'), may hold values from 2.9e-10 to 1.2e-09
- project_weight: float32 [112, 672], P(None, 'chan'), may hold values from -0.25 to 0.25
- project_weight_first: float32 [112, 672], P(None, 'chan'), may hold values from -0.0048828125 to 0.0048828125
- project_weight_second: float32 [112, 672], P(None, 'chan'), may hold values from 1e-08 to 4.1e-08
- project_gains: float32 [2, 112], P(None, 'chan'), may hold values from 0.5 to 1.5
- project_gains_first: float32 [2, 112], P(None, 'chan'), may hold values from -0.0048828125 to 0.0048828125
- project_gains_second: float32 [2, 112], P(None, 'chan'), may hold values from 1e-08 to 4.1e-08
Outputs:
- block_output: bfloat16 [112, 6, 4, 128], P('chan', None, None, 'dp')
- input_grad: float32 [112, 6, 4, 128], P('chan', None, None, 'dp')
- expand_weight_new: float32 [672, 112], P('chan')
- expand_weight_first_new: float32 [672, 112], P('chan')
- expand_weight_second_new: float32 [672, 112], P('chan')
- expand_gains_new: float32 [2, 672], P(None, 'chan')
- expand_gains_first_new: float32 [2, 672], P(None, 'chan')
- expand_gains_second_new: float32 [2, 672], P(None, 'chan')
- depth_weight_new: float32 [25, 672], P(None, 'chan')
- depth_weight_first_new: float32 [25, 672], P(None, 'chan')
- depth_weight_second_new: float32 [25, 672], P(None, 'chan')
- depth_gains_new: float32 [2, 672], P(None, 'chan')
- depth_gains_first_new: float32 [2, 672], P(None, 'chan')
- depth_gains_second_new: float32 [2, 672], P(None, 'chan')
- squeeze_weight_new: float32 [28, 672], P(None, 'chan')
- squeeze_weight_first_new: float32 [28, 672], P(None, 'chan')
- squeeze_weight_second_new: float32 [28, 672], P(None, 'chan')
- squeeze_bias_new: float32 [28], replicated
- squeeze_bias_first_new: float32 [28], replicated
- squeeze_bias_second_new: float32 [28], replicated
- excite_weight_new: float32 [28, 672], P(None, 'chan')
- excite_weight_first_new: float32 [28, 672], P(None, 'chan')
- excite_weight_second_new: float32 [28, 672], P(None, 'chan')
- excite_bias_new: float32 [672], P('chan')
- excite_bias_first_new: float32 [672], P('chan')
- excite_bias_second_new: float32 [672], P('chan')
- project_weight_new: float32 [112, 672], P(None, 'chan')
- project_weight_first_new: float32 [112, 672], P(None, 'chan')
- project_weight_second_new: float32 [112, 672], P(None, 'chan')
- project_gains_new: float32 [2, 112], P(None, 'chan')
- project_gains_first_new: float32 [2, 112], P(None, 'chan')
- project_gains_second_new: float32 [2, 112], P(None, 'chan')
- grad_norm: float32 [], replicated
All inputs are finite; a program needn't handle non-finite values.
Results may differ from a plain program's by a relative error of at most 0.0067.
Values may be sent and summed in bfloat16 or wider, within the bound.
No kernel may reach another device: no remote copies, remote signals or barrier semaphores. Data moves between devices by JAX's collectives and lax.ppermute only.
A program may use at most 64 MiB of HBM per device.

v0:
```python
import jax
import jax.numpy as jnp
from jax import lax
from jax.sharding import PartitionSpec as P

C_IN = 112
KS = 5
HT = 6
WD = 4
STEP = 10


norm_epsilon = 1e-05
beta_first = 0.9
beta_second = 0.999
adam_epsilon = 1e-08
decay_rate = 0.01
clip_limit = 1.0
step_rates = (0.3, 0.6, 0.6, 0.6, 0.12, 0.6, 0.6, 0.6, 0.12, 0.6)
decay_flags = (1.0, 0.0, 1.0, 0.0, 1.0, 0.0, 1.0, 0.0, 1.0, 0.0)
contract_rows = (((0,), (0,)), ((), ()))
contract_cols = (((1,), (1,)), ((), ()))
contract_plain = (((1,), (0,)), ((), ()))


def swish(values):
    return values * jax.nn.sigmoid(values)


def swish_slope(values):
    logistic = jax.nn.sigmoid(values)
    return logistic * (1.0 + values * (1.0 - logistic))


def highest(left, right, numbers):
    return lax.dot_general(
        left, right, numbers, precision=lax.Precision.HIGHEST, preferred_element_type=jnp.float32
    )


def depthwise(activity, kernel):
    half = KS // 2
    padded = jnp.pad(activity, ((0, 0), (half, half), (half, half), (0, 0)))
    result = jnp.zeros_like(activity)
    for row_shift in range(KS):
        for col_shift in range(KS):
            window = padded[:, row_shift : row_shift + HT, col_shift : col_shift + WD, :]
            result = result + kernel[row_shift * KS + col_shift][:, None, None, None] * window
    return result


def depthwise_back(grad_field, activity, kernel):
    half = KS // 2
    padded = jnp.pad(activity, ((0, 0), (half, half), (half, half), (0, 0)))
    grad_padded = jnp.pad(grad_field, ((0, 0), (half, half), (half, half), (0, 0)))
    activity_grad = jnp.zeros_like(activity)
    kernel_rows = []
    for row_shift in range(KS):
        for col_shift in range(KS):
            window = padded[:, row_shift : row_shift + HT, col_shift : col_shift + WD, :]
            kernel_rows.append(jnp.sum(grad_field * window, axis=(1, 2, 3)))
            back_window = grad_padded[
                :,
                2 * half - row_shift : 2 * half - row_shift + HT,
                2 * half - col_shift : 2 * half - col_shift + WD,
                :,
            ]
            activity_grad = (
                activity_grad
                + kernel[row_shift * KS + col_shift][:, None, None, None] * back_window
            )
    return (activity_grad, jnp.stack(kernel_rows))


def adam_step(weight, first_moment, second, gradient, step_rate, decay_flag):
    first_new = beta_first * first_moment + (1.0 - beta_first) * gradient
    second_new = beta_second * second + (1.0 - beta_second) * gradient * gradient
    first_hat = first_new / (1.0 - beta_first**STEP)
    second_hat = second_new / (1.0 - beta_second**STEP)
    weight_new = weight - step_rate * (
        first_hat / (jnp.sqrt(second_hat) + adam_epsilon) + decay_flag * decay_rate * weight
    )
    return (weight_new, first_new, second_new)


def on_device(
    block_input,
    cotangent,
    expand_weight,
    expand_weight_first,
    expand_weight_second,
    expand_gains,
    expand_gains_first,
    expand_gains_second,
    depth_weight,
    depth_weight_first,
    depth_weight_second,
    depth_gains,
    depth_gains_first,
    depth_gains_second,
    squeeze_weight,
    squeeze_weight_first,
    squeeze_weight_second,
    squeeze_bias,
    squeeze_bias_first,
    squeeze_bias_second,
    excite_weight,
    excite_weight_first,
    excite_weight_second,
    excite_bias,
    excite_bias_first,
    excite_bias_second,
    project_weight,
    project_weight_first,
    project_weight_second,
    project_gains,
    project_gains_first,
    project_gains_second,
):
    shards = lax.axis_size("chan")
    position = lax.axis_index("chan")
    segments = block_input.shape[3]
    batch_rows = HT * WD * segments * lax.axis_size("dp")
    narrow = cotangent.shape[0]
    local_channels = expand_weight.shape[0]
    flattened = block_input.reshape(C_IN, -1)
    expand_low = expand_weight.astype(jnp.bfloat16)
    expanded = jnp.dot(expand_low, flattened, preferred_element_type=jnp.float32)
    one_sums, one_squares = lax.psum(
        (jnp.sum(expanded, axis=1), jnp.sum(expanded * expanded, axis=1)), "dp"
    )
    one_average = one_sums / batch_rows
    one_spread = lax.rsqrt(one_squares / batch_rows - one_average * one_average + norm_epsilon)
    one_normal = (expanded - one_average[:, None]) * one_spread[:, None]
    one_before = one_normal * expand_gains[0][:, None] + expand_gains[1][:, None]
    active_one = swish(one_before).reshape(local_channels, HT, WD, segments)
    depth_out = depthwise(active_one, depth_weight).reshape(local_channels, -1)
    two_sums, two_squares = lax.psum(
        (jnp.sum(depth_out, axis=1), jnp.sum(depth_out * depth_out, axis=1)), "dp"
    )
    two_average = two_sums / batch_rows
    two_spread = lax.rsqrt(two_squares / batch_rows - two_average * two_average + norm_epsilon)
    two_normal = (depth_out - two_average[:, None]) * two_spread[:, None]
    two_before = two_normal * depth_gains[0][:, None] + depth_gains[1][:, None]
    active_two = swish(two_before).reshape(local_channels, HT, WD, segments)
    pooled = jnp.mean(active_two, axis=(1, 2))
    squeeze_part = highest(squeeze_weight, pooled, contract_plain)
    squeeze_pre = lax.psum(squeeze_part, "chan") + squeeze_bias[:, None]
    hidden = swish(squeeze_pre)
    gating = jax.nn.sigmoid(highest(excite_weight, hidden, contract_rows) + excite_bias[:, None])
    scaled = (
        (active_two * gating[:, None, None, :]).astype(jnp.bfloat16).reshape(local_channels, -1)
    )
    project_low = project_weight.astype(jnp.bfloat16)
    projected = lax.psum_scatter(
        jnp.dot(project_low, scaled, preferred_element_type=jnp.float32),
        "chan",
        scatter_dimension=0,
        tiled=True,
    )
    three_sums, three_squares = lax.psum(
        (jnp.sum(projected, axis=1), jnp.sum(projected * projected, axis=1)), "dp"
    )
    three_average = three_sums / batch_rows
    three_spread = lax.rsqrt(
        three_squares / batch_rows - three_average * three_average + norm_epsilon
    )
    three_normal = (projected - three_average[:, None]) * three_spread[:, None]
    three_after = three_normal * project_gains[0][:, None] + project_gains[1][:, None]
    own_input = lax.dynamic_slice_in_dim(flattened, position * narrow, narrow, 0).astype(
        jnp.float32
    )
    block_output = (own_input + three_after).astype(jnp.bfloat16).reshape(narrow, HT, WD, segments)
    upstream = cotangent.astype(jnp.float32).reshape(narrow, -1)
    three_beta, three_gamma = lax.psum(
        (jnp.sum(upstream, axis=1), jnp.sum(upstream * three_normal, axis=1)), "dp"
    )
    project_gains_grad = jnp.stack([three_gamma, three_beta])
    three_delta = (project_gains[0] * three_spread)[:, None] * (
        upstream
        - (three_beta / batch_rows)[:, None]
        - three_normal * (three_gamma / batch_rows)[:, None]
    )
    delta_whole = lax.all_gather(three_delta.astype(jnp.bfloat16), "chan", axis=0, tiled=True)
    scaled_grad = lax.dot_general(
        project_low, delta_whole, contract_rows, preferred_element_type=jnp.float32
    )
    project_weight_grad = lax.dot_general(
        delta_whole, scaled, contract_cols, preferred_element_type=jnp.float32
    )
    scaled_four = scaled_grad.reshape(local_channels, HT, WD, segments)
    gating_grad = jnp.sum(scaled_four * active_two, axis=(1, 2))
    excite_delta = gating_grad * gating * (1.0 - gating)
    excite_bias_grad = jnp.sum(excite_delta, axis=1)
    excite_weight_grad = highest(hidden, excite_delta, contract_cols)
    hidden_part = highest(excite_weight, excite_delta, contract_plain)
    hidden_grad = lax.psum(hidden_part, "chan")
    squeeze_delta = hidden_grad * swish_slope(squeeze_pre)
    squeeze_bias_grad = jnp.sum(squeeze_delta, axis=1)
    squeeze_weight_grad = highest(squeeze_delta, pooled, contract_cols)
    pooled_grad = highest(squeeze_weight, squeeze_delta, contract_rows)
    active_grad = scaled_four * gating[:, None, None, :] + pooled_grad[:, None, None, :] / (HT * WD)
    two_delta = active_grad.reshape(local_channels, -1) * swish_slope(two_before)
    two_gamma, two_beta = lax.psum(
        (jnp.sum(two_delta * two_normal, axis=1), jnp.sum(two_delta, axis=1)), "dp"
    )
    depth_gains_grad = jnp.stack([two_gamma, two_beta])
    depth_grad = (depth_gains[0] * two_spread)[:, None] * (
        two_delta
        - (two_beta / batch_rows)[:, None]
        - two_normal * (two_gamma / batch_rows)[:, None]
    )
    active_one_grad, depth_weight_grad = depthwise_back(
        depth_grad.reshape(local_channels, HT, WD, segments), active_one, depth_weight
    )
    one_delta = active_one_grad.reshape(local_channels, -1) * swish_slope(one_before)
    one_gamma, one_beta = lax.psum(
        (jnp.sum(one_delta * one_normal, axis=1), jnp.sum(one_delta, axis=1)), "dp"
    )
    expand_gains_grad = jnp.stack([one_gamma, one_beta])
    expand_delta = (
        (expand_gains[0] * one_spread)[:, None]
        * (
            one_delta
            - (one_beta / batch_rows)[:, None]
            - one_normal * (one_gamma / batch_rows)[:, None]
        )
    ).astype(jnp.bfloat16)
    expand_weight_grad = lax.dot_general(
        expand_delta, flattened, contract_cols, preferred_element_type=jnp.float32
    )
    input_part = lax.psum_scatter(
        lax.dot_general(
            expand_low, expand_delta, contract_rows, preferred_element_type=jnp.float32
        ).astype(jnp.bfloat16),
        "chan",
        scatter_dimension=0,
        tiled=True,
    ).astype(jnp.float32)
    input_grad = (input_part + upstream).reshape(narrow, HT, WD, segments)
    partials = (
        expand_weight_grad,
        depth_weight_grad,
        squeeze_weight_grad,
        excite_weight_grad,
        excite_bias_grad,
        project_weight_grad,
        squeeze_bias_grad,
    )
    gains_square = (
        jnp.sum(expand_gains_grad * expand_gains_grad)
        + jnp.sum(depth_gains_grad * depth_gains_grad)
        + jnp.sum(project_gains_grad * project_gains_grad)
    )
    summed = lax.psum(
        (partials[0], partials[1], partials[2], partials[3], partials[4], partials[5], partials[6]),
        "dp",
    )
    local_square = gains_square + jnp.sum(summed[6] * summed[6]) / shards
    for member in summed[:6]:
        local_square = local_square + jnp.sum(member * member)
    total_square = lax.psum(local_square, "chan")
    grad_norm = jnp.sqrt(total_square)
    factor = clip_limit / jnp.maximum(grad_norm, clip_limit)
    weights = (
        expand_weight,
        expand_gains,
        depth_weight,
        depth_gains,
        squeeze_weight,
        squeeze_bias,
        excite_weight,
        excite_bias,
        project_weight,
        project_gains,
    )
    firsts = (
        expand_weight_first,
        expand_gains_first,
        depth_weight_first,
        depth_gains_first,
        squeeze_weight_first,
        squeeze_bias_first,
        excite_weight_first,
        excite_bias_first,
        project_weight_first,
        project_gains_first,
    )
    seconds = (
        expand_weight_second,
        expand_gains_second,
        depth_weight_second,
        depth_gains_second,
        squeeze_weight_second,
        squeeze_bias_second,
        excite_weight_second,
        excite_bias_second,
        project_weight_second,
        project_gains_second,
    )
    gradients = (
        summed[0],
        expand_gains_grad,
        summed[1],
        depth_gains_grad,
        summed[2],
        summed[6],
        summed[3],
        summed[4],
        summed[5],
        project_gains_grad,
    )
    updated = [
        adam_step(
            weights[entry],
            firsts[entry],
            seconds[entry],
            gradients[entry] * factor,
            step_rates[entry],
            decay_flags[entry],
        )
        for entry in range(10)
    ]
    return (
        block_output,
        input_grad,
        updated[0][0],
        updated[0][1],
        updated[0][2],
        updated[1][0],
        updated[1][1],
        updated[1][2],
        updated[2][0],
        updated[2][1],
        updated[2][2],
        updated[3][0],
        updated[3][1],
        updated[3][2],
        updated[4][0],
        updated[4][1],
        updated[4][2],
        updated[5][0],
        updated[5][1],
        updated[5][2],
        updated[6][0],
        updated[6][1],
        updated[6][2],
        updated[7][0],
        updated[7][1],
        updated[7][2],
        updated[8][0],
        updated[8][1],
        updated[8][2],
        updated[9][0],
        updated[9][1],
        updated[9][2],
        grad_norm,
    )


def solution(mesh):
    return jax.shard_map(
        on_device,
        mesh=mesh,
        in_specs=(
            P(None, None, None, "dp"),
            P("chan", None, None, "dp"),
            P("chan", None),
            P("chan", None),
            P("chan", None),
            P(None, "chan"),
            P(None, "chan"),
            P(None, "chan"),
            P(None, "chan"),
            P(None, "chan"),
            P(None, "chan"),
            P(None, "chan"),
            P(None, "chan"),
            P(None, "chan"),
            P(None, "chan"),
            P(None, "chan"),
            P(None, "chan"),
            P(),
            P(),
            P(),
            P(None, "chan"),
            P(None, "chan"),
            P(None, "chan"),
            P("chan"),
            P("chan"),
            P("chan"),
            P(None, "chan"),
            P(None, "chan"),
            P(None, "chan"),
            P(None, "chan"),
            P(None, "chan"),
            P(None, "chan"),
        ),
        out_specs=(
            P("chan", None, None, "dp"),
            P("chan", None, None, "dp"),
            P("chan", None),
            P("chan", None),
            P("chan", None),
            P(None, "chan"),
            P(None, "chan"),
            P(None, "chan"),
            P(None, "chan"),
            P(None, "chan"),
            P(None, "chan"),
            P(None, "chan"),
            P(None, "chan"),
            P(None, "chan"),
            P(None, "chan"),
            P(None, "chan"),
            P(None, "chan"),
            P(),
            P(),
            P(),
            P(None, "chan"),
            P(None, "chan"),
            P(None, "chan"),
            P("chan"),
            P("chan"),
            P("chan"),
            P(None, "chan"),
            P(None, "chan"),
            P(None, "chan"),
            P(None, "chan"),
            P(None, "chan"),
            P(None, "chan"),
            P(),
        ),
        check_vma=False,
    )
```

profile of v0, /device:TPU:0, one launch (start us, length us, event | category | flops | bytes accessed | tf_op | source)
XLA Modules:
  0.0 292.7 jit_solution(14161792712379678238)
XLA Ops:
  7.3 0.9 fusion.108
  8.2 1.0 fusion.107
  9.2 0.8 fusion.109
  10.7 1.2 fusion.95
  12.0 23.1 %all-reduce.11 = (f32[168]{0:T(256)S(1)}, f32[168]{0:T(256)S(1)}) all-reduce(f32[168]{0:T(256)S(1)} %get-tuple-element.97, f32[168]{0:T(256)S(1)} %get-tuple-element.96), channel_id=1, replica_groups=mesh['dp'=8,'chan'=4] {'dp'}, use_global_device_ids=true, to_apply=%region_3.0 | all-reduce | flops 336 | bytes 2688 | tf_op jit(solution)/shard_map/psum | solution.py:129
  36.3 17.1 %all-reduce.10 = (f32[168]{0:T(256)S(1)}, f32[168]{0:T(256)S(1)}) all-reduce(f32[168]{0:T(256)S(1)} %get-tuple-element.91, f32[168]{0:T(256)S(1)} %get-tuple-element.90), channel_id=1, replica_groups=mesh['dp'=8,'chan'=4] {'dp'}, use_global_device_ids=true, to_apply=%region_7.8 | all-reduce | flops 336 | bytes 2688 | tf_op jit(solution)/shard_map/psum | solution.py:138
  53.7 5.8 %psum.158 = f32[28,16]{0,1:T(8,128)S(1)} all-reduce(f32[28,16]{0,1:T(8,128)S(1)} %convolution_bitcast_fusion.3), channel_id=1, replica_groups=mesh['dp'=8,'chan'=4] {'chan'}, use_global_device_ids=true, to_apply=%region_9.10 | all-reduce | flops 448 | bytes 3584 | tf_op jit(solution)/shard_map/psum | solution.py:148
  60.1 8.8 %fusion = f32[32,384]{1,0:T(8,128)S(1)} fusion(f32[112,384]{1,0:T(8,128)S(1)} %convolution_bitcast_fusion.1), kind=kCustom, calls=%all-reduce-scatter | all-reduce-scatter fusion | flops 49153 | bytes 221696
  69.0 1.3 collective-permute-start
  73.1 19.1 %all-reduce.9 = (f32[28]{0:T(128)S(1)}, f32[28]{0:T(128)S(1)}) all-reduce(f32[28]{0:T(128)S(1)} %get-tuple-element.99, f32[28]{0:T(128)S(1)} %get-tuple-element.98), channel_id=1, replica_groups=mesh['dp'=8,'chan'=4] {'dp'}, use_global_device_ids=true, to_apply=%region_14.15 | all-reduce | flops 56 | bytes 448 | tf_op jit(solution)/shard_map/psum | solution.py:161
  92.5 17.1 %all-reduce.8 = (f32[28]{0:T(128)S(1)}, f32[28]{0:T(128)S(1)}) all-reduce(f32[28]{0:T(128)S(1)} %multiply_reduce_fusion.32, f32[28]{0:T(128)S(1)} %convert_reduce_fusion), channel_id=1, replica_groups=mesh['dp'=8,'chan'=4] {'dp'}, use_global_device_ids=true, to_apply=%region_18.19 | all-reduce | flops 56 | bytes 448 | tf_op jit(solution)/shard_map/psum | solution.py:175
  109.7 5.8 %all-gather = bf16[4,28,384]{2,1,0:T(8,128)(2,1)S(1)} all-gather(bf16[1,28,384]{2,1,0:T(8,128)(2,1)S(1)} %get-tuple-element.158), channel_id=1, replica_groups=mesh['dp'=8,'chan'=4] {'chan'}, dimensions={0}, use_global_device_ids=true | all-gather | bytes 107520 | tf_op jit(solution)/shard_map/all_gather | solution.py:184
  115.5 0.9 fusion.112
  117.4 7.7 %psum.163 = f32[28,16]{0,1:T(8,128)S(1)} all-reduce(f32[28,16]{0,1:T(8,128)S(1)} %convolution_bitcast_fusion.2), channel_id=1, replica_groups=mesh['dp'=8,'chan'=4] {'chan'}, use_global_device_ids=true, to_apply=%region_20.21 | all-reduce | flops 448 | bytes 3584 | tf_op jit(solution)/shard_map/psum | solution.py:197
  126.0 19.1 %all-reduce.7 = (f32[168]{0:T(256)S(1)}, f32[168]{0:T(256)S(1)}) all-reduce(f32[168]{0:T(256)S(1)} %get-tuple-element.95, f32[168]{0:T(256)S(1)} %get-tuple-element.94), channel_id=1, replica_groups=mesh['dp'=8,'chan'=4] {'dp'}, use_global_device_ids=true, to_apply=%region_24.25 | all-reduce | flops 336 | bytes 2688 | tf_op jit(solution)/shard_map/psum | solution.py:204
  147.7 34.2 %all-reduce.6 = (f32[168]{0:T(256)S(1)}, f32[168]{0:T(256)S(1)}, f32[28]{0:T(128)S(1)}, f32[25,168]{1,0:T(8,128)S(1)}, f32[28,168]{1,0:T(8,128)S(1)}, /*index=5*/f32[28,168]{1,0:T(8,128)S(1)}, f32[168]{0:T(256)S(1)}) all-reduce(f32[168]{0:T(256)S(1)} %get-tuple-element.93, ...), channel_id=1, replica_groups=mesh['dp'=8,'chan'=4] {'dp'}, use_global_device_ids=true, to_apply=%region_28.29 | all-reduce | flops 14140 | bytes 113120 | tf_op jit(solution)/shard_map/psum | solution.py:217
  182.1 0.8 fusion.111
  185.6 6.9 %fusion.1 = bf16[32,384]{1,0:T(8,128)(2,1)S(1)} fusion(bf16[112,384]{1,0:T(8,128)(2,1)S(1)} %fusion.2), kind=kCustom, calls=%all-reduce-scatter.1 | all-reduce-scatter fusion | flops 49153 | bytes 111104
  192.5 1.3 collective-permute-start.1
  194.5 0.8 copy.96
  200.3 63.3 %all-reduce.15.cloned.1.call-done = (f32[168,112]{1,0:T(8,128)}, f32[112,168]{0,1:T(8,128)}) async-done(((f32[168,112]{1,0:T(8,128)}, f32[112,168]{0,1:T(8,128)}), (f32[168,112]{1,0:T(8,128)}, f32[112,168]{0,1:T(8,128)})) %all-reduce.15.cloned.1.call-update) | async-done | bytes 150544 | tf_op jit(solution)/shard_map/psum | solution.py:255
  263.6 1.5 multiply_reduce_fusion.30
  265.1 1.5 multiply_reduce_fusion.31
  271.2 6.3 %psum.175 = f32[]{:T(128)} all-reduce(f32[]{:T(128)S(6)} %add.558), channel_id=1, replica_groups=mesh['dp'=8,'chan'=4] {'chan'}, use_global_device_ids=true, to_apply=%region_74.75 | all-reduce | flops 1 | bytes 8 | tf_op jit(solution)/shard_map/psum | solution.py:262
  (152 shorter events, 22.6 us)
Async XLA Ops:
  7.2 256.3 %all-reduce.15.cloned.1.call-start = ((), (), s32[]{:S(2)}) async-start(), calls=%async_computation | async-start | bytes 344064 | tf_op jit(solution)/shard_map/psum | solution.py:255
  36.2 17.3 %copy-start.6 = (f32[28,168]{1,0:T(8,128)S(1)}, f32[28,168]{1,0:T(8,128)}, u32[]{:S(2)}) copy-start(f32[28,168]{1,0:T(8,128)} %param.46) | copy-start | bytes 56452
  36.2 23.3 %copy-start.7 = (f32[28,168]{1,0:T(8,128)S(1)}, f32[28,168]{1,0:T(8,128)}, u32[]{:S(2)}) copy-start(f32[28,168]{1,0:T(8,128)} %param.52) | copy-start | bytes 56452
  36.2 23.3 %copy-start.22 = (f32[28]{0:T(128)S(1)}, f32[28]{0:T(128)}, u32[]{:S(2)}) copy-start(f32[28]{0:T(128)} %param.49) | copy-start | bytes 340
  36.2 23.3 %copy-start.29 = (f32[168]{0:T(256)S(1)}, f32[168]{0:T(256)}, u32[]{:S(2)}) copy-start(f32[168]{0:T(256)} %param.55) | copy-start | bytes 2020
  69.0 3.8 %collective-permute-start = (f32[12,384]{1,0:T(8,128)S(1)}, f32[12,384]{1,0:T(8,128)S(1)}, u32[]{:S(2)}, u32[]{:S(2)}) collective-permute-start(f32[12,384]{1,0:T(8,128)S(1)} %slice.371), channel_id=1, source_target_pairs={{0,1},{1,2},{2,3},{4,5},{5,6},{6,7},{8,9},{9,10},{10,11},{12,13},{... | collective-permute-start | bytes 55304
  192.5 7.1 %collective-permute-start.1 = (bf16[12,384]{1,0:T(8,128)(2,1)S(1)}, bf16[12,384]{1,0:T(8,128)(2,1)S(1)}, u32[]{:S(2)}, u32[]{:S(2)}) collective-permute-start(bf16[12,384]{1,0:T(8,128)(2,1)S(1)} %slice.372), channel_id=1, source_target_pairs={{0,1},{1,2},{2,3},{4,5},{5,6},{6,7},{8,9},{9,10},{10,11},{12,13},{... | collective-permute-start | bytes 27656
  200.0 78.3 %copy-start.33 = (f32[28]{0:T(128)S(1)}, f32[28]{0:T(128)}, u32[]{:S(2)}) copy-start(f32[28]{0:T(128)} %param.50) | copy-start | bytes 340
  200.0 78.3 %copy-start.34 = (f32[28]{0:T(128)S(1)}, f32[28]{0:T(128)}, u32[]{:S(2)}) copy-start(f32[28]{0:T(128)} %param.51) | copy-start | bytes 340
  200.0 78.8 %copy-start.27 = (f32[2,28]{1,0:T(2,128)S(1)}, f32[2,28]{1,0:T(2,128)}, u32[]{:S(2)}) copy-start(f32[2,28]{1,0:T(2,128)} %param.62) | copy-start | bytes 676
  200.0 78.8 %copy-start.28 = (f32[2,28]{1,0:T(2,128)S(1)}, f32[2,28]{1,0:T(2,128)}, u32[]{:S(2)}) copy-start(f32[2,28]{1,0:T(2,128)} %param.63) | copy-start | bytes 676
  200.0 79.4 %copy-start.30 = (f32[168]{0:T(256)S(1)}, f32[168]{0:T(256)}, u32[]{:S(2)}) copy-start(f32[168]{0:T(256)} %param.56) | copy-start | bytes 2020
  200.0 79.4 %copy-start.31 = (f32[168]{0:T(256)S(1)}, f32[168]{0:T(256)}, u32[]{:S(2)}) copy-start(f32[168]{0:T(256)} %param.57) | copy-start | bytes 2020
  200.0 80.0 %copy-start.19 = (f32[2,168]{1,0:T(2,128)S(1)}, f32[2,168]{1,0:T(2,128)}, u32[]{:S(2)}) copy-start(f32[2,168]{1,0:T(2,128)} %param.43) | copy-start | bytes 4036
  200.0 80.0 %copy-start.23 = (f32[2,168]{1,0:T(2,128)S(1)}, f32[2,168]{1,0:T(2,128)}, u32[]{:S(2)}) copy-start(f32[2,168]{1,0:T(2,128)} %param.44) | copy-start | bytes 4036
  200.0 80.0 %copy-start.24 = (f32[2,168]{1,0:T(2,128)S(1)}, f32[2,168]{1,0:T(2,128)}, u32[]{:S(2)}) copy-start(f32[2,168]{1,0:T(2,128)} %param.45) | copy-start | bytes 4036
  200.1 80.6 %copy-start.20 = (f32[2,168]{1,0:T(2,128)S(1)}, f32[2,168]{1,0:T(2,128)}, u32[]{:S(2)}) copy-start(f32[2,168]{1,0:T(2,128)} %param.37) | copy-start | bytes 4036
  200.1 80.6 %copy-start.25 = (f32[2,168]{1,0:T(2,128)S(1)}, f32[2,168]{1,0:T(2,128)}, u32[]{:S(2)}) copy-start(f32[2,168]{1,0:T(2,128)} %param.38) | copy-start | bytes 4036
  200.1 80.5 %copy-start.26 = (f32[2,168]{1,0:T(2,128)S(1)}, f32[2,168]{1,0:T(2,128)}, u32[]{:S(2)}) copy-start(f32[2,168]{1,0:T(2,128)} %param.39) | copy-start | bytes 4036
  200.1 81.1 %copy-start.13 = (f32[28,168]{1,0:T(8,128)S(1)}, f32[28,168]{1,0:T(8,128)}, u32[]{:S(2)}) copy-start(f32[28,168]{1,0:T(8,128)} %param.53) | copy-start | bytes 56452
  200.1 81.1 %copy-start.14 = (f32[28,168]{1,0:T(8,128)S(1)}, f32[28,168]{1,0:T(8,128)}, u32[]{:S(2)}) copy-start(f32[28,168]{1,0:T(8,128)} %param.54) | copy-start | bytes 56452
  265.1 16.8 %copy-start.15 = (f32[28,168]{1,0:T(8,128)S(1)}, f32[28,168]{1,0:T(8,128)}, u32[]{:S(2)}) copy-start(f32[28,168]{1,0:T(8,128)} %param.47) | copy-start | bytes 56452
  265.1 16.8 %copy-start.16 = (f32[28,168]{1,0:T(8,128)S(1)}, f32[28,168]{1,0:T(8,128)}, u32[]{:S(2)}) copy-start(f32[28,168]{1,0:T(8,128)} %param.48) | copy-start | bytes 56452
  270.5 12.1 %copy-start.8 = (f32[25,168]{1,0:T(8,128)S(1)}, f32[25,168]{1,0:T(8,128)}, u32[]{:S(2)}) copy-start(f32[25,168]{1,0:T(8,128)} %param.40) | copy-start | bytes 50404
  (14 other events, 97.0 us)
Sparse Core Ops, SparseCore 0:
  194.0 69.5 all-reduce.14
where the time goes:
time: 294 us; the launch traced here: 293 us
  blocking collectives  171 us (58%)
  waiting for transfers between devices  63.3 us (22%)
  between operations  23.8 us (8%)
  other arithmetic  19.6 us (7%)
  local copies, waits for them, and re-layouts  7.69 us (3%)
  matrix products  4.63 us (2%)
    psum x1, waiting for transfers between devices, on_device(): lax.psum((partials[0], partials[1], partials[2], partials[3], partials[4]...  63.3 us
    psum x1, blocking collectives, on_device(): lax.psum((jnp.sum(one_delta * one_normal, axis=1), jnp.sum(one_delta, axi...  34.2 us
    psum x1, blocking collectives, on_device(): lax.psum((jnp.sum(expanded, axis=1), jnp.sum(expanded * expanded, axis=1)...  23.1 us
    psum x1, blocking collectives, on_device(): lax.psum((jnp.sum(projected, axis=1), jnp.sum(projected * projected, axis...  19.1 us
    psum x1, blocking collectives, on_device(): lax.psum((jnp.sum(two_delta * two_normal, axis=1), jnp.sum(two_delta, axi...  19.1 us
    psum x1, blocking collectives, on_device(): lax.psum((jnp.sum(upstream, axis=1), jnp.sum(upstream * three_normal, axi...  17.1 us
    psum x1, blocking collectives, on_device(): lax.psum((jnp.sum(depth_out, axis=1), jnp.sum(depth_out * depth_out, axis...  17.1 us
    unnamed x2, blocking collectives  15.7 us
  transfers between devices with their start and end apart: 3, of which 1 were waited for; matrix products, arithmetic and copies ran while one was open for 2% of the time, Pallas kernels for 0%

commit v1 on v0

--- a/solution.py
+++ b/solution.py
@@ -1,6 +1,10 @@
+import functools
+
 import jax
 import jax.numpy as jnp
 from jax import lax
+from jax.experimental import pallas as pl
+from jax.experimental.pallas import tpu as pltpu
 from jax.sharding import PartitionSpec as P
 
 C_IN = 112
@@ -358,9 +362,716 @@
     )
 
 
+POSITIONS = HT * WD
+HALF_KS = KS // 2
+PAIR_LANES = 384
+HIDDEN_ROWS = 32
+TAPS = KS * KS
+ROW_SQUEEZE = 32
+ROW_EXCITE = 64
+ROW_EXCITE_BIAS = 96
+ROW_EXPAND_GAINS = 97
+ROW_DEPTH_GAINS = 99
+ROW_PROJECT_GAINS = 101
+STACK_ROWS = 104
+PAIRED_ROWS_LIMIT = 3072
+contract_lanes = (((1,), (1,)), ((), ()))
+f32 = jnp.float32
+bf16 = jnp.bfloat16
+
+
+def paired_fits(mesh):
+    return mesh.shape["chan"] == 4 and mesh.shape["dp"] * POSITIONS * 8 <= PAIRED_ROWS_LIMIT
+
+
+def dot(left, right, numbers):
+    return lax.dot_general(left, right, numbers, preferred_element_type=f32)
+
+
+def rows_sum(values):
+    return jnp.broadcast_to(jnp.sum(values, axis=0, keepdims=True), (8, values.shape[1]))
+
+
+def lane_tile(index, start=0):
+    return pl.ds(pl.multiple_of(start + index * 128, 128), 128)
+
+
+def swish_of_half(half):
+    return half * jnp.tanh(half) + half
+
+
+def slope_of_half(half):
+    bent = jnp.tanh(half)
+    up = 1.0 + bent
+    return 0.5 * up * (1.0 + half * (1.0 - bent))
+
+
+def taps_of(row, col):
+    found = []
+    for i in range(KS):
+        for j in range(KS):
+            r, c = row + i - HALF_KS, col + j - HALF_KS
+            if 0 <= r < HT and 0 <= c < WD:
+                found.append((i * KS + j, r * WD + c))
+    return found
+
+
+def gram_kernel(x_ref, gram_ref):
+    blocks = x_ref.shape[0]
+    flat = x_ref[...].reshape(blocks * x_ref.shape[1], x_ref.shape[2])
+    gram_ref[0:C_IN, :] = dot(flat, flat, contract_rows)
+    ones = jnp.ones((8, flat.shape[0]), bf16)
+    gram_ref[C_IN : C_IN + 8, :] = dot(ones, flat, contract_plain)
+
+
+def expand_kernel(
+    total_rows, gram_own, gram_other, x_ref, we_ref, stack_ref,
+    depth_ref, sums_ref, norm_ref, expanded_scr, taps_scr,
+):
+    blocks = x_ref.shape[0]
+    width = we_ref.shape[0]
+    gram = gram_own[...] + gram_other[...]
+    weights = we_ref[...].astype(f32)
+    average = highest(gram[C_IN : C_IN + 8], weights, contract_lanes) / total_rows
+    turned = highest(weights, gram[0:C_IN], contract_plain)
+    squares = highest(jnp.ones((8, C_IN), f32), turned * weights, contract_lanes) / total_rows
+    spread = lax.rsqrt(squares - average * average + norm_epsilon)
+    gain = stack_ref[ROW_EXPAND_GAINS : ROW_EXPAND_GAINS + 1, :] * spread
+    shift = stack_ref[ROW_EXPAND_GAINS + 1 : ROW_EXPAND_GAINS + 2, :] - average * gain
+    norm_ref[0:8, :] = 0.5 * gain
+    norm_ref[8:16, :] = 0.5 * shift
+    norm_ref[16:24, :] = average
+    norm_ref[24:32, :] = spread
+    for tap in range(TAPS):
+        taps_scr[tap] = jnp.broadcast_to(stack_ref[tap : tap + 1, :], (8, width))
+    sums_ref[...] = jnp.zeros_like(sums_ref)
+
+    def one_block(block, carry):
+        expanded_scr[...] = dot(x_ref[block], we_ref[...], contract_lanes)
+
+        def one_tile(tile, carry):
+            lanes = lane_tile(tile)
+            gain_half = norm_ref[0:8, lanes]
+            shift_half = norm_ref[8:16, lanes]
+            active = [
+                swish_of_half(expanded_scr[8 * at : 8 * at + 8, lanes] * gain_half + shift_half)
+                for at in range(POSITIONS)
+            ]
+            total = jnp.zeros((8, 128), f32)
+            square = jnp.zeros((8, 128), f32)
+            for row in range(HT):
+                for col in range(WD):
+                    at = row * WD + col
+                    value = None
+                    for tap, source in taps_of(row, col):
+                        term = taps_scr[tap, :, lanes] * active[source]
+                        value = term if value is None else value + term
+                    depth_ref[block, 8 * at : 8 * at + 8, lanes] = value
+                    total = total + value
+                    square = square + value * value
+            sums_ref[0:8, lanes] += total
+            sums_ref[8:16, lanes] += square
+            return carry
+
+        return lax.fori_loop(0, width // 128, one_tile, carry)
+
+    lax.fori_loop(0, blocks, one_block, 0)
+
+
+def squeeze_kernel(
+    total_rows, index_ref, depth_ref, sums_own, sums_other, stack_ref, wp_ref, cot_ref, bias_ref,
+    projected_ref, scaled_ref, sums_ref, gate_ref, before_ref, pooled_ref, norm_ref,
+    active_scr, scaled_scr,
+):
+    blocks = depth_ref.shape[0]
+    width = depth_ref.shape[2]
+    own = pl.multiple_of(index_ref[1] // 2 * PAIR_LANES, 128)
+    average = rows_sum(sums_own[0:8] + sums_other[0:8]) / total_rows
+    squares = rows_sum(sums_own[8:16] + sums_other[8:16]) / total_rows
+    spread = lax.rsqrt(squares - average * average + norm_epsilon)
+    gain = stack_ref[ROW_DEPTH_GAINS : ROW_DEPTH_GAINS + 1, :] * spread
+    shift = stack_ref[ROW_DEPTH_GAINS + 1 : ROW_DEPTH_GAINS + 2, :] - average * gain
+    norm_ref[0:8, :] = 0.5 * gain
+    norm_ref[8:16, :] = 0.5 * shift
+    norm_ref[16:24, :] = average
+    norm_ref[24:32, :] = spread
+
+    def pool_block(block, carry):
+        def pool_tile(tile, carry):
+            lanes = lane_tile(tile)
+            gain_half = norm_ref[0:8, lanes]
+            shift_half = norm_ref[8:16, lanes]
+            total = jnp.zeros((8, 128), f32)
+            for at in range(POSITIONS):
+                value = swish_of_half(
+                    depth_ref[block, 8 * at : 8 * at + 8, lanes] * gain_half + shift_half
+                )
+                active_scr[block, 8 * at : 8 * at + 8, lanes] = value
+                total = total + value
+            pooled_ref[pl.ds(pl.multiple_of(block * 8, 8), 8), lanes] = total / POSITIONS
+            return carry
+
+        return lax.fori_loop(0, width // 128, pool_tile, carry)
+
+    lax.fori_loop(0, blocks, pool_block, 0)
+    squeeze = stack_ref[ROW_SQUEEZE : ROW_SQUEEZE + HIDDEN_ROWS, :]
+    excite = stack_ref[ROW_EXCITE : ROW_EXCITE + HIDDEN_ROWS, :]
+    before = highest(pooled_ref[...], squeeze, contract_lanes) + bias_ref[...]
+    before_ref[...] = before
+    hidden = swish_of_half(0.5 * before)
+    raised = highest(hidden, excite, contract_plain)
+    raised = raised + stack_ref[ROW_EXCITE_BIAS : ROW_EXCITE_BIAS + 1, :]
+    gate_ref[...] = 0.5 + 0.5 * jnp.tanh(0.5 * raised)
+    sums_ref[...] = jnp.zeros_like(sums_ref)
+
+    def scale_block(block, carry):
+        for tile in range(width // 128):
+            lanes = slice(tile * 128, tile * 128 + 128)
+            gate = gate_ref[pl.ds(pl.multiple_of(block * 8, 8), 8), lanes]
+            value = active_scr[block, :, lanes].reshape(POSITIONS, 8, 128) * gate[None]
+            scaled_scr[:, lanes] = value.reshape(POSITIONS * 8, 128).astype(bf16)
+        projected = dot(scaled_scr[...], wp_ref[...], contract_plain)
+        projected_ref[block] = projected
+        scaled_ref[block] = scaled_scr[:, pl.ds(own, PAIR_LANES)]
+        shaped = projected.reshape(POSITIONS, 8, C_IN)
+        upstream = cot_ref[block].astype(f32).reshape(POSITIONS, 8, C_IN)
+        sums_ref[0:8, :] += jnp.sum(shaped, axis=0)
+        sums_ref[8:16, :] += jnp.sum(shaped * shaped, axis=0)
+        sums_ref[16:24, :] += jnp.sum(shaped * upstream, axis=0)
+        sums_ref[24:32, :] += jnp.sum(upstream, axis=0)
+        return carry
+
+    lax.fori_loop(0, blocks, scale_block, 0)
+
+
+def gate_back_kernel(
+    total_rows, index_ref, projected_ref, cot_ref, sums_own, sums_other, gains_ref, depth_ref,
+    norm_ref, stack_ref, wp_ref, gate_ref, before_ref, pooled_ref, scaled_ref, x_ref,
+    two_ref, sums_ref, project_ref, lanes_ref, bias_ref, gains_grad_ref, output_ref,
+    delta_scr, grad_scr, gate_grad_scr, pooled_scr,
+):
+    blocks = depth_ref.shape[0]
+    width = depth_ref.shape[2]
+    own = pl.multiple_of(index_ref[1] // 2 * PAIR_LANES, 128)
+    own_lanes = pl.ds(own, PAIR_LANES)
+    sums = [rows_sum(sums_own[8 * k : 8 * k + 8] + sums_other[8 * k : 8 * k + 8])[0:1] for k in range(4)]
+    average = sums[0] / total_rows
+    spread = lax.rsqrt(sums[1] / total_rows - average * average + norm_epsilon)
+    beta = sums[3]
+    gamma = spread * (sums[2] - average * beta)
+    gains_grad_ref[0:1, :] = gamma
+    gains_grad_ref[1:2, :] = beta
+    gain = gains_ref[0:1, :]
+    shift = gains_ref[1:2, :]
+    mine = index_ref[0]
+    output_ref[...] = (
+        x_ref[mine].astype(f32) + (projected_ref[mine] - average) * spread * gain + shift
+    ).astype(output_ref.dtype)
+    outer = gain * spread
+
+    def back_block(block, carry):
+        normal = (projected_ref[block] - average) * spread
+        delta = outer * (
+            cot_ref[block].astype(f32) - beta / total_rows - normal * (gamma / total_rows)
+        )
+        delta_scr[block] = delta.astype(bf16)
+        grad_scr[...] = dot(delta_scr[block], wp_ref[...], contract_lanes)
+        two_ref[block] = grad_scr[:, own_lanes]
+
+        def gate_tile(tile, carry):
+            lanes = lane_tile(tile)
+            gain_half = norm_ref[0:8, lanes]
+            shift_half = norm_ref[8:16, lanes]
+            total = jnp.zeros((8, 128), f32)
+            for at in range(POSITIONS):
+                active = swish_of_half(
+                    depth_ref[block, 8 * at : 8 * at + 8, lanes] * gain_half + shift_half
+                )
+                total = total + active * grad_scr[8 * at : 8 * at + 8, lanes]
+            gate_grad_scr[pl.ds(pl.multiple_of(block * 8, 8), 8), lanes] = total
+            return carry
+
+        return lax.fori_loop(0, width // 128, gate_tile, carry)
+
+    lax.fori_loop(0, blocks, back_block, 0)
+    excite = stack_ref[ROW_EXCITE : ROW_EXCITE + HIDDEN_ROWS, :]
+    gate = gate_ref[...]
+    gate_grad_scr[...] = gate_grad_scr[...] * gate * (1.0 - gate)
+    half = 0.5 * before_ref[...]
+    hidden = swish_of_half(half)
+    squeeze_delta = highest(gate_grad_scr[...], excite, contract_lanes) * slope_of_half(half)
+    own_delta = gate_grad_scr[:, own_lanes]
+    lanes_ref[0:HIDDEN_ROWS, :] = highest(squeeze_delta, pooled_ref[:, own_lanes], contract_rows)
+    lanes_ref[HIDDEN_ROWS : 2 * HIDDEN_ROWS, :] = highest(hidden, own_delta, contract_rows)
+    lanes_ref[2 * HIDDEN_ROWS : 2 * HIDDEN_ROWS + 8, :] = rows_sum(own_delta)
+    bias_ref[...] = rows_sum(squeeze_delta)
+    squeeze = stack_ref[ROW_SQUEEZE : ROW_SQUEEZE + HIDDEN_ROWS, own_lanes]
+    pooled_scr[...] = highest(squeeze_delta, squeeze, contract_plain) / POSITIONS
+    sums_ref[...] = jnp.zeros_like(sums_ref)
+
+    def two_block(block, carry):
+        rows = pl.ds(pl.multiple_of(block * 8, 8), 8)
+
+        def two_tile(tile, carry):
+            lanes = lane_tile(tile)
+            whole = lane_tile(tile, own)
+            gain_half = norm_ref[0:8, whole]
+            shift_half = norm_ref[8:16, whole]
+            average = norm_ref[16:24, whole]
+            gate = gate_ref[rows, whole]
+            pooled_grad = pooled_scr[rows, lanes]
+            total = jnp.zeros((8, 128), f32)
+            product = jnp.zeros((8, 128), f32)
+            for at in range(POSITIONS):
+                spot = slice(8 * at, 8 * at + 8)
+                depth = depth_ref[block, spot, whole]
+                value = two_ref[block, spot, lanes] * gate + pooled_grad
+                value = value * slope_of_half(depth * gain_half + shift_half)
+                two_ref[block, spot, lanes] = value
+                total = total + value
+                product = product + value * (depth - average)
+            sums_ref[0:8, lanes] += total
+            sums_ref[8:16, lanes] += product
+            return carry
+
+        return lax.fori_loop(0, PAIR_LANES // 128, two_tile, carry)
+
+    lax.fori_loop(0, blocks, two_block, 0)
+    rows = blocks * POSITIONS * 8
+    project_ref[...] = dot(
+        scaled_ref[...].reshape(rows, PAIR_LANES), delta_scr[...].reshape(rows, C_IN), contract_rows
+    )
+
+
+def depth_back_kernel(
+    total_rows, index_ref, sums_own, sums_other, two_ref, depth_ref, x_ref, we_ref, stack_ref,
+    norm_one_ref, norm_two_ref,
+    one_ref, sums_ref, kernel_ref, gains_grad_ref, expanded_scr, taps_scr, kernel_scr, factors_scr,
+):
+    blocks = depth_ref.shape[0]
+    own = pl.multiple_of(index_ref[1] // 2 * PAIR_LANES, 128)
+    own_lanes = pl.ds(own, PAIR_LANES)
+    spread = norm_two_ref[24:32, own_lanes]
+    average = norm_two_ref[16:24, own_lanes]
+    beta = rows_sum(sums_own[0:8] + sums_other[0:8])
+    gamma = rows_sum(sums_own[8:16] + sums_other[8:16]) * spread
+    gains_grad_ref[0:1, :] = gamma[0:1]
+    gains_grad_ref[1:2, :] = beta[0:1]
+    outer = stack_ref[ROW_DEPTH_GAINS : ROW_DEPTH_GAINS + 1, own_lanes] * spread
+    slope = outer * spread * gamma / total_rows
+    factors_scr[0:8, :] = outer
+    factors_scr[8:16, :] = slope
+    factors_scr[16:24, :] = outer * (beta / total_rows)
+    for tap in range(TAPS):
+        taps_scr[tap] = jnp.broadcast_to(stack_ref[tap : tap + 1, own_lanes], (8, PAIR_LANES))
+    sums_ref[...] = jnp.zeros_like(sums_ref)
+    kernel_scr[...] = jnp.zeros_like(kernel_scr)
+    own_weights = we_ref[own_lanes, :]
+
+    def one_block(block, carry):
+        expanded_scr[...] = dot(x_ref[block], own_weights, contract_lanes)
+
+        def one_tile(tile, carry):
+            lanes = lane_tile(tile)
+            whole = lane_tile(tile, own)
+            gain_half = norm_one_ref[0:8, whole]
+            shift_half = norm_one_ref[8:16, whole]
+            average_one = norm_one_ref[16:24, whole]
+            average_two = norm_two_ref[16:24, whole]
+            outer = factors_scr[0:8, lanes]
+            slope = factors_scr[8:16, lanes]
+            level = factors_scr[16:24, lanes]
+            grads = []
+            active = []
+            for at in range(POSITIONS):
+                spot = slice(8 * at, 8 * at + 8)
+                grads.append(
+                    outer * two_ref[block, spot, lanes]
+                    - level
+                    - slope * (depth_ref[block, spot, whole] - average_two)
+                )
+                active.append(swish_of_half(expanded_scr[spot, lanes] * gain_half + shift_half))
+            pairs = {}
+            for row in range(HT):
+                for col in range(WD):
+                    for tap, source in taps_of(row, col):
+                        pairs.setdefault(tap, []).append((row * WD + col, source))
+            for tap in range(TAPS):
+                value = None
+                for target, source in pairs[tap]:
+                    term = grads[target] * active[source]
+                    value = term if value is None else value + term
+                kernel_scr[tap, :, lanes] += value
+            back = {}
+            for tap in range(TAPS):
+                for target, source in pairs[tap]:
+                    back.setdefault(source, []).append((tap, target))
+            total = jnp.zeros((8, 128), f32)
+            product = jnp.zeros((8, 128), f32)
+            for at in range(POSITIONS):
+                spot = slice(8 * at, 8 * at + 8)
+                value = None
+                for tap, target in back[at]:
+                    term = taps_scr[tap, :, lanes] * grads[target]
+                    value = term if value is None else value + term
+                expanded = expanded_scr[spot, lanes]
+                value = value * slope_of_half(expanded * gain_half + shift_half)
+                one_ref[block, spot, lanes] = value
+                total = total + value
+                product = product + value * (expanded - average_one)
+            sums_ref[0:8, lanes] += total
+            sums_ref[8:16, lanes] += product
+            return carry
+
+        return lax.fori_loop(0, PAIR_LANES // 128, one_tile, carry)
+
+    lax.fori_loop(0, blocks, one_block, 0)
+    kernel_ref[...] = jnp.zeros_like(kernel_ref)
+    for tap in range(TAPS):
+        kernel_ref[tap : tap + 1, :] = jnp.sum(kernel_scr[tap], axis=0, keepdims=True)
+
+
+def expand_back_kernel(
+    total_rows, index_ref, sums_own, sums_other, one_ref, x_ref, we_ref, stack_ref, norm_ref,
+    expand_ref, input_ref, gains_grad_ref, delta_scr,
+):
+    blocks = x_ref.shape[0]
+    own = pl.multiple_of(index_ref[1] // 2 * PAIR_LANES, 128)
+    own_lanes = pl.ds(own, PAIR_LANES)
+    spread = norm_ref[24:32, own_lanes]
+    average = norm_ref[16:17, own_lanes]
+    beta = rows_sum(sums_own[0:8] + sums_other[0:8])
+    gamma = rows_sum(sums_own[8:16] + sums_other[8:16]) * spread
+    gains_grad_ref[0:1, :] = gamma[0:1]
+    gains_grad_ref[1:2, :] = beta[0:1]
+    outer = stack_ref[ROW_EXPAND_GAINS : ROW_EXPAND_GAINS + 1, own_lanes] * spread[0:1]
+    slope = outer * spread[0:1] * gamma[0:1] / total_rows
+    level = outer * (beta[0:1] / total_rows)
+    own_weights = we_ref[own_lanes, :]
+
+    def one_block(block, carry):
+        expanded = dot(x_ref[block], own_weights, contract_lanes)
+        delta = outer * one_ref[block] - level - slope * (expanded - average)
+        delta_scr[block] = delta.astype(bf16)
+        return carry
+
+    lax.fori_loop(0, blocks, one_block, 0)
+    rows = blocks * POSITIONS * 8
+    expand_ref[...] = dot(
+        delta_scr[...].reshape(rows, PAIR_LANES), x_ref[...].reshape(rows, C_IN), contract_rows
+    )
+    input_ref[...] = dot(delta_scr[index_ref[0]], own_weights, contract_plain)
+
+
+def call(kernel, outs, operands, scratch=(), name=None):
+    spaces = [
+        pl.BlockSpec(memory_space=pltpu.SMEM)
+        if operand.dtype == jnp.int32
+        else pl.BlockSpec(memory_space=pltpu.VMEM)
+        for operand in operands
+    ]
+    return pl.pallas_call(
+        kernel,
+        out_shape=[jax.ShapeDtypeStruct(shape, dtype) for shape, dtype in outs],
+        in_specs=spaces,
+        out_specs=[pl.BlockSpec(memory_space=pltpu.VMEM)] * len(outs),
+        scratch_shapes=[pltpu.VMEM(shape, dtype) for shape, dtype in scratch],
+        compiler_params=pltpu.CompilerParams(vmem_limit_bytes=56 * 1024 * 1024),
+        name=name,
+    )(*operands)
+
+
+def settle_kernel(
+    index_ref, expand_own, expand_other, project_own, project_other, lanes_own, lanes_other,
+    kernel_own, kernel_other, bias_own, bias_other, three_ref, two_ref, one_ref, input_own, input_other,
+    expand_ref, project_ref, lanes_ref, bias_ref, square_ref, input_ref,
+):
+    first = index_ref[1] % 2 == 0
+    rows = expand_ref.shape[0]
+    mine = pl.ds(pl.multiple_of(index_ref[1] % 2 * rows, 8), rows)
+    total = jnp.zeros((1, 1), f32)
+
+    def squared(values):
+        return jnp.sum(jnp.sum(values * values, axis=0, keepdims=True), axis=1, keepdims=True)
+
+    for own, other, out in (
+        (expand_own, expand_other, expand_ref),
+        (project_own, project_other, project_ref),
+    ):
+        total = total + squared(own[...] + other[...])
+        out[...] = own[mine, :] + other[mine, :]
+
+    def keep(start, values):
+        lanes_ref[start : start + values.shape[0], :] = jnp.where(
+            first, values[:, 0:rows], values[:, rows : 2 * rows]
+        )
+
+    summed = lanes_own[...] + lanes_other[...]
+    summed = summed[0 : 2 * HIDDEN_ROWS + 1]
+    kernel = kernel_own[...] + kernel_other[...]
+    total = total + squared(summed) + squared(kernel)
+    keep(0, kernel)
+    keep(ROW_SQUEEZE, summed)
+    for start, ref in ((ROW_EXPAND_GAINS, one_ref), (ROW_DEPTH_GAINS, two_ref)):
+        values = ref[0:2, :]
+        total = total + squared(values)
+        keep(start, values)
+    bias = bias_own[0:1, :] + bias_other[0:1, :]
+    bias_ref[...] = bias
+    square_ref[0:8, :] = jnp.broadcast_to(total, (8, 128))
+    square_ref[8:16, :] = jnp.broadcast_to(squared(bias) + squared(three_ref[0:2, :]), (8, 128))
+    input_ref[...] = input_own[...] + input_other[...].astype(f32)
+
+
+def adam_kernel(
+    index_ref, square_own, square_other, expand_grad, project_grad, lanes_grad, bias_grad, three_grad,
+    input_own, input_other, output_own, output_other, cot_ref, *refs,
+):
+    first = index_ref[1] % 2 == 0
+    params, outs = refs[:30], refs[30:]
+    narrow = cot_ref.shape[2]
+    total = square_own[0:1, 0:1] + square_other[0:1, 0:1] + square_own[8:9, 0:1]
+    grad_norm = jnp.sqrt(total)
+    factor = clip_limit / jnp.maximum(grad_norm, clip_limit)
+    outs[32][...] = grad_norm
+    pick = (
+        lax.broadcasted_iota(jnp.int32, (C_IN, narrow), 0)
+        == lax.broadcasted_iota(jnp.int32, (C_IN, narrow), 1) + index_ref[1] * narrow
+    ).astype(f32)
+
+    def halves(own, other):
+        mine = highest(own[...].astype(f32), pick, contract_plain).reshape(POSITIONS, 8, narrow)
+        theirs = highest(other[...].astype(f32), pick, contract_plain).reshape(POSITIONS, 8, narrow)
+        return jnp.concatenate(
+            [jnp.where(first, mine, theirs), jnp.where(first, theirs, mine)], axis=1
+        )
+
+    outs[0][...] = halves(output_own, output_other).astype(bf16)
+    outs[1][...] = halves(input_own, input_other) + cot_ref[...].astype(f32)
+    gradients = (
+        expand_grad[...],
+        lanes_grad[ROW_EXPAND_GAINS : ROW_EXPAND_GAINS + 2, :],
+        lanes_grad[0:TAPS, :],
+        lanes_grad[ROW_DEPTH_GAINS : ROW_DEPTH_GAINS + 2, :],
+        lanes_grad[ROW_SQUEEZE : ROW_SQUEEZE + params[12].shape[0], :],
+        bias_grad[:, 0 : params[15].shape[1]],
+        lanes_grad[ROW_EXCITE : ROW_EXCITE + params[18].shape[0], :],
+        lanes_grad[ROW_EXCITE_BIAS : ROW_EXCITE_BIAS + 1, :],
+        project_grad[...],
+        highest(three_grad[0:2, :], pick, contract_plain),
+    )
+    for entry in range(10):
+        updated = adam_step(
+            params[3 * entry][...],
+            params[3 * entry + 1][...],
+            params[3 * entry + 2][...],
+            gradients[entry] * factor,
+            step_rates[entry],
+            decay_flags[entry],
+        )
+        for part in range(3):
+            outs[2 + 3 * entry + part][...] = updated[part]
+
+
+def on_device_paired(*arrays):
+    block_input, cotangent = arrays[:2]
+    (
+        expand_weight, expand_gains, depth_weight, depth_gains, squeeze_weight,
+        squeeze_bias, excite_weight, excite_bias, project_weight, project_gains,
+    ) = arrays[2::3]
+    segments = block_input.shape[3]
+    if segments != 16:
+        return on_device(*arrays)
+    shards = lax.axis_size("dp")
+    position = lax.axis_index("chan")
+    core = position % 2
+    index = jnp.stack([lax.axis_index("dp"), position]).astype(jnp.int32)
+    total_rows = float(POSITIONS * segments * shards)
+    narrow = cotangent.shape[0]
+    channels = expand_weight.shape[0]
+    hidden_units = squeeze_weight.shape[0]
+    rows = POSITIONS * 8
+    width = 2 * PAIR_LANES
+
+    def swap(values, mask):
+        return lax.ppermute(values, "chan", [(at, at ^ mask) for at in range(4)])
+
+    def spread(values):
+        copies = jnp.broadcast_to(values[None], (shards,) + values.shape)
+        return lax.all_to_all(copies, "dp", 0, 0).reshape(shards, rows, C_IN)
+
+    def whole(own, others):
+        distance = [position ^ place for place in range(4)]
+        return [
+            jnp.where(
+                at == 0, own, jnp.where(at == 1, others[0], jnp.where(at == 2, others[1], others[2]))
+            )
+            for at in distance
+        ]
+
+    def gather(values):
+        return whole(values, [swap(values, mask) for mask in (1, 2, 3)])
+
+    input_rows = jnp.transpose(block_input, (1, 2, 3, 0)).reshape(POSITIONS, segments, C_IN)
+    cot_rows = jnp.transpose(cotangent, (1, 2, 3, 0)).reshape(POSITIONS, segments, narrow)
+    x = spread(lax.dynamic_slice_in_dim(input_rows, core * 8, 8, 1))
+
+    def padded(values, count):
+        return jnp.pad(values, ((0, count - values.shape[0]), (0, channels - values.shape[1])))
+
+    stack = jnp.concatenate(
+        [
+            padded(depth_weight, 32),
+            padded(squeeze_weight, HIDDEN_ROWS),
+            padded(excite_weight, HIDDEN_ROWS),
+            excite_bias[None],
+            expand_gains,
+            depth_gains,
+            padded(project_gains, 3),
+        ],
+        axis=0,
+    )
+    matrices = jnp.concatenate([expand_weight, project_weight.T], axis=0).astype(bf16)
+    stacks = gather(stack)
+    pairs = gather(matrices)
+    kept = lax.dynamic_slice_in_dim(cot_rows, core * 8, 8, 1)
+    sent = lax.dynamic_slice_in_dim(cot_rows, 8 - core * 8, 8, 1)
+    cots = whole(kept, [swap(sent, 1), swap(kept, 2), swap(sent, 3)])
+    cot = spread(jnp.concatenate(cots, axis=2))
+    gap = jnp.zeros((PAIR_LANES - 2 * channels, C_IN), bf16)
+    expand_all = jnp.concatenate(
+        [pairs[0][:channels], pairs[1][:channels], gap, pairs[2][:channels], pairs[3][:channels], gap]
+    )
+    project_all = jnp.concatenate(
+        [pairs[0][channels:], pairs[1][channels:], gap, pairs[2][channels:], pairs[3][channels:], gap]
+    )
+    side = jnp.zeros((STACK_ROWS, PAIR_LANES - 2 * channels), f32)
+    stack_all = jnp.concatenate([stacks[0], stacks[1], side, stacks[2], stacks[3], side], axis=1)
+    gains_all = jnp.concatenate(
+        [part[ROW_PROJECT_GAINS : ROW_PROJECT_GAINS + 2, :narrow] for part in stacks], axis=1
+    )
+    bias_row = jnp.pad(squeeze_bias, (0, HIDDEN_ROWS - hidden_units))[None]
+
+    (gram,) = call(gram_kernel, [((C_IN + 8, C_IN), f32)], [x], name="gram")
+    depth, sums, norm_one = call(
+        functools.partial(expand_kernel, total_rows),
+        [((shards, rows, width), f32), ((16, width), f32), ((32, width), f32)],
+        [gram, swap(gram, 1), x, expand_all, stack_all],
+        [((rows, width), f32), ((TAPS, 8, width), f32)],
+        name="expand",
+    )
+    projected, scaled, sums, gate, before, pooled, norm_two = call(
+        functools.partial(squeeze_kernel, total_rows),
+        [
+            ((shards, rows, C_IN), f32),
+            ((shards, rows, PAIR_LANES), bf16),
+            ((32, C_IN), f32),
+            ((shards * 8, width), f32),
+            ((shards * 8, HIDDEN_ROWS), f32),
+            ((shards * 8, width), f32),
+            ((32, width), f32),
+        ],
+        [index, depth, sums, swap(sums, 1), stack_all, project_all, cot, bias_row],
+        [((shards, rows, width), f32), ((rows, width), bf16)],
+        name="squeeze",
+    )
+    two, sums, project_grad, lanes_grad, bias_grad, three_grad, output = call(
+        functools.partial(gate_back_kernel, total_rows),
+        [
+            ((shards, rows, PAIR_LANES), f32),
+            ((16, PAIR_LANES), f32),
+            ((PAIR_LANES, C_IN), f32),
+            ((2 * HIDDEN_ROWS + 8, PAIR_LANES), f32),
+            ((8, HIDDEN_ROWS), f32),
+            ((2, C_IN), f32),
+            ((rows, C_IN), bf16),
+        ],
+        [
+            index, projected, cot, sums, swap(sums, 1), gains_all, depth, norm_two, stack_all,
+            project_all, gate, before, pooled, scaled, x,
+        ],
+        [
+            ((shards, rows, C_IN), bf16),
+            ((rows, width), f32),
+            ((shards * 8, width), f32),
+            ((shards * 8, PAIR_LANES), f32),
+        ],
+        name="gate_back",
+    )
+    sums_other = swap(sums, 1)
+    early = [swap(project_grad, 1), swap(lanes_grad, 1), swap(bias_grad, 1), swap(output, 1)]
+    one, sums, kernel_grad, two_grad = call(
+        functools.partial(depth_back_kernel, total_rows),
+        [
+            ((shards, rows, PAIR_LANES), f32),
+            ((16, PAIR_LANES), f32),
+            ((32, PAIR_LANES), f32),
+            ((2, PAIR_LANES), f32),
+        ],
+        [index, sums, sums_other, two, depth, x, expand_all, stack_all, norm_one, norm_two],
+        [
+            ((rows, PAIR_LANES), f32),
+            ((TAPS, 8, PAIR_LANES), f32),
+            ((TAPS, 8, PAIR_LANES), f32),
+            ((24, PAIR_LANES), f32),
+        ],
+        name="depth_back",
+    )
+    expand_grad, input_part, one_grad = call(
+        functools.partial(expand_back_kernel, total_rows),
+        [((PAIR_LANES, C_IN), f32), ((rows, C_IN), f32), ((2, PAIR_LANES), f32)],
+        [index, sums, swap(sums, 1), one, x, expand_all, stack_all, norm_one],
+        [((shards, rows, PAIR_LANES), bf16)],
+        name="expand_back",
+    )
+    expand_own, project_own, lanes_own, bias_own, square, input_half = call(
+        settle_kernel,
+        [
+            ((channels, C_IN), f32),
+            ((channels, C_IN), f32),
+            ((STACK_ROWS, channels), f32),
+            ((1, HIDDEN_ROWS), f32),
+            ((16, 128), f32),
+            ((rows, C_IN), f32),
+        ],
+        [
+            index, expand_grad, swap(expand_grad, 1), project_grad, early[0], lanes_grad, early[1],
+            kernel_grad, swap(kernel_grad, 1), bias_grad, early[2], three_grad, two_grad, one_grad,
+            input_part, swap(input_part.astype(bf16), 2),
+        ],
+        name="settle",
+    )
+    params = list(arrays[2:])
+    for at in (15, 16, 17, 21, 22, 23):
+        params[at] = params[at][None]
+    for at in (24, 25, 26):
+        params[at] = params[at].T
+    updated = call(
+        adam_kernel,
+        [((POSITIONS, segments, narrow), bf16), ((POSITIONS, segments, narrow), f32)]
+        + [(value.shape, f32) for value in params]
+        + [((1, 1), f32)],
+        [
+            index, square, swap(square, 2), expand_own, project_own, lanes_own, bias_own, three_grad,
+            input_half, swap(input_half, 1), output, early[3], cot_rows, *params,
+        ],
+        name="adam",
+    )
+    results = list(updated)
+    for at in (0, 1):
+        results[at] = jnp.transpose(results[at].reshape(HT, WD, segments, narrow), (3, 0, 1, 2))
+    for at in (17, 18, 19, 23, 24, 25):
+        results[at] = results[at][0]
+    for at in (26, 27, 28):
+        results[at] = results[at].T
+    results[32] = results[32][0, 0]
+    return tuple(results)
+
+
 def solution(mesh):
+    body = on_device_paired if paired_fits(mesh) else on_device
     return jax.shard_map(
-        on_device,
+        body,
         mesh=mesh,
         in_specs=(
             P(None, None, None, "dp"),

time: 294 us -> 118 us (0.40)
  blocking collectives: 171 us -> 0 us
  Pallas kernels: 0 us -> 58.3 us
  waiting for transfers between devices: 63.3 us -> 16.6 us
  between operations: 23.8 us -> 0.97 us
  starting transfers between devices: 2.64 us -> 24 us
  other arithmetic: 19.6 us -> 4.39 us
  local copies, waits for them, and re-layouts: 7.69 us -> 12.9 us
  matrix products: 4.63 us -> 0 us
    psum x9 -> x0, blocking collectives: 150 us -> none  [the longest x1 34.2 us: on_device(): lax.psum((jnp.sum(one_delta * one_normal, axis=1), jnp.sum(one_delta, axi...]
    psum x1 -> x0, waiting for transfers between devices: 63.3 us -> none  [on_device(): lax.psum((partials[0], partials[1], partials[2], partials[3], partials[4]...]
    pallas_call x0 -> x8, Pallas kernels: none -> 58.3 us  [call(): pl.pallas_call(kernel, out_shape=[jax.ShapeDtypeStruct(shape, dtype) for...]
    ppermute x0 -> x23, waiting for transfers between devices: none -> 16.6 us  [swap(): return lax.ppermute(values, 'chan', [(at, at ^ mask) for at in range(4)])]
    unnamed x2 -> x0, blocking collectives: 15.7 us -> none
    ppermute x0 -> x23, starting transfers between devices: none -> 12.2 us  [swap(): return lax.ppermute(values, 'chan', [(at, at ^ mask) for at in range(4)])]
    all_to_all x0 -> x2, starting transfers between devices: none -> 11.8 us  [spread(): return lax.all_to_all(copies, 'dp', 0, 0).reshape(shards, rows, C_IN)]
    reduce_sum x23 -> x0, other arithmetic: 11.1 us -> none  [the longest x6 5.46 us: on_device(): local_square = local_square + jnp.sum(member * member)]
  transfers between devices with their start and end apart: 3 -> 25, of which waited for: 1 -> 9; matrix products, arithmetic and copies ran while one was open for 2% -> 9% of each run, Pallas kernels for 0% -> 17%
where the time goes in v1:
time: 118 us; the launch traced here: 117 us
  Pallas kernels  58.3 us (49%)
  starting transfers between devices  24 us (20%)
  waiting for transfers between devices  16.6 us (14%)
  local copies, waits for them, and re-layouts  12.9 us (11%)
  other arithmetic  4.39 us (4%)
    pallas_call x8, Pallas kernels, call(): pl.pallas_call(kernel, out_shape=[jax.ShapeDtypeStruct(shape, dtype) for...  58.3 us
    ppermute x23, waiting for transfers between devices, swap(): return lax.ppermute(values, 'chan', [(at, at ^ mask) for at in range(4)])  16.6 us
    ppermute x23, starting transfers between devices, swap(): return lax.ppermute(values, 'chan', [(at, at ^ mask) for at in range(4)])  12.2 us
    all_to_all x2, starting transfers between devices, spread(): return lax.all_to_all(copies, 'dp', 0, 0).reshape(shards, rows, C_IN)  11.8 us
    unnamed x53, local copies, waits for them, and re-layouts  4.55 us
    pad x4, local copies, waits for them, and re-layouts, padded(): jnp.pad(values, ((0, count - values.shape[0]), (0, channels - values.shap...  2.97 us
  transfers between devices with their start and end apart: 25, of which 9 were waited for; matrix products, arithmetic and copies ran while one was open for 9% of the time, Pallas kernels for 17%

profile of v1, /device:TPU:0, one launch (start us, length us, event | category | flops | bytes accessed | tf_op | source)
XLA Modules:
  0.0 117.2 jit_solution(15071803066326597659)
XLA Ops:
  0.7 0.9 convert.6
  2.5 2.4 %collective-permute-start.3 = (bf16[336,112]{1,0:T(8,128)(2,1)S(1)}, bf16[336,112]{1,0:T(8,128)(2,1)S(1)}, u32[]{:S(2)}, u32[]{:S(2)}) collective-permute-start(bf16[336,112]{1,0:T(8,128)(2,1)S(1)} %pad_maximum_fusion), channel_id=1, source_target_pairs={{0,3},{1,2},{2,1},{3,0},{4,7},{5,6},{6,5},{7,4},{8,11},{9,10},{10,... | collective-permute-start | bytes 225800 | tf_op jit(solution)/shard_map/ppermute | solution.py:897
  6.5 1.5 %collective-permute-start.10 = (bf16[24,8,28]{2,1,0:T(8,128)(2,1)S(1)}, bf16[24,8,28]{2,1,0:T(8,128)(2,1)S(1)}, u32[]{:S(2)}, u32[]{:S(2)}) collective-permute-start(bf16[24,8,28]{2,1,0:T(8,128)(2,1)S(1)} %get-tuple-element.170), channel_id=1, source_target_pairs={{0,3},{1,2},{2,1},{3,0},{4,7},{5,6},{6,5},{7,4},{8,11},{9,10},{10,... | collective-permute-start | bytes 32264 | tf_op jit(solution)/shard_map/ppermute | solution.py:897
  9.5 5.8 %all-to-all-start = ((bf16[8,24,8,112]{3,2,1,0:T(8,128)(2,1)}), bf16[8,24,8,112]{3,2,1,0:T(8,128)(2,1)S(1)}, u32[]{:S(2)}, u32[]{:S(2)}) async-start(bf16[8,24,8,112]{3,2,1,0:T(8,128)(2,1)} %broadcast_in_dim.40), calls=%async_computation | async-start | bytes 786432 | tf_op jit(solution)/shard_map/all_to_all | solution.py:901
  15.3 1.2 pad_bitcast_fusion.bias_ref
  20.8 0.9 collective-permute-start.6
  22.9 3.2 %collective-permute-done.6 = f32[104,168]{1,0:T(8,128)S(1)} collective-permute-done((f32[104,168]{1,0:T(8,128)S(1)}, f32[104,168]{1,0:T(8,128)S(1)}, u32[]{:S(2)}, u32[]{:S(2)}) %collective-permute-start.6) | collective-permute-done | bytes 69920 | tf_op jit(solution)/shard_map/ppermute | solution.py:897
  26.2 2.2 %collective-permute-done.5 = f32[104,168]{1,0:T(8,128)S(1)} collective-permute-done((f32[104,168]{1,0:T(8,128)S(1)}, f32[104,168]{1,0:T(8,128)S(1)}, u32[]{:S(2)}, u32[]{:S(2)}) %collective-permute-start.5) | collective-permute-done | bytes 69920 | tf_op jit(solution)/shard_map/ppermute | solution.py:897
  30.5 6.0 %all-to-all-start.1 = ((bf16[8,24,8,112]{3,2,1,0:T(8,128)(2,1)}), bf16[8,24,8,112]{3,2,1,0:T(8,128)(2,1)S(1)}, u32[]{:S(2)}, u32[]{:S(2)}) async-start(bf16[8,24,8,112]{3,2,1,0:T(8,128)(2,1)} %broadcast_in_dim.44), calls=%async_computation.1 | async-start | bytes 786432 | tf_op jit(solution)/shard_map/all_to_all | solution.py:901
  36.6 1.9 %gram.1.gram_own = f32[120,112]{1,0:T(8,128)} custom-call(bf16[8,192,112]{2,1,0:T(8,128)(2,1)} %bitcast.39), custom_call_target="tpu_custom_call" | custom-call | tf_op jit(solution)/shard_map/gram/pallas_call | solution.py:773
  38.5 1.4 %collective-permute-done.gram_other = f32[120,112]{1,0:T(8,128)S(1)} collective-permute-done((f32[120,112]{1,0:T(8,128)}, f32[120,112]{1,0:T(8,128)S(1)}, u32[]{:S(2)}, u32[]{:S(2)}) %collective-permute-start) | collective-permute-done | bytes 53792 | tf_op jit(solution)/shard_map/ppermute | solution.py:897
  40.6 12.7 %expand.1 = (f32[8,192,768]{2,1,0:T(8,128)}, f32[16,768]{1,0:T(8,128)}, f32[32,768]{1,0:T(8,128)}) custom-call(f32[120,112]{1,0:T(8,128)} %gram.1.gram_own, f32[120,112]{1,0:T(8,128)} %copy-done.11, bf16[8,192,112]{2,1,0:T(8,128)(2,1)} %bitcast.40, bf16[768,112]{1,0:T(8,128)(2,1)} %copy-done.3, f32[104,768]{1,0:T(8,128)} %concatenate.25.stack_ref), custom_call_target="tpu_custom_call" | custom-call | tf_op jit(solution)/shard_map/expand/pallas_call | solution.py:773
  53.5 1.3 %collective-permute-done.7.sums_other = f32[16,768]{1,0:T(8,128)S(1)} collective-permute-done((f32[16,768]{1,0:T(8,128)}, f32[16,768]{1,0:T(8,128)S(1)}, u32[]{:S(2)}, u32[]{:S(2)}) %collective-permute-start.7) | collective-permute-done | bytes 49184 | tf_op jit(solution)/shard_map/ppermute | solution.py:897
  55.3 8.6 %squeeze.29 = (f32[8,192,112]{2,1,0:T(8,128)}, bf16[8,192,384]{2,1,0:T(8,128)(2,1)}, f32[32,112]{1,0:T(8,128)}, f32[64,768]{1,0:T(8,128)}, f32[64,32]{1,0:T(8,12...) custom-call(s32[2]{0:T(128)} %pad_add_fusion.index_ref, f32[8,192,768]{2,1,0:T(8,128)} %get-tuple-element.96.depth_ref, ...), custom_call_target="tpu_custom_call" | custom-call | tf_op jit(solution)/shard_map/squeeze/pallas_call | solution.py:773
  65.9 11.6 %gate_back.1 = (f32[8,192,384]{2,1,0:T(8,128)}, f32[16,384]{1,0:T(8,128)}, f32[384,112]{1,0:T(8,128)}, f32[72,384]{1,0:T(8,128)}, f32[8,32]{1,0:T(8,128)}, /*index=5*/f32[2,112]{1,0:T(2,128)}, bf16[192,112]{1,0:T(8,128)(2,1)}) custom-call(s32[2]{0:T(128)} %pad_add_fusion.index_ref, f32[8,192,112]{2,1,0:T(8,128)} %get-tuple-element.98.projected_ref, ...), custom_call_target="tpu_custom_call" | custom-call | tf_op jit(solution)/shard_map/gate_back/pallas_call | solution.py:773
  77.7 1.2 %collective-permute-done.12.sums_other = f32[16,384]{1,0:T(8,128)S(1)} collective-permute-done((f32[16,384]{1,0:T(8,128)}, f32[16,384]{1,0:T(8,128)S(1)}, u32[]{:S(2)}, u32[]{:S(2)}) %collective-permute-start.12) | collective-permute-done | bytes 24608 | tf_op jit(solution)/shard_map/ppermute | solution.py:897
  79.6 13.2 %depth_back.1 = (f32[8,192,384]{2,1,0:T(8,128)}, f32[16,384]{1,0:T(8,128)}, f32[32,384]{1,0:T(8,128)}, f32[2,384]{1,0:T(2,128)}) custom-call(s32[2]{0:T(128)} %pad_add_fusion.index_ref, f32[16,384]{1,0:T(8,128)} %get-tuple-element.105.sums_own, f32[16,384]{1,0:T(8,128)} %copy-done.19, f32[8,192,384]{2,1,0:T(8,128)} %get-tuple-element.106.two_ref, ...), custom_call_target="tpu_custom_call" | custom-call | tf_op jit(solution)/shard_map/depth_back/pallas_call | solution.py:773
  94.9 5.0 %expand_back.1 = (f32[384,112]{1,0:T(8,128)}, f32[192,112]{1,0:T(8,128)}, f32[2,384]{1,0:T(2,128)}) custom-call(s32[2]{0:T(128)} %pad_add_fusion.index_ref, f32[16,384]{1,0:T(8,128)} %get-tuple-element.108.sums_own, f32[16,384]{1,0:T(8,128)} %copy-done.18, f32[8,192,384]{2,1,0:T(8,128)} %get-tuple-element.109.one_ref, bf16[8,192,112]{2,1,0:T(8,128)(2,1)} %bitcast.43, ...), custom_call_target="tpu_custom_call" | custom-call | tf_op jit(solution)/shard_map/expand_back/pallas_call | solution.py:773
  101.8 1.2 collective-permute-start.19
  103.0 3.0 %collective-permute-done.19.input_other = bf16[192,112]{1,0:T(8,128)(2,1)S(1)} collective-permute-done((bf16[192,112]{1,0:T(8,128)(2,1)S(1)}, bf16[192,112]{1,0:T(8,128)(2,1)S(1)}, u32[]{:S(2)}, u32[]{:S(2)}) %collective-permute-start.19) | collective-permute-done | bytes 43040 | tf_op jit(solution)/shard_map/ppermute | solution.py:897
  106.8 2.3 %settle.1 = (f32[168,112]{1,0:T(8,128)}, f32[168,112]{1,0:T(8,128)}, f32[104,168]{1,0:T(8,128)}, f32[1,32]{1,0:T(1,128)}, f32[16,128]{1,0:T(8,128)}, /*index=5*/f32[192,112]{1,0:T(8,128)}) custom-call(s32[2]{0:T(128)} %pad_add_fusion.index_ref, f32[384,112]{1,0:T(8,128)} %get-tuple-element.110.expand_own, f32[384,112]{1,0:T(8,128)} %copy-done.7, ...), custom_call_target="tpu_custom_call" | custom-call | tf_op jit(solution)/shard_map/settle/pallas_call | solution.py:773
  109.6 1.1 collective-permute-start.20
  110.8 2.8 %collective-permute-done.20.square_other = f32[16,128]{1,0:T(8,128)S(1)} collective-permute-done((f32[16,128]{1,0:T(8,128)}, f32[16,128]{1,0:T(8,128)S(1)}, u32[]{:S(2)}, u32[]{:S(2)}) %collective-permute-start.20) | collective-permute-done | bytes 8224 | tf_op jit(solution)/shard_map/ppermute | solution.py:897
  114.1 3.1 %adam.1 = (bf16[24,16,28]{2,1,0:T(8,128)(2,1)}, f32[24,16,28]{2,1,0:T(8,128)}, f32[168,112]{1,0:T(8,128)}, f32[168,112]{1,0:T(8,128)}, f32[168,112]{1,0:T(8,128)...) custom-call(s32[2]{0:T(128)} %pad_add_fusion.index_ref, ...), custom_call_target="tpu_custom_call" | custom-call | tf_op jit(solution)/shard_map/adam/pallas_call | solution.py:773
  (116 shorter events, 21.8 us)
Async XLA Ops:
  2.5 26.8 %collective-permute-start.3 = (bf16[336,112]{1,0:T(8,128)(2,1)S(1)}, bf16[336,112]{1,0:T(8,128)(2,1)S(1)}, u32[]{:S(2)}, u32[]{:S(2)}) collective-permute-start(bf16[336,112]{1,0:T(8,128)(2,1)S(1)} %pad_maximum_fusion), channel_id=1, source_target_pairs={{0,3},{1,2},{2,1},{3,0},{4,7},{5,6},{6,5},{7,4},{8,11},{9,10},{10,... | collective-permute-start | bytes 225800 | tf_op jit(solution)/shard_map/ppermute | solution.py:897
  5.0 24.4 %collective-permute-start.2 = (bf16[336,112]{1,0:T(8,128)(2,1)S(1)}, bf16[336,112]{1,0:T(8,128)(2,1)S(1)}, u32[]{:S(2)}, u32[]{:S(2)}) collective-permute-start(bf16[336,112]{1,0:T(8,128)(2,1)S(1)} %pad_maximum_fusion), channel_id=1, source_target_pairs={{0,2},{1,3},{2,0},{3,1},{4,6},{5,7},{6,4},{7,5},{8,10},{9,11},{10,... | collective-permute-start | bytes 225800 | tf_op jit(solution)/shard_map/ppermute | solution.py:897
  6.5 14.4 %collective-permute-start.10 = (bf16[24,8,28]{2,1,0:T(8,128)(2,1)S(1)}, bf16[24,8,28]{2,1,0:T(8,128)(2,1)S(1)}, u32[]{:S(2)}, u32[]{:S(2)}) collective-permute-start(bf16[24,8,28]{2,1,0:T(8,128)(2,1)S(1)} %get-tuple-element.170), channel_id=1, source_target_pairs={{0,3},{1,2},{2,1},{3,0},{4,7},{5,6},{6,5},{7,4},{8,11},{9,10},{10,... | collective-permute-start | bytes 32264 | tf_op jit(solution)/shard_map/ppermute | solution.py:897
  7.9 13.9 %collective-permute-start.8 = (bf16[24,8,28]{2,1,0:T(8,128)(2,1)S(1)}, bf16[24,8,28]{2,1,0:T(8,128)(2,1)S(1)}, u32[]{:S(2)}, u32[]{:S(2)}) collective-permute-start(bf16[24,8,28]{2,1,0:T(8,128)(2,1)S(1)} %get-tuple-element.170), channel_id=1, source_target_pairs={{0,1},{1,0},{2,3},{3,2},{4,5},{5,4},{6,7},{7,6},{8,9},{9,8},{10,11... | collective-permute-start | bytes 32264 | tf_op jit(solution)/shard_map/ppermute | solution.py:897
  8.0 14.4 %collective-permute-start.9 = (bf16[24,8,28]{2,1,0:T(8,128)(2,1)S(1)}, bf16[24,8,28]{2,1,0:T(8,128)(2,1)S(1)}, u32[]{:S(2)}, u32[]{:S(2)}) collective-permute-start(bf16[24,8,28]{2,1,0:T(8,128)(2,1)S(1)} %get-tuple-element.171), channel_id=1, source_target_pairs={{0,2},{1,3},{2,0},{3,1},{4,6},{5,7},{6,4},{7,5},{8,10},{9,11},{10,... | collective-permute-start | bytes 32264 | tf_op jit(solution)/shard_map/ppermute | solution.py:897
  9.5 20.1 %all-to-all-start = ((bf16[8,24,8,112]{3,2,1,0:T(8,128)(2,1)}), bf16[8,24,8,112]{3,2,1,0:T(8,128)(2,1)S(1)}, u32[]{:S(2)}, u32[]{:S(2)}) async-start(bf16[8,24,8,112]{3,2,1,0:T(8,128)(2,1)} %broadcast_in_dim.40), calls=%async_computation | async-start | bytes 786432 | tf_op jit(solution)/shard_map/all_to_all | solution.py:901
  20.8 5.3 %collective-permute-start.6 = (f32[104,168]{1,0:T(8,128)S(1)}, f32[104,168]{1,0:T(8,128)S(1)}, u32[]{:S(2)}, u32[]{:S(2)}) collective-permute-start(f32[104,168]{1,0:T(8,128)S(1)} %concatenate.24), channel_id=1, source_target_pairs={{0,3},{1,2},{2,1},{3,0},{4,7},{5,6},{6,5},{7,4},{8,11},{9,10},{10,... | collective-permute-start | bytes 209672 | tf_op jit(solution)/shard_map/ppermute | solution.py:897
  21.8 6.6 %collective-permute-start.5 = (f32[104,168]{1,0:T(8,128)S(1)}, f32[104,168]{1,0:T(8,128)S(1)}, u32[]{:S(2)}, u32[]{:S(2)}) collective-permute-start(f32[104,168]{1,0:T(8,128)S(1)} %concatenate.24), channel_id=1, source_target_pairs={{0,2},{1,3},{2,0},{3,1},{4,6},{5,7},{6,4},{7,5},{8,10},{9,11},{10,... | collective-permute-start | bytes 209672 | tf_op jit(solution)/shard_map/ppermute | solution.py:897
  22.4 6.0 %collective-permute-start.4 = (f32[104,168]{1,0:T(8,128)S(1)}, f32[104,168]{1,0:T(8,128)S(1)}, u32[]{:S(2)}, u32[]{:S(2)}) collective-permute-start(f32[104,168]{1,0:T(8,128)S(1)} %concatenate.24), channel_id=1, source_target_pairs={{0,1},{1,0},{2,3},{3,2},{4,5},{5,4},{6,7},{7,6},{8,9},{9,8},{10,11... | collective-permute-start | bytes 209672 | tf_op jit(solution)/shard_map/ppermute | solution.py:897
  26.2 3.2 %collective-permute-start.1 = (bf16[336,112]{1,0:T(8,128)(2,1)S(1)}, bf16[336,112]{1,0:T(8,128)(2,1)S(1)}, u32[]{:S(2)}, u32[]{:S(2)}) collective-permute-start(bf16[336,112]{1,0:T(8,128)(2,1)S(1)} %pad_maximum_fusion), channel_id=1, source_target_pairs={{0,1},{1,0},{2,3},{3,2},{4,5},{5,4},{6,7},{7,6},{8,9},{9,8},{10,11... | collective-permute-start | bytes 225800 | tf_op jit(solution)/shard_map/ppermute | solution.py:897
  30.5 22.9 %all-to-all-start.1 = ((bf16[8,24,8,112]{3,2,1,0:T(8,128)(2,1)}), bf16[8,24,8,112]{3,2,1,0:T(8,128)(2,1)S(1)}, u32[]{:S(2)}, u32[]{:S(2)}) async-start(bf16[8,24,8,112]{3,2,1,0:T(8,128)(2,1)} %broadcast_in_dim.44), calls=%async_computation.1 | async-start | bytes 786432 | tf_op jit(solution)/shard_map/all_to_all | solution.py:901
  38.5 1.5 %collective-permute-start = (f32[120,112]{1,0:T(8,128)}, f32[120,112]{1,0:T(8,128)S(1)}, u32[]{:S(2)}, u32[]{:S(2)}) collective-permute-start(f32[120,112]{1,0:T(8,128)} %gram.1.gram_own), channel_id=1, source_target_pairs={{0,1},{1,0},{2,3},{3,2},{4,5},{5,4},{6,7},{7,6},{8,9},{9,8},{10,11... | collective-permute-start | bytes 161288 | tf_op jit(solution)/shard_map/ppermute | solution.py:897
  53.3 1.4 %collective-permute-start.7 = (f32[16,768]{1,0:T(8,128)}, f32[16,768]{1,0:T(8,128)S(1)}, u32[]{:S(2)}, u32[]{:S(2)}) collective-permute-start(f32[16,768]{1,0:T(8,128)} %get-tuple-element.97.sums_own), channel_id=1, source_target_pairs={{0,1},{1,0},{2,3},{3,2},{4,5},{5,4},{6,7},{7,6},{8,9},{9,8},{10,11... | collective-permute-start | bytes 147464 | tf_op jit(solution)/shard_map/ppermute | solution.py:897
  63.9 1.4 %collective-permute-start.11 = (f32[32,112]{1,0:T(8,128)}, f32[32,112]{1,0:T(8,128)S(1)}, u32[]{:S(2)}, u32[]{:S(2)}) collective-permute-start(f32[32,112]{1,0:T(8,128)} %get-tuple-element.99.sums_own), channel_id=1, source_target_pairs={{0,1},{1,0},{2,3},{3,2},{4,5},{5,4},{6,7},{7,6},{8,9},{9,8},{10,11... | collective-permute-start | bytes 43016 | tf_op jit(solution)/shard_map/ppermute | solution.py:897
  77.5 1.5 %collective-permute-start.12 = (f32[16,384]{1,0:T(8,128)}, f32[16,384]{1,0:T(8,128)S(1)}, u32[]{:S(2)}, u32[]{:S(2)}) collective-permute-start(f32[16,384]{1,0:T(8,128)} %get-tuple-element.105.sums_own), channel_id=1, source_target_pairs={{0,1},{1,0},{2,3},{3,2},{4,5},{5,4},{6,7},{7,6},{8,9},{9,8},{10,11... | collective-permute-start | bytes 73736 | tf_op jit(solution)/shard_map/ppermute | solution.py:897
  92.8 1.5 %collective-permute-start.13 = (f32[16,384]{1,0:T(8,128)}, f32[16,384]{1,0:T(8,128)S(1)}, u32[]{:S(2)}, u32[]{:S(2)}) collective-permute-start(f32[16,384]{1,0:T(8,128)} %get-tuple-element.108.sums_own), channel_id=1, source_target_pairs={{0,1},{1,0},{2,3},{3,2},{4,5},{5,4},{6,7},{7,6},{8,9},{9,8},{10,11... | collective-permute-start | bytes 73736 | tf_op jit(solution)/shard_map/ppermute | solution.py:897
  93.0 12.9 %collective-permute-start.15 = (f32[384,112]{1,0:T(8,128)S(1)}, f32[384,112]{1,0:T(8,128)S(1)}, u32[]{:S(2)}, u32[]{:S(2)}) collective-permute-start(f32[384,112]{1,0:T(8,128)S(1)} %copy-done.5), channel_id=1, source_target_pairs={{0,1},{1,0},{2,3},{3,2},{4,5},{5,4},{6,7},{7,6},{8,9},{9,8},{10,11... | collective-permute-start | bytes 516104 | tf_op jit(solution)/shard_map/ppermute | solution.py:897
  99.9 6.1 %collective-permute-start.14 = (f32[384,112]{1,0:T(8,128)}, f32[384,112]{1,0:T(8,128)S(1)}, u32[]{:S(2)}, u32[]{:S(2)}) collective-permute-start(f32[384,112]{1,0:T(8,128)} %get-tuple-element.110.expand_own), channel_id=1, source_target_pairs={{0,1},{1,0},{2,3},{3,2},{4,5},{5,4},{6,7},{7,6},{8,9},{9,8},{10,11... | collective-permute-start | bytes 516104 | tf_op jit(solution)/shard_map/ppermute | solution.py:897
  100.0 5.9 %collective-permute-start.16 = (f32[72,384]{1,0:T(8,128)S(1)}, f32[72,384]{1,0:T(8,128)S(1)}, u32[]{:S(2)}, u32[]{:S(2)}) collective-permute-start(f32[72,384]{1,0:T(8,128)S(1)} %copy-done.8), channel_id=1, source_target_pairs={{0,1},{1,0},{2,3},{3,2},{4,5},{5,4},{6,7},{7,6},{8,9},{9,8},{10,11... | collective-permute-start | bytes 331784 | tf_op jit(solution)/shard_map/ppermute | solution.py:897
  100.4 2.6 %collective-permute-start.17 = (f32[32,384]{1,0:T(8,128)S(1)}, f32[32,384]{1,0:T(8,128)S(1)}, u32[]{:S(2)}, u32[]{:S(2)}) collective-permute-start(f32[32,384]{1,0:T(8,128)S(1)} %copy-done.15), channel_id=1, source_target_pairs={{0,1},{1,0},{2,3},{3,2},{4,5},{5,4},{6,7},{7,6},{8,9},{9,8},{10,11... | collective-permute-start | bytes 147464 | tf_op jit(solution)/shard_map/ppermute | solution.py:897
  101.8 4.2 %collective-permute-start.19 = (bf16[192,112]{1,0:T(8,128)(2,1)S(1)}, bf16[192,112]{1,0:T(8,128)(2,1)S(1)}, u32[]{:S(2)}, u32[]{:S(2)}) collective-permute-start(bf16[192,112]{1,0:T(8,128)(2,1)S(1)} %convert_element_type.13), channel_id=1, source_target_pairs={{0,2},{1,3},{2,0},{3,1},{4,6},{5,7},{6,4},{7,5},{8,10},{9,11},{10,... | collective-permute-start | bytes 129032 | tf_op jit(solution)/shard_map/ppermute | solution.py:897
  109.1 4.4 %collective-permute-start.21 = (f32[192,112]{1,0:T(8,128)}, f32[192,112]{1,0:T(8,128)S(1)}, u32[]{:S(2)}, u32[]{:S(2)}) collective-permute-start(f32[192,112]{1,0:T(8,128)} %get-tuple-element.124.input_own), channel_id=1, source_target_pairs={{0,1},{1,0},{2,3},{3,2},{4,5},{5,4},{6,7},{7,6},{8,9},{9,8},{10,11... | collective-permute-start | bytes 258056 | tf_op jit(solution)/shard_map/ppermute | solution.py:897
  109.1 1.6 %collective-permute-start.22 = (bf16[192,112]{1,0:T(8,128)(2,1)S(1)}, bf16[192,112]{1,0:T(8,128)(2,1)S(1)}, u32[]{:S(2)}, u32[]{:S(2)}) collective-permute-start(bf16[192,112]{1,0:T(8,128)(2,1)S(1)} %copy-done.13), channel_id=1, source_target_pairs={{0,1},{1,0},{2,3},{3,2},{4,5},{5,4},{6,7},{7,6},{8,9},{9,8},{10,11... | collective-permute-start | bytes 129032 | tf_op jit(solution)/shard_map/ppermute | solution.py:897
  109.6 3.9 %collective-permute-start.20 = (f32[16,128]{1,0:T(8,128)}, f32[16,128]{1,0:T(8,128)S(1)}, u32[]{:S(2)}, u32[]{:S(2)}) collective-permute-start(f32[16,128]{1,0:T(8,128)} %get-tuple-element.119.square_own), channel_id=1, source_target_pairs={{0,2},{1,3},{2,0},{3,1},{4,6},{5,7},{6,4},{7,5},{8,10},{9,11},{10,... | collective-permute-start | bytes 24584 | tf_op jit(solution)/shard_map/ppermute | solution.py:897
  (25 other events, 87.5 us)

commit v2 on v1

--- a/solution.py
+++ b/solution.py
@@ -1,4 +1,5 @@
 import functools
+import math
 
 import jax
 import jax.numpy as jnp
@@ -374,6 +375,12 @@
 ROW_DEPTH_GAINS = 99
 ROW_PROJECT_GAINS = 101
 STACK_ROWS = 104
+KEEP_BIASES = 64
+KEEP_PROJECT = 80
+KEEP_KERNEL = 192
+KEEP_ROWS = 224
+PACKED_ROWS = 96
+BLOCK_ROWS = POSITIONS * 8
 PAIRED_ROWS_LIMIT = 3072
 contract_lanes = (((1,), (1,)), ((), ()))
 f32 = jnp.float32
@@ -416,12 +423,13 @@
     return found
 
 
-def gram_kernel(x_ref, gram_ref):
+def gram_kernel(x_ref, gram_ref, packed_ref):
     blocks = x_ref.shape[0]
-    flat = x_ref[...].reshape(blocks * x_ref.shape[1], x_ref.shape[2])
+    flat = x_ref[:, 0:BLOCK_ROWS, :].reshape(blocks * BLOCK_ROWS, C_IN)
     gram_ref[0:C_IN, :] = dot(flat, flat, contract_rows)
     ones = jnp.ones((8, flat.shape[0]), bf16)
     gram_ref[C_IN : C_IN + 8, :] = dot(ones, flat, contract_plain)
+    packed_ref[...] = x_ref[:, BLOCK_ROWS : BLOCK_ROWS + PACKED_ROWS, :]
 
 
 def expand_kernel(
@@ -447,7 +455,7 @@
     sums_ref[...] = jnp.zeros_like(sums_ref)
 
     def one_block(block, carry):
-        expanded_scr[...] = dot(x_ref[block], we_ref[...], contract_lanes)
+        expanded_scr[...] = dot(x_ref[block, 0:BLOCK_ROWS, :], we_ref[...], contract_lanes)
 
         def one_tile(tile, carry):
             lanes = lane_tile(tile)
@@ -547,7 +555,7 @@
 def gate_back_kernel(
     total_rows, index_ref, projected_ref, cot_ref, sums_own, sums_other, gains_ref, depth_ref,
     norm_ref, stack_ref, wp_ref, gate_ref, before_ref, pooled_ref, scaled_ref, x_ref,
-    two_ref, sums_ref, project_ref, lanes_ref, bias_ref, gains_grad_ref, output_ref,
+    two_ref, sums_ref, lanes_ref, gains_grad_ref, output_ref,
     delta_scr, grad_scr, gate_grad_scr, pooled_scr,
 ):
     blocks = depth_ref.shape[0]
@@ -565,7 +573,7 @@
     shift = gains_ref[1:2, :]
     mine = index_ref[0]
     output_ref[...] = (
-        x_ref[mine].astype(f32) + (projected_ref[mine] - average) * spread * gain + shift
+        x_ref[mine, 0:BLOCK_ROWS, :].astype(f32) + (projected_ref[mine] - average) * spread * gain + shift
     ).astype(output_ref.dtype)
     outer = gain * spread
 
@@ -603,8 +611,9 @@
     own_delta = gate_grad_scr[:, own_lanes]
     lanes_ref[0:HIDDEN_ROWS, :] = highest(squeeze_delta, pooled_ref[:, own_lanes], contract_rows)
     lanes_ref[HIDDEN_ROWS : 2 * HIDDEN_ROWS, :] = highest(hidden, own_delta, contract_rows)
-    lanes_ref[2 * HIDDEN_ROWS : 2 * HIDDEN_ROWS + 8, :] = rows_sum(own_delta)
-    bias_ref[...] = rows_sum(squeeze_delta)
+    lanes_ref[KEEP_BIASES : KEEP_BIASES + 8, :] = rows_sum(own_delta)
+    lanes_ref[KEEP_BIASES + 8 : KEEP_BIASES + 16, :] = jnp.zeros((8, PAIR_LANES), f32)
+    lanes_ref[KEEP_BIASES + 8 : KEEP_BIASES + 16, 0:HIDDEN_ROWS] = rows_sum(squeeze_delta)
     squeeze = stack_ref[ROW_SQUEEZE : ROW_SQUEEZE + HIDDEN_ROWS, own_lanes]
     pooled_scr[...] = highest(squeeze_delta, squeeze, contract_plain) / POSITIONS
     sums_ref[...] = jnp.zeros_like(sums_ref)
@@ -638,13 +647,13 @@
 
     lax.fori_loop(0, blocks, two_block, 0)
     rows = blocks * POSITIONS * 8
-    project_ref[...] = dot(
-        scaled_ref[...].reshape(rows, PAIR_LANES), delta_scr[...].reshape(rows, C_IN), contract_rows
+    lanes_ref[KEEP_PROJECT : KEEP_PROJECT + C_IN, :] = dot(
+        delta_scr[...].reshape(rows, C_IN), scaled_ref[...].reshape(rows, PAIR_LANES), contract_rows
     )
 
 
 def depth_back_kernel(
-    total_rows, index_ref, sums_own, sums_other, two_ref, depth_ref, x_ref, we_ref, stack_ref,
+    total_rows, index_ref, sums_own, sums_other, two_ref, depth_ref, x_ref, we_ref, stack_ref, lanes_ref,
     norm_one_ref, norm_two_ref,
     one_ref, sums_ref, kernel_ref, gains_grad_ref, expanded_scr, taps_scr, kernel_scr, factors_scr,
 ):
@@ -669,7 +678,7 @@
     own_weights = we_ref[own_lanes, :]
 
     def one_block(block, carry):
-        expanded_scr[...] = dot(x_ref[block], own_weights, contract_lanes)
+        expanded_scr[...] = dot(x_ref[block, 0:BLOCK_ROWS, :], own_weights, contract_lanes)
 
         def one_tile(tile, carry):
             lanes = lane_tile(tile)
@@ -726,9 +735,11 @@
         return lax.fori_loop(0, PAIR_LANES // 128, one_tile, carry)
 
     lax.fori_loop(0, blocks, one_block, 0)
-    kernel_ref[...] = jnp.zeros_like(kernel_ref)
+    kernel_ref[0:KEEP_KERNEL, :] = lanes_ref[...]
+    kernel_ref[KEEP_KERNEL : KEEP_KERNEL + 32, :] = jnp.zeros((32, PAIR_LANES), f32)
     for tap in range(TAPS):
-        kernel_ref[tap : tap + 1, :] = jnp.sum(kernel_scr[tap], axis=0, keepdims=True)
+        row = KEEP_KERNEL + tap
+        kernel_ref[row : row + 1, :] = jnp.sum(kernel_scr[tap], axis=0, keepdims=True)
 
 
 def expand_back_kernel(
@@ -750,7 +761,7 @@
     own_weights = we_ref[own_lanes, :]
 
     def one_block(block, carry):
-        expanded = dot(x_ref[block], own_weights, contract_lanes)
+        expanded = dot(x_ref[block, 0:BLOCK_ROWS, :], own_weights, contract_lanes)
         delta = outer * one_ref[block] - level - slope * (expanded - average)
         delta_scr[block] = delta.astype(bf16)
         return carry
@@ -758,96 +769,203 @@
     lax.fori_loop(0, blocks, one_block, 0)
     rows = blocks * POSITIONS * 8
     expand_ref[...] = dot(
-        delta_scr[...].reshape(rows, PAIR_LANES), x_ref[...].reshape(rows, C_IN), contract_rows
+        x_ref[:, 0:BLOCK_ROWS, :].reshape(rows, C_IN), delta_scr[...].reshape(rows, PAIR_LANES), contract_rows
     )
     input_ref[...] = dot(delta_scr[index_ref[0]], own_weights, contract_plain)
 
 
-def call(kernel, outs, operands, scratch=(), name=None):
-    spaces = [
-        pl.BlockSpec(memory_space=pltpu.SMEM)
-        if operand.dtype == jnp.int32
-        else pl.BlockSpec(memory_space=pltpu.VMEM)
-        for operand in operands
-    ]
-    return pl.pallas_call(
-        kernel,
-        out_shape=[jax.ShapeDtypeStruct(shape, dtype) for shape, dtype in outs],
-        in_specs=spaces,
-        out_specs=[pl.BlockSpec(memory_space=pltpu.VMEM)] * len(outs),
-        scratch_shapes=[pltpu.VMEM(shape, dtype) for shape, dtype in scratch],
-        compiler_params=pltpu.CompilerParams(vmem_limit_bytes=56 * 1024 * 1024),
-        name=name,
-    )(*operands)
+def one_hot(rows, columns, matches):
+    return matches(
+        lax.broadcasted_iota(jnp.int32, (rows, columns), 0),
+        lax.broadcasted_iota(jnp.int32, (rows, columns), 1),
+    )
+
+
+def copies_kernel(index_ref, rows_ref, cot_ref, copies_ref):
+    whole = rows_ref[...].astype(f32)
+    half = jnp.where(index_ref[1] % 2 == 0, whole[:, 0:8, :], whole[:, 8:16, :])
+    half = half.reshape(BLOCK_ROWS, C_IN).astype(bf16)
+    narrow = cot_ref.shape[2]
+    rows = cot_ref[...].reshape(4 * PACKED_ROWS, narrow)
+    packed = None
+    for group in range(4):
+        place = one_hot(narrow, C_IN, lambda r, c: c == r + group * narrow).astype(bf16)
+        part = dot(rows[group * PACKED_ROWS : (group + 1) * PACKED_ROWS], place, contract_plain)
+        packed = part if packed is None else packed + part
+    packed = packed.astype(bf16)
+    for at in range(copies_ref.shape[0]):
+        copies_ref[at, 0:BLOCK_ROWS, :] = half
+        copies_ref[at, BLOCK_ROWS : BLOCK_ROWS + PACKED_ROWS, :] = packed
+
+
+def cot_kernel(index_ref, own_ref, near_ref, far_ref, cross_ref, cot_ref):
+    position = index_ref[1]
+    first = position % 2 == 0
+    near = position + 1 - position % 2 * 2
+    blocks = cot_ref.shape[0]
+    narrow = C_IN // 4
+    rows = blocks * PACKED_ROWS
+    pieces = (
+        (own_ref, position), (near_ref, near), (far_ref, (position + 2) % 4),
+        (cross_ref, (near + 2) % 4),
+    )
+    for group in range(4):
+        total = None
+        for ref, place in pieces:
+            move = one_hot(
+                C_IN,
+                C_IN,
+                lambda r, c: (c - place * narrow == r - group * narrow)
+                & (r >= group * narrow) & (r < (group + 1) * narrow),
+            ).astype(bf16)
+            part = dot(ref[...].reshape(rows, C_IN), move, contract_plain)
+            total = part if total is None else total + part
+        total = total.reshape(rows // 16, 16, C_IN)
+        half = jnp.where(first, total[:, 0:8, :], total[:, 8:16, :])
+        half = half.reshape(blocks, PACKED_ROWS // 2, C_IN).astype(bf16)
+        start = group * (PACKED_ROWS // 2)
+        cot_ref[:, start : start + PACKED_ROWS // 2, :] = half
+
+
+def pack_kernel(
+    expand_ref, project_ref, depth_ref, squeeze_ref, excite_ref, excite_bias_ref, expand_gains_ref,
+    depth_gains_ref, project_gains_ref, stack_ref, matrix_ref,
+):
+    channels = expand_ref.shape[0]
+    narrow = project_gains_ref.shape[1]
+    stack_ref[...] = jnp.zeros_like(stack_ref)
+    for start, ref in (
+        (0, depth_ref), (ROW_SQUEEZE, squeeze_ref), (ROW_EXCITE, excite_ref),
+        (ROW_EXCITE_BIAS, excite_bias_ref), (ROW_EXPAND_GAINS, expand_gains_ref),
+        (ROW_DEPTH_GAINS, depth_gains_ref),
+    ):
+        stack_ref[start : start + ref.shape[0], :] = ref[...]
+    stack_ref[ROW_PROJECT_GAINS : ROW_PROJECT_GAINS + 2, 0:narrow] = project_gains_ref[...]
+    matrix_ref[...] = jnp.concatenate(
+        [expand_ref[...], project_ref[...]], axis=0
+    ).astype(bf16)
+
+
+def assemble_kernel(
+    index_ref, stack_0, stack_1, stack_2, stack_3, matrix_0, matrix_1, matrix_2, matrix_3,
+    x_ref, stack_ref, expand_ref, project_ref, gains_ref,
+):
+    position = index_ref[1]
+    first = position % 2 == 0
+    front = position // 2 == 0
+    channels = stack_0.shape[1]
+    narrow = C_IN // 4
+
+    def ordered(own, near, far, cross):
+        low, high = jnp.where(first, own, near), jnp.where(first, near, own)
+        far_low, far_high = jnp.where(first, far, cross), jnp.where(first, cross, far)
+        return (
+            jnp.where(front, low, far_low), jnp.where(front, high, far_high),
+            jnp.where(front, far_low, low), jnp.where(front, far_high, high),
+        )
+
+    stacks = ordered(stack_0[...], stack_1[...], stack_2[...], stack_3[...])
+    stack_ref[...] = jnp.zeros_like(stack_ref)
+    for place in range(4):
+        start = place // 2 * PAIR_LANES + place % 2 * channels
+        stack_ref[:, start : start + channels] = stacks[place]
+        gains_ref[:, place * narrow : (place + 1) * narrow] = stacks[place][
+            ROW_PROJECT_GAINS : ROW_PROJECT_GAINS + 2, 0:narrow
+        ]
+    matrices = ordered(*[ref[...].astype(f32) for ref in (matrix_0, matrix_1, matrix_2, matrix_3)])
+    gap = jnp.zeros((PAIR_LANES - 2 * channels, C_IN), f32)
+    for ref, start in ((expand_ref, 0), (project_ref, channels)):
+        parts = [matrix[start : start + channels] for matrix in matrices]
+        ref[...] = jnp.concatenate(parts[0:2] + [gap] + parts[2:4] + [gap], axis=0).astype(bf16)
 
 
 def settle_kernel(
-    index_ref, expand_own, expand_other, project_own, project_other, lanes_own, lanes_other,
-    kernel_own, kernel_other, bias_own, bias_other, three_ref, two_ref, one_ref, input_own, input_other,
-    expand_ref, project_ref, lanes_ref, bias_ref, square_ref, input_ref,
+    index_ref, expand_own, expand_other, keep_own, keep_other, three_ref, two_ref, one_ref,
+    input_own, input_other,
+    expand_ref, project_ref, lanes_ref, bias_ref, square_ref, input_ref, packed_ref,
 ):
-    first = index_ref[1] % 2 == 0
-    rows = expand_ref.shape[0]
-    mine = pl.ds(pl.multiple_of(index_ref[1] % 2 * rows, 8), rows)
-    total = jnp.zeros((1, 1), f32)
+    position = index_ref[1]
+    first = position % 2 == 0
+    channels = expand_ref.shape[0]
+    narrow = C_IN // 4
 
     def squared(values):
         return jnp.sum(jnp.sum(values * values, axis=0, keepdims=True), axis=1, keepdims=True)
 
-    for own, other, out in (
-        (expand_own, expand_other, expand_ref),
-        (project_own, project_other, project_ref),
-    ):
-        total = total + squared(own[...] + other[...])
-        out[...] = own[mine, :] + other[mine, :]
-
-    def keep(start, values):
-        lanes_ref[start : start + values.shape[0], :] = jnp.where(
-            first, values[:, 0:rows], values[:, rows : 2 * rows]
-        )
-
-    summed = lanes_own[...] + lanes_other[...]
-    summed = summed[0 : 2 * HIDDEN_ROWS + 1]
-    kernel = kernel_own[...] + kernel_other[...]
-    total = total + squared(summed) + squared(kernel)
-    keep(0, kernel)
-    keep(ROW_SQUEEZE, summed)
-    for start, ref in ((ROW_EXPAND_GAINS, one_ref), (ROW_DEPTH_GAINS, two_ref)):
-        values = ref[0:2, :]
-        total = total + squared(values)
-        keep(start, values)
-    bias = bias_own[0:1, :] + bias_other[0:1, :]
+    def mine(values):
+        return jnp.where(first, values[:, 0:channels], values[:, channels : 2 * channels])
+
+    def both(start, stop):
+        return keep_own[start:stop, :] + keep_other[start:stop, :]
+
+    expand = expand_own[...] + expand_other[...]
+    project = both(KEEP_PROJECT, KEEP_PROJECT + C_IN)
+    hidden = both(0, 2 * HIDDEN_ROWS)
+    excite_bias = both(KEEP_BIASES, KEEP_BIASES + 1)
+    kernel = both(KEEP_KERNEL, KEEP_KERNEL + 32)
+    total = squared(expand) + squared(project) + squared(hidden) + squared(kernel)
+    total = total + squared(excite_bias) + squared(one_ref[...]) + squared(two_ref[...])
+    bias = both(KEEP_BIASES + 8, KEEP_BIASES + 9)[:, 0:HIDDEN_ROWS]
+    square_ref[0:8, :] = jnp.broadcast_to(total, (8, 128))
+    square_ref[8:16, :] = jnp.broadcast_to(squared(bias) + squared(three_ref[...]), (8, 128))
     bias_ref[...] = bias
-    square_ref[0:8, :] = jnp.broadcast_to(total, (8, 128))
-    square_ref[8:16, :] = jnp.broadcast_to(squared(bias) + squared(three_ref[0:2, :]), (8, 128))
-    input_ref[...] = input_own[...] + input_other[...].astype(f32)
+    expand_ref[...] = jnp.transpose(mine(expand))
+    project_ref[...] = jnp.transpose(mine(project))
+    lanes_ref[0:32, :] = mine(kernel)
+    lanes_ref[ROW_SQUEEZE : ROW_SQUEEZE + 2 * HIDDEN_ROWS, :] = mine(hidden)
+    lanes_ref[ROW_EXCITE_BIAS : ROW_EXCITE_BIAS + 1, :] = mine(excite_bias)
+    lanes_ref[ROW_EXPAND_GAINS : ROW_EXPAND_GAINS + 2, :] = mine(one_ref[...])
+    lanes_ref[ROW_DEPTH_GAINS : ROW_DEPTH_GAINS + 2, :] = mine(two_ref[...])
+    own = input_own[...].reshape(POSITIONS, 8, C_IN)
+    other = input_other[...].reshape(POSITIONS, 8, C_IN)
+    whole = jnp.concatenate(
+        [jnp.where(first, own, other), jnp.where(first, other, own)], axis=1
+    ).reshape(4 * PACKED_ROWS, C_IN)
+    pick = one_hot(C_IN, narrow, lambda r, c: r == c + position * narrow).astype(f32)
+    input_ref[...] = highest(whole, pick, contract_plain).reshape(POSITIONS, 16, narrow)
+    across = position + 2 - position // 2 * 4
+    low = whole.astype(bf16)
+    packed = None
+    for group in range(4):
+        move = one_hot(
+            C_IN,
+            C_IN,
+            lambda r, c: (r - across * narrow == c - group * narrow)
+            & (c >= group * narrow) & (c < (group + 1) * narrow),
+        ).astype(bf16)
+        part = dot(low[group * PACKED_ROWS : (group + 1) * PACKED_ROWS], move, contract_plain)
+        packed = part if packed is None else packed + part
+    packed_ref[...] = packed.astype(bf16)
+
+
+def output_kernel(index_ref, own_ref, other_ref, output_ref):
+    first = index_ref[1] % 2 == 0
+    narrow = output_ref.shape[2]
+    pick = one_hot(C_IN, narrow, lambda r, c: r == c + index_ref[1] * narrow).astype(bf16)
+    own = dot(own_ref[...], pick, contract_plain).reshape(POSITIONS, 8, narrow)
+    other = dot(other_ref[...], pick, contract_plain).reshape(POSITIONS, 8, narrow)
+    output_ref[...] = jnp.concatenate(
+        [jnp.where(first, own, other), jnp.where(first, other, own)], axis=1
+    ).astype(bf16)
 
 
 def adam_kernel(
     index_ref, square_own, square_other, expand_grad, project_grad, lanes_grad, bias_grad, three_grad,
-    input_own, input_other, output_own, output_other, cot_ref, *refs,
+    input_own, packed_other, cot_ref, *refs,
 ):
-    first = index_ref[1] % 2 == 0
     params, outs = refs[:30], refs[30:]
     narrow = cot_ref.shape[2]
     total = square_own[0:1, 0:1] + square_other[0:1, 0:1] + square_own[8:9, 0:1]
     grad_norm = jnp.sqrt(total)
     factor = clip_limit / jnp.maximum(grad_norm, clip_limit)
-    outs[32][...] = grad_norm
-    pick = (
-        lax.broadcasted_iota(jnp.int32, (C_IN, narrow), 0)
-        == lax.broadcasted_iota(jnp.int32, (C_IN, narrow), 1) + index_ref[1] * narrow
-    ).astype(f32)
-
-    def halves(own, other):
-        mine = highest(own[...].astype(f32), pick, contract_plain).reshape(POSITIONS, 8, narrow)
-        theirs = highest(other[...].astype(f32), pick, contract_plain).reshape(POSITIONS, 8, narrow)
-        return jnp.concatenate(
-            [jnp.where(first, mine, theirs), jnp.where(first, theirs, mine)], axis=1
-        )
-
-    outs[0][...] = halves(output_own, output_other).astype(bf16)
-    outs[1][...] = halves(input_own, input_other) + cot_ref[...].astype(f32)
+    outs[31][...] = grad_norm
+    groups = []
+    for group in range(4):
+        pick = one_hot(C_IN, narrow, lambda r, c: r == c + group * narrow).astype(bf16)
+        groups.append(dot(packed_other[...], pick, contract_plain))
+    crossed = jnp.concatenate(groups, axis=0).reshape(POSITIONS, 16, narrow)
+    outs[0][...] = input_own[...] + crossed + cot_ref[...].astype(f32)
+    pick = one_hot(C_IN, narrow, lambda r, c: r == c + index_ref[1] * narrow).astype(f32)
     gradients = (
         expand_grad[...],
         lanes_grad[ROW_EXPAND_GAINS : ROW_EXPAND_GAINS + 2, :],
@@ -870,89 +988,112 @@
             decay_flags[entry],
         )
         for part in range(3):
-            outs[2 + 3 * entry + part][...] = updated[part]
+            outs[1 + 3 * entry + part][...] = updated[part]
+
+
+def call(kernel, outs, operands, scratch=(), name=None, keep=True, place=True):
+    spaces = [
+        pl.BlockSpec(memory_space=pltpu.SMEM)
+        if operand.dtype == jnp.int32
+        else pl.BlockSpec(memory_space=pltpu.VMEM)
+        for operand in operands
+    ]
+    operands = [
+        operand
+        if operand.dtype == jnp.int32
+        else pltpu.with_memory_space_constraint(operand, pltpu.VMEM if place else pltpu.HBM)
+        for operand in operands
+    ]
+    limit = 4 * 1024 * 1024 + sum(4 * math.prod(shape) for shape, _ in scratch)
+    made = pltpu.VMEM if keep else jax.ShapeDtypeStruct
+    return pl.pallas_call(
+        kernel,
+        out_shape=[made(shape, dtype) for shape, dtype in outs],
+        in_specs=spaces,
+        out_specs=[pl.BlockSpec(memory_space=pltpu.VMEM)] * len(outs),
+        scratch_shapes=[pltpu.VMEM(shape, dtype) for shape, dtype in scratch],
+        compiler_params=pltpu.CompilerParams(vmem_limit_bytes=limit),
+        name=name,
+    )(*operands)
 
 
 def on_device_paired(*arrays):
     block_input, cotangent = arrays[:2]
+    segments = block_input.shape[3]
+    if segments != 16:
+        return on_device(*arrays)
+    params = list(arrays[2:])
+    for at in (15, 16, 17, 21, 22, 23):
+        params[at] = params[at][None]
+    for at in (24, 25, 26):
+        params[at] = params[at].T
     (
         expand_weight, expand_gains, depth_weight, depth_gains, squeeze_weight,
         squeeze_bias, excite_weight, excite_bias, project_weight, project_gains,
-    ) = arrays[2::3]
-    segments = block_input.shape[3]
-    if segments != 16:
-        return on_device(*arrays)
+    ) = params[::3]
     shards = lax.axis_size("dp")
-    position = lax.axis_index("chan")
-    core = position % 2
-    index = jnp.stack([lax.axis_index("dp"), position]).astype(jnp.int32)
+    index = jnp.stack([lax.axis_index("dp"), lax.axis_index("chan")]).astype(jnp.int32)
     total_rows = float(POSITIONS * segments * shards)
     narrow = cotangent.shape[0]
     channels = expand_weight.shape[0]
-    hidden_units = squeeze_weight.shape[0]
     rows = POSITIONS * 8
     width = 2 * PAIR_LANES
 
     def swap(values, mask):
         return lax.ppermute(values, "chan", [(at, at ^ mask) for at in range(4)])
 
-    def spread(values):
-        copies = jnp.broadcast_to(values[None], (shards,) + values.shape)
-        return lax.all_to_all(copies, "dp", 0, 0).reshape(shards, rows, C_IN)
-
-    def whole(own, others):
-        distance = [position ^ place for place in range(4)]
-        return [
-            jnp.where(
-                at == 0, own, jnp.where(at == 1, others[0], jnp.where(at == 2, others[1], others[2]))
-            )
-            for at in distance
-        ]
-
-    def gather(values):
-        return whole(values, [swap(values, mask) for mask in (1, 2, 3)])
-
     input_rows = jnp.transpose(block_input, (1, 2, 3, 0)).reshape(POSITIONS, segments, C_IN)
     cot_rows = jnp.transpose(cotangent, (1, 2, 3, 0)).reshape(POSITIONS, segments, narrow)
-    x = spread(lax.dynamic_slice_in_dim(input_rows, core * 8, 8, 1))
-
-    def padded(values, count):
-        return jnp.pad(values, ((0, count - values.shape[0]), (0, channels - values.shape[1])))
-
-    stack = jnp.concatenate(
+    (copies,) = call(
+        copies_kernel,
+        [((shards, rows + PACKED_ROWS, C_IN), bf16)],
+        [index, input_rows, cot_rows],
+        name="copies",
+        keep=False,
+        place=False,
+    )
+    x = lax.all_to_all(copies, "dp", 0, 0)
+    stack, matrix = call(
+        pack_kernel,
+        [((STACK_ROWS, channels), f32), ((2 * channels, C_IN), bf16)],
         [
-            padded(depth_weight, 32),
-            padded(squeeze_weight, HIDDEN_ROWS),
-            padded(excite_weight, HIDDEN_ROWS),
-            excite_bias[None],
-            expand_gains,
-            depth_gains,
-            padded(project_gains, 3),
+            expand_weight, project_weight, depth_weight, squeeze_weight, excite_weight, excite_bias,
+            expand_gains, depth_gains, project_gains,
         ],
-        axis=0,
-    )
-    matrices = jnp.concatenate([expand_weight, project_weight.T], axis=0).astype(bf16)
-    stacks = gather(stack)
-    pairs = gather(matrices)
-    kept = lax.dynamic_slice_in_dim(cot_rows, core * 8, 8, 1)
-    sent = lax.dynamic_slice_in_dim(cot_rows, 8 - core * 8, 8, 1)
-    cots = whole(kept, [swap(sent, 1), swap(kept, 2), swap(sent, 3)])
-    cot = spread(jnp.concatenate(cots, axis=2))
-    gap = jnp.zeros((PAIR_LANES - 2 * channels, C_IN), bf16)
-    expand_all = jnp.concatenate(
-        [pairs[0][:channels], pairs[1][:channels], gap, pairs[2][:channels], pairs[3][:channels], gap]
-    )
-    project_all = jnp.concatenate(
-        [pairs[0][channels:], pairs[1][channels:], gap, pairs[2][channels:], pairs[3][channels:], gap]
-    )
-    side = jnp.zeros((STACK_ROWS, PAIR_LANES - 2 * channels), f32)
-    stack_all = jnp.concatenate([stacks[0], stacks[1], side, stacks[2], stacks[3], side], axis=1)
-    gains_all = jnp.concatenate(
-        [part[ROW_PROJECT_GAINS : ROW_PROJECT_GAINS + 2, :narrow] for part in stacks], axis=1
-    )
-    bias_row = jnp.pad(squeeze_bias, (0, HIDDEN_ROWS - hidden_units))[None]
-
-    (gram,) = call(gram_kernel, [((C_IN + 8, C_IN), f32)], [x], name="gram")
+        name="pack",
+        keep=False,
+        place=False,
+    )
+    stack_far, matrix_far = swap(stack, 2), swap(matrix, 2)
+    pieces = [
+        stack, swap(stack, 1), stack_far, swap(stack_far, 1),
+        matrix, swap(matrix, 1), matrix_far, swap(matrix_far, 1),
+    ]
+    gram, packed = call(
+        gram_kernel,
+        [((C_IN + 8, C_IN), f32), ((shards, PACKED_ROWS, C_IN), bf16)],
+        [x],
+        name="gram",
+    )
+    stack_all, expand_all, project_all, gains_all = call(
+        assemble_kernel,
+        [
+            ((STACK_ROWS, width), f32),
+            ((width, C_IN), bf16),
+            ((width, C_IN), bf16),
+            ((2, C_IN), f32),
+        ],
+        [index, *pieces, packed],
+        name="assemble",
+    )
+    (cot,) = call(
+        cot_kernel,
+        [((shards, rows, C_IN), bf16)],
+        [index, packed, swap(packed, 1), swap(packed, 2), swap(packed, 3)],
+        name="cot",
+    )
+    bias_row = jnp.pad(squeeze_bias, ((0, 0), (0, HIDDEN_ROWS - squeeze_bias.shape[1])))
+
     depth, sums, norm_one = call(
         functools.partial(expand_kernel, total_rows),
         [((shards, rows, width), f32), ((16, width), f32), ((32, width), f32)],
@@ -975,14 +1116,12 @@
         [((shards, rows, width), f32), ((rows, width), bf16)],
         name="squeeze",
     )
-    two, sums, project_grad, lanes_grad, bias_grad, three_grad, output = call(
+    two, sums, lanes_grad, three_grad, output = call(
         functools.partial(gate_back_kernel, total_rows),
         [
             ((shards, rows, PAIR_LANES), f32),
             ((16, PAIR_LANES), f32),
-            ((PAIR_LANES, C_IN), f32),
-            ((2 * HIDDEN_ROWS + 8, PAIR_LANES), f32),
-            ((8, HIDDEN_ROWS), f32),
+            ((KEEP_KERNEL, PAIR_LANES), f32),
             ((2, C_IN), f32),
             ((rows, C_IN), bf16),
         ],
@@ -998,17 +1137,18 @@
         ],
         name="gate_back",
     )
-    sums_other = swap(sums, 1)
-    early = [swap(project_grad, 1), swap(lanes_grad, 1), swap(bias_grad, 1), swap(output, 1)]
-    one, sums, kernel_grad, two_grad = call(
+    one, sums, keep, two_grad = call(
         functools.partial(depth_back_kernel, total_rows),
         [
             ((shards, rows, PAIR_LANES), f32),
             ((16, PAIR_LANES), f32),
-            ((32, PAIR_LANES), f32),
+            ((KEEP_ROWS, PAIR_LANES), f32),
             ((2, PAIR_LANES), f32),
         ],
-        [index, sums, sums_other, two, depth, x, expand_all, stack_all, norm_one, norm_two],
+        [
+            index, sums, swap(sums, 1), two, depth, x, expand_all, stack_all, lanes_grad,
+            norm_one, norm_two,
+        ],
         [
             ((rows, PAIR_LANES), f32),
             ((TAPS, 8, PAIR_LANES), f32),
@@ -1019,12 +1159,12 @@
     )
     expand_grad, input_part, one_grad = call(
         functools.partial(expand_back_kernel, total_rows),
-        [((PAIR_LANES, C_IN), f32), ((rows, C_IN), f32), ((2, PAIR_LANES), f32)],
+        [((C_IN, PAIR_LANES), f32), ((rows, C_IN), f32), ((2, PAIR_LANES), f32)],
         [index, sums, swap(sums, 1), one, x, expand_all, stack_all, norm_one],
         [((shards, rows, PAIR_LANES), bf16)],
         name="expand_back",
     )
-    expand_own, project_own, lanes_own, bias_own, square, input_half = call(
+    expand_own, project_own, lanes_own, bias_own, square, input_own, packed = call(
         settle_kernel,
         [
             ((channels, C_IN), f32),
@@ -1032,32 +1172,35 @@
             ((STACK_ROWS, channels), f32),
             ((1, HIDDEN_ROWS), f32),
             ((16, 128), f32),
-            ((rows, C_IN), f32),
+            ((POSITIONS, segments, narrow), f32),
+            ((PACKED_ROWS, C_IN), bf16),
         ],
         [
-            index, expand_grad, swap(expand_grad, 1), project_grad, early[0], lanes_grad, early[1],
-            kernel_grad, swap(kernel_grad, 1), bias_grad, early[2], three_grad, two_grad, one_grad,
-            input_part, swap(input_part.astype(bf16), 2),
+            index, expand_grad, swap(expand_grad, 1), keep, swap(keep, 1), three_grad, two_grad,
+            one_grad, input_part, swap(input_part, 1),
         ],
         name="settle",
     )
-    params = list(arrays[2:])
-    for at in (15, 16, 17, 21, 22, 23):
-        params[at] = params[at][None]
-    for at in (24, 25, 26):
-        params[at] = params[at].T
+    (block_output,) = call(
+        output_kernel,
+        [((POSITIONS, segments, narrow), bf16)],
+        [index, output, swap(output, 1)],
+        name="output",
+        keep=False,
+    )
     updated = call(
         adam_kernel,
-        [((POSITIONS, segments, narrow), bf16), ((POSITIONS, segments, narrow), f32)]
+        [((POSITIONS, segments, narrow), f32)]
         + [(value.shape, f32) for value in params]
         + [((1, 1), f32)],
         [
             index, square, swap(square, 2), expand_own, project_own, lanes_own, bias_own, three_grad,
-            input_half, swap(input_half, 1), output, early[3], cot_rows, *params,
+            input_own, swap(packed, 2), cot_rows, *params,
         ],
         name="adam",
-    )
-    results = list(updated)
+        keep=False,
+    )
+    results = [block_output] + list(updated)
     for at in (0, 1):
         results[at] = jnp.transpose(results[at].reshape(HT, WD, segments, narrow), (3, 0, 1, 2))
     for at in (17, 18, 19, 23, 24, 25):

time: 118 us -> 80.6 us (0.68)
  Pallas kernels: 58.3 us -> 43.3 us
  local copies, waits for them, and re-layouts: 12.9 us -> 0.19 us
  starting transfers between devices: 24 us -> 16.7 us
  other arithmetic: 4.39 us -> 0.08 us
  waiting for transfers between devices: 16.6 us -> 18.8 us
    pallas_call x8 -> x13, Pallas kernels: 58.3 us -> 43.3 us  [call(): pl.pallas_call(kernel, out_shape=[made(shape, dtype) for shape, dtype in...]
    all_to_all x2 -> x1, waiting for transfers between devices: 0.01 us -> 8.24 us  [on_device_paired(): x = lax.all_to_all(copies, 'dp', 0, 0)]
    ppermute x23 -> x20, waiting for transfers between devices: 16.6 us -> 10.6 us  [swap(): return lax.ppermute(values, 'chan', [(at, at ^ mask) for at in range(4)])]
    all_to_all x2 -> x1, starting transfers between devices: 11.8 us -> 7.28 us  [on_device_paired(): x = lax.all_to_all(copies, 'dp', 0, 0)]
    unnamed x53 -> x62, local copies, waits for them, and re-layouts: 4.55 us -> 0.18 us
    pad x4 -> x1, local copies, waits for them, and re-layouts: 2.97 us -> 0.01 us  [on_device_paired(): jnp.pad(squeeze_bias, ((0, 0), (0, HIDDEN_ROWS - squeeze_bias.shape[1])))]
    broadcast_in_dim x4 -> x0, local copies, waits for them, and re-layouts: 2.88 us -> none  [the longest x2 1.71 us: spread(): copies = jnp.broadcast_to(values[None], (shards,) + values.shape)]
    ppermute x23 -> x20, starting transfers between devices: 12.2 us -> 9.41 us  [swap(): return lax.ppermute(values, 'chan', [(at, at ^ mask) for at in range(4)])]
  transfers between devices with their start and end apart: 25 -> 21, of which waited for: 9 -> 8; matrix products, arithmetic and copies ran while one was open for 9% -> 0% of each run, Pallas kernels for 17% -> 22%
where the time goes in v2:
time: 80.6 us; the launch traced here: 80.3 us
  Pallas kernels  43.3 us (54%)
  waiting for transfers between devices  18.8 us (23%)
  starting transfers between devices  16.7 us (21%)
  between operations  1.25 us (2%)
    pallas_call x13, Pallas kernels, call(): pl.pallas_call(kernel, out_shape=[made(shape, dtype) for shape, dtype in...  43.3 us
    ppermute x20, waiting for transfers between devices, swap(): return lax.ppermute(values, 'chan', [(at, at ^ mask) for at in range(4)])  10.6 us
    ppermute x20, starting transfers between devices, swap(): return lax.ppermute(values, 'chan', [(at, at ^ mask) for at in range(4)])  9.41 us
    all_to_all x1, waiting for transfers between devices, on_device_paired(): x = lax.all_to_all(copies, 'dp', 0, 0)  8.24 us
    all_to_all x1, starting transfers between devices, on_device_paired(): x = lax.all_to_all(copies, 'dp', 0, 0)  7.28 us
  transfers between devices with their start and end apart: 21, of which 8 were waited for; matrix products, arithmetic and copies ran while one was open for 0% of the time, Pallas kernels for 22%

profile of v2, /device:TPU:0, one launch (start us, length us, event | category | flops | bytes accessed | tf_op | source)
XLA Modules:
  0.0 80.3 jit_solution(15667279669377729176)
XLA Ops:
  0.8 2.0 %copies.1 = bf16[8,288,112]{2,1,0:T(8,128)(2,1)} custom-call(s32[2]{0:T(128)S(1)} %pad_add_fusion.index_ref, bf16[24,16,112]{2,1,0:T(8,128)(2,1)} %bitcast.48, bf16[24,16,28]{2,1,0:T(8,128)(2,1)} %bitcast.33), custom_call_target="tpu_custom_call" | custom-call | tf_op jit(solution)/shard_map/copies/pallas_call | solution.py:1009
  2.7 7.3 %all-to-all-start = ((bf16[8,288,112]{2,1,0:T(8,128)(2,1)}), bf16[8,288,112]{2,1,0:T(8,128)(2,1)S(1)}, u32[]{:S(2)}, u32[]{:S(2)}) async-start(bf16[8,288,112]{2,1,0:T(8,128)(2,1)} %copies.1), calls=%async_computation | async-start | bytes 1179648 | tf_op jit(solution)/shard_map/all_to_all | solution.py:1055
  10.0 1.0 %pack.1 = (f32[104,168]{1,0:T(8,128)S(1)}, bf16[336,112]{1,0:T(8,128)(2,1)S(1)}) custom-call(f32[168,112]{1,0:T(8,128)} %refs_0_.1, f32[168,112]{1,0:T(8,128)} %bitcast.35, f32[25,168]{1,0:T(8,128)} %refs_6_.1, f32[28,168]{1,0:T(8,128)} %refs_12_.1, f32[28,168]{1,0:T(8,128)} %refs_18_.1, f32[1,168]{1,0:T(1,128)} %bitcast.39, f32[2,168]{1,0:T(2,128)} %refs_3_.1, ...), custom_call_target="tpu_custom_call" | custom-call | tf_op jit(solution)/shard_map/pack/pallas_call | solution.py:1009
  11.0 1.6 %collective-permute-start.5 = (bf16[336,112]{1,0:T(8,128)(2,1)S(1)}, bf16[336,112]{1,0:T(8,128)(2,1)S(1)}, u32[]{:S(2)}, u32[]{:S(2)}) collective-permute-start(bf16[336,112]{1,0:T(8,128)(2,1)S(1)} %get-tuple-element.104.matrix_0), channel_id=1, source_target_pairs={{0,2},{1,3},{2,0},{3,1},{4,6},{5,7},{6,4},{7,5},{8,10},{9,11},{10,... | collective-permute-start | bytes 225800 | tf_op jit(solution)/shard_map/ppermute | solution.py:1043
  13.6 4.0 %collective-permute-done.2.stack_2 = f32[104,168]{1,0:T(8,128)S(1)} collective-permute-done((f32[104,168]{1,0:T(8,128)S(1)}, f32[104,168]{1,0:T(8,128)S(1)}, u32[]{:S(2)}, u32[]{:S(2)}) %collective-permute-start.2) | collective-permute-done | bytes 69920 | tf_op jit(solution)/shard_map/ppermute | solution.py:1043
  17.7 8.2 %all-to-all-done.x_ref = bf16[8,288,112]{2,1,0:T(8,128)(2,1)S(1)} async-done(((bf16[8,288,112]{2,1,0:T(8,128)(2,1)}), bf16[8,288,112]{2,1,0:T(8,128)(2,1)S(1)}, u32[]{:S(2)}, u32[]{:S(2)}) %all-to-all-start) | async-done | bytes 516128 | tf_op jit(solution)/shard_map/all_to_all | solution.py:1055
  26.3 1.6 %collective-permute-start.9 = (bf16[8,96,112]{2,1,0:T(8,128)(2,1)S(1)}, bf16[8,96,112]{2,1,0:T(8,128)(2,1)S(1)}, u32[]{:S(2)}, u32[]{:S(2)}) collective-permute-start(bf16[8,96,112]{2,1,0:T(8,128)(2,1)S(1)} %get-tuple-element.105.x_ref.own_ref), channel_id=1, source_target_pairs={{0,2},{1,3},{2,0},{3,1},{4,6},{5,7},{6,4},{7,5},{8,10},{9,11},{10,... | collective-permute-start | bytes 516104 | tf_op jit(solution)/shard_map/ppermute | solution.py:1043
  28.7 0.8 collective-permute-done.6.matrix_3
  29.4 0.8 %assemble.1 = (f32[104,768]{1,0:T(8,128)S(1)}, bf16[768,112]{1,0:T(8,128)(2,1)S(1)}, bf16[768,112]{1,0:T(8,128)(2,1)S(1)}, f32[2,112]{1,0:T(2,128)S(1)}) custom-call(s32[2]{0:T(128)S(1)} %pad_add_fusion.index_ref, f32[104,168]{1,0:T(8,128)S(1)} %get-tuple-element.103.stack_0, f32[104,168]{1,0:T(8,128)S(1)} %collective-permute-done.1.stack_1, ...), custom_call_target="tpu_custom_call" | custom-call | tf_op jit(solution)/shard_map/assemble/pallas_call | solution.py:1009
  30.3 9.2 %expand.1 = (f32[8,192,768]{2,1,0:T(8,128)S(1)}, f32[16,768]{1,0:T(8,128)S(1)}, f32[32,768]{1,0:T(8,128)S(1)}) custom-call(f32[120,112]{1,0:T(8,128)S(1)} %get-tuple-element.102.gram_own, f32[120,112]{1,0:T(8,128)S(1)} %collective-permute-done.gram_other, bf16[8,288,112]{2,1,0:T(8,128)(2,1)S(1)} %all-to-all-done.x_ref, ...), custom_call_target="tpu_custom_call" | custom-call | tf_op jit(solution)/shard_map/expand/pallas_call | solution.py:1009
  39.8 1.5 %cot.1.cot_ref = bf16[8,192,112]{2,1,0:T(8,128)(2,1)S(1)} custom-call(s32[2]{0:T(128)S(1)} %pad_add_fusion.index_ref, bf16[8,96,112]{2,1,0:T(8,128)(2,1)S(1)} %get-tuple-element.105.x_ref.own_ref, bf16[8,96,112]{2,1,0:T(8,128)(2,1)S(1)} %collective-permute-done.8.near_ref, bf16[8,96,112]{2,1,0:T(8,128)(2,1)S(1)} %collective-permute-done.9.far_ref, ...), custom_call_target="tpu_custom_call" | custom-call | tf_op jit(solution)/shard_map/cot/pallas_call | solution.py:1009
  41.3 5.2 %squeeze.29 = (f32[8,192,112]{2,1,0:T(8,128)S(1)}, bf16[8,192,384]{2,1,0:T(8,128)(2,1)S(1)}, f32[32,112]{1,0:T(8,128)S(1)}, f32[64,768]{1,0:T(8,128)S(1)}, f32[6...) custom-call(s32[2]{0:T(128)S(1)} %pad_add_fusion.index_ref, ...), custom_call_target="tpu_custom_call" | custom-call | tf_op jit(solution)/shard_map/squeeze/pallas_call | solution.py:1009
  46.9 1.0 %collective-permute-done.11.sums_other = f32[32,112]{1,0:T(8,128)S(1)} collective-permute-done((f32[32,112]{1,0:T(8,128)S(1)}, f32[32,112]{1,0:T(8,128)S(1)}, u32[]{:S(2)}, u32[]{:S(2)}) %collective-permute-start.11) | collective-permute-done | bytes 14368 | tf_op jit(solution)/shard_map/ppermute | solution.py:1043
  47.8 7.5 %gate_back.1 = (f32[8,192,384]{2,1,0:T(8,128)S(1)}, f32[16,384]{1,0:T(8,128)S(1)}, f32[192,384]{1,0:T(8,128)S(1)}, f32[2,112]{1,0:T(2,128)S(1)}, bf16[192,112]{1,0:T(8,128)(2,1)S(1)}) custom-call(s32[2]{0:T(128)S(1)} %pad_add_fusion.index_ref, f32[8,192,112]{2,1,0:T(8,128)S(1)} %get-tuple-element.111.projected_ref, bf16[8,192,112]{2,1,0:T(8,128)(2,1)S(1)} %cot.1.cot_ref, ...), custom_call_target="tpu_custom_call" | custom-call | tf_op jit(solution)/shard_map/gate_back/pallas_call | solution.py:1009
  55.6 1.0 %collective-permute-done.13.sums_other = f32[16,384]{1,0:T(8,128)S(1)} collective-permute-done((f32[16,384]{1,0:T(8,128)S(1)}, f32[16,384]{1,0:T(8,128)S(1)}, u32[]{:S(2)}, u32[]{:S(2)}) %collective-permute-start.13) | collective-permute-done | bytes 24608 | tf_op jit(solution)/shard_map/ppermute | solution.py:1043
  56.6 8.9 %depth_back.1 = (f32[8,192,384]{2,1,0:T(8,128)S(1)}, f32[16,384]{1,0:T(8,128)S(1)}, f32[224,384]{1,0:T(8,128)S(1)}, f32[2,384]{1,0:T(2,128)S(1)}) custom-call(s32[2]{0:T(128)S(1)} %pad_add_fusion.index_ref, f32[16,384]{1,0:T(8,128)S(1)} %get-tuple-element.120.sums_own, f32[16,384]{1,0:T(8,128)S(1)} %collective-permute-done.13.sums_other, ...), custom_call_target="tpu_custom_call" | custom-call | tf_op jit(solution)/shard_map/depth_back/pallas_call | solution.py:1009
  66.1 1.2 %collective-permute-done.14.sums_other = f32[16,384]{1,0:T(8,128)S(1)} collective-permute-done((f32[16,384]{1,0:T(8,128)S(1)}, f32[16,384]{1,0:T(8,128)S(1)}, u32[]{:S(2)}, u32[]{:S(2)}) %collective-permute-start.14) | collective-permute-done | bytes 24608 | tf_op jit(solution)/shard_map/ppermute | solution.py:1043
  67.6 2.7 %expand_back.1 = (f32[112,384]{1,0:T(8,128)S(1)}, f32[192,112]{1,0:T(8,128)S(1)}, f32[2,384]{1,0:T(2,128)S(1)}) custom-call(s32[2]{0:T(128)S(1)} %pad_add_fusion.index_ref, f32[16,384]{1,0:T(8,128)S(1)} %get-tuple-element.124.sums_own, f32[16,384]{1,0:T(8,128)S(1)} %collective-permute-done.14.sums_other, f32[8,192,384]{2,1,0:T(8,128)S(1)} %get-tuple-element.125.one_ref, ...), custom_call_target="tpu_custom_call" | custom-call | tf_op jit(solution)/shard_map/expand_back/pallas_call | solution.py:1009
  71.1 0.8 %collective-permute-done.17.input_other = f32[192,112]{1,0:T(8,128)S(1)} collective-permute-done((f32[192,112]{1,0:T(8,128)S(1)}, f32[192,112]{1,0:T(8,128)S(1)}, u32[]{:S(2)}, u32[]{:S(2)}) %collective-permute-start.17) | collective-permute-done | bytes 86048 | tf_op jit(solution)/shard_map/ppermute | solution.py:1043
  71.9 1.0 %settle.1 = (f32[168,112]{1,0:T(8,128)S(1)}, f32[168,112]{1,0:T(8,128)S(1)}, f32[104,168]{1,0:T(8,128)S(1)}, f32[1,32]{1,0:T(1,128)S(1)}, f32[16,128]{1,0:T(8,12...) custom-call(s32[2]{0:T(128)S(1)} %pad_add_fusion.index_ref, ...), custom_call_target="tpu_custom_call" | custom-call | tf_op jit(solution)/shard_map/settle/pallas_call | solution.py:1009
  72.9 1.6 %collective-permute-start.19 = (bf16[96,112]{1,0:T(8,128)(2,1)S(1)}, bf16[96,112]{1,0:T(8,128)(2,1)S(1)}, u32[]{:S(2)}, u32[]{:S(2)}) collective-permute-start(bf16[96,112]{1,0:T(8,128)(2,1)S(1)} %get-tuple-element.138), channel_id=1, source_target_pairs={{0,2},{1,3},{2,0},{3,1},{4,6},{5,7},{6,4},{7,5},{8,10},{9,11},{10,... | collective-permute-start | bytes 64520 | tf_op jit(solution)/shard_map/ppermute | solution.py:1043
  75.0 1.4 %output.1 = bf16[24,16,28]{2,1,0:T(8,128)(2,1)} custom-call(s32[2]{0:T(128)S(1)} %pad_add_fusion.index_ref, bf16[192,112]{1,0:T(8,128)(2,1)S(1)} %get-tuple-element.119.own_ref, bf16[192,112]{1,0:T(8,128)(2,1)S(1)} %collective-permute-done.12.other_ref), custom_call_target="tpu_custom_call" | custom-call | tf_op jit(solution)/shard_map/output/pallas_call | solution.py:1009
  76.3 1.8 %collective-permute-done.18.square_other = f32[16,128]{1,0:T(8,128)S(1)} collective-permute-done((f32[16,128]{1,0:T(8,128)S(1)}, f32[16,128]{1,0:T(8,128)S(1)}, u32[]{:S(2)}, u32[]{:S(2)}) %collective-permute-start.18) | collective-permute-done | bytes 8224 | tf_op jit(solution)/shard_map/ppermute | solution.py:1043
  78.4 1.9 %adam.1 = (f32[24,16,28]{2,1,0:T(8,128)}, f32[168,112]{1,0:T(8,128)}, f32[168,112]{1,0:T(8,128)}, f32[168,112]{1,0:T(8,128)}, f32[2,168]{1,0:T(2,128)}, /*index=...) custom-call(s32[2]{0:T(128)S(1)} %pad_add_fusion.index_ref, ...), custom_call_target="tpu_custom_call" | custom-call | tf_op jit(solution)/shard_map/adam/pallas_call | solution.py:1009
  (95 shorter events, 5.3 us)
Async XLA Ops:
  0.8 39.0 %copy-start.28 = (f32[28]{0:T(128)S(1)}, f32[28]{0:T(128)}, u32[]{:S(2)}) copy-start(f32[28]{0:T(128)} %param.49) | copy-start | bytes 340
  2.7 23.2 %all-to-all-start = ((bf16[8,288,112]{2,1,0:T(8,128)(2,1)}), bf16[8,288,112]{2,1,0:T(8,128)(2,1)S(1)}, u32[]{:S(2)}, u32[]{:S(2)}) async-start(bf16[8,288,112]{2,1,0:T(8,128)(2,1)} %copies.1), calls=%async_computation | async-start | bytes 1179648 | tf_op jit(solution)/shard_map/all_to_all | solution.py:1055
  11.0 16.8 %collective-permute-start.5 = (bf16[336,112]{1,0:T(8,128)(2,1)S(1)}, bf16[336,112]{1,0:T(8,128)(2,1)S(1)}, u32[]{:S(2)}, u32[]{:S(2)}) collective-permute-start(bf16[336,112]{1,0:T(8,128)(2,1)S(1)} %get-tuple-element.104.matrix_0), channel_id=1, source_target_pairs={{0,2},{1,3},{2,0},{3,1},{4,6},{5,7},{6,4},{7,5},{8,10},{9,11},{10,... | collective-permute-start | bytes 225800 | tf_op jit(solution)/shard_map/ppermute | solution.py:1043
  12.6 5.1 %collective-permute-start.2 = (f32[104,168]{1,0:T(8,128)S(1)}, f32[104,168]{1,0:T(8,128)S(1)}, u32[]{:S(2)}, u32[]{:S(2)}) collective-permute-start(f32[104,168]{1,0:T(8,128)S(1)} %get-tuple-element.103.stack_0), channel_id=1, source_target_pairs={{0,2},{1,3},{2,0},{3,1},{4,6},{5,7},{6,4},{7,5},{8,10},{9,11},{10,... | collective-permute-start | bytes 209672 | tf_op jit(solution)/shard_map/ppermute | solution.py:1043
  13.1 13.2 %collective-permute-start.1 = (f32[104,168]{1,0:T(8,128)S(1)}, f32[104,168]{1,0:T(8,128)S(1)}, u32[]{:S(2)}, u32[]{:S(2)}) collective-permute-start(f32[104,168]{1,0:T(8,128)S(1)} %get-tuple-element.103.stack_0), channel_id=1, source_target_pairs={{0,1},{1,0},{2,3},{3,2},{4,5},{5,4},{6,7},{7,6},{8,9},{9,8},{10,11... | collective-permute-start | bytes 209672 | tf_op jit(solution)/shard_map/ppermute | solution.py:1043
  13.1 15.0 %collective-permute-start.4 = (bf16[336,112]{1,0:T(8,128)(2,1)S(1)}, bf16[336,112]{1,0:T(8,128)(2,1)S(1)}, u32[]{:S(2)}, u32[]{:S(2)}) collective-permute-start(bf16[336,112]{1,0:T(8,128)(2,1)S(1)} %get-tuple-element.104.matrix_0), channel_id=1, source_target_pairs={{0,1},{1,0},{2,3},{3,2},{4,5},{5,4},{6,7},{7,6},{8,9},{9,8},{10,11... | collective-permute-start | bytes 225800 | tf_op jit(solution)/shard_map/ppermute | solution.py:1043
  17.6 10.7 %collective-permute-start.3 = (f32[104,168]{1,0:T(8,128)S(1)}, f32[104,168]{1,0:T(8,128)S(1)}, u32[]{:S(2)}, u32[]{:S(2)}) collective-permute-start(f32[104,168]{1,0:T(8,128)S(1)} %collective-permute-done.2.stack_2), channel_id=1, source_target_pairs={{0,1},{1,0},{2,3},{3,2},{4,5},{5,4},{6,7},{7,6},{8,9},{9,8},{10,11... | collective-permute-start | bytes 209672 | tf_op jit(solution)/shard_map/ppermute | solution.py:1043
  26.2 13.6 %collective-permute-start.10 = (bf16[8,96,112]{2,1,0:T(8,128)(2,1)S(1)}, bf16[8,96,112]{2,1,0:T(8,128)(2,1)S(1)}, u32[]{:S(2)}, u32[]{:S(2)}) collective-permute-start(bf16[8,96,112]{2,1,0:T(8,128)(2,1)S(1)} %get-tuple-element.105.x_ref.own_ref), channel_id=1, source_target_pairs={{0,3},{1,2},{2,1},{3,0},{4,7},{5,6},{6,5},{7,4},{8,11},{9,10},{10,... | collective-permute-start | bytes 516104 | tf_op jit(solution)/shard_map/ppermute | solution.py:1043
  26.3 13.5 %collective-permute-start.9 = (bf16[8,96,112]{2,1,0:T(8,128)(2,1)S(1)}, bf16[8,96,112]{2,1,0:T(8,128)(2,1)S(1)}, u32[]{:S(2)}, u32[]{:S(2)}) collective-permute-start(bf16[8,96,112]{2,1,0:T(8,128)(2,1)S(1)} %get-tuple-element.105.x_ref.own_ref), channel_id=1, source_target_pairs={{0,2},{1,3},{2,0},{3,1},{4,6},{5,7},{6,4},{7,5},{8,10},{9,11},{10,... | collective-permute-start | bytes 516104 | tf_op jit(solution)/shard_map/ppermute | solution.py:1043
  27.8 12.0 %collective-permute-start.8 = (bf16[8,96,112]{2,1,0:T(8,128)(2,1)S(1)}, bf16[8,96,112]{2,1,0:T(8,128)(2,1)S(1)}, u32[]{:S(2)}, u32[]{:S(2)}) collective-permute-start(bf16[8,96,112]{2,1,0:T(8,128)(2,1)S(1)} %get-tuple-element.105.x_ref.own_ref), channel_id=1, source_target_pairs={{0,1},{1,0},{2,3},{3,2},{4,5},{5,4},{6,7},{7,6},{8,9},{9,8},{10,11... | collective-permute-start | bytes 516104 | tf_op jit(solution)/shard_map/ppermute | solution.py:1043
  28.1 1.3 %collective-permute-start.6 = (bf16[336,112]{1,0:T(8,128)(2,1)S(1)}, bf16[336,112]{1,0:T(8,128)(2,1)S(1)}, u32[]{:S(2)}, u32[]{:S(2)}) collective-permute-start(bf16[336,112]{1,0:T(8,128)(2,1)S(1)} %collective-permute-done.5.matrix_2), channel_id=1, source_target_pairs={{0,1},{1,0},{2,3},{3,2},{4,5},{5,4},{6,7},{7,6},{8,9},{9,8},{10,11... | collective-permute-start | bytes 225800 | tf_op jit(solution)/shard_map/ppermute | solution.py:1043
  28.4 1.9 %collective-permute-start = (f32[120,112]{1,0:T(8,128)S(1)}, f32[120,112]{1,0:T(8,128)S(1)}, u32[]{:S(2)}, u32[]{:S(2)}) collective-permute-start(f32[120,112]{1,0:T(8,128)S(1)} %get-tuple-element.102.gram_own), channel_id=1, source_target_pairs={{0,1},{1,0},{2,3},{3,2},{4,5},{5,4},{6,7},{7,6},{8,9},{9,8},{10,11... | collective-permute-start | bytes 161288 | tf_op jit(solution)/shard_map/ppermute | solution.py:1043
  39.4 1.9 %collective-permute-start.7 = (f32[16,768]{1,0:T(8,128)S(1)}, f32[16,768]{1,0:T(8,128)S(1)}, u32[]{:S(2)}, u32[]{:S(2)}) collective-permute-start(f32[16,768]{1,0:T(8,128)S(1)} %get-tuple-element.109.sums_own), channel_id=1, source_target_pairs={{0,1},{1,0},{2,3},{3,2},{4,5},{5,4},{6,7},{7,6},{8,9},{9,8},{10,11... | collective-permute-start | bytes 147464 | tf_op jit(solution)/shard_map/ppermute | solution.py:1043
  46.6 1.2 %collective-permute-start.11 = (f32[32,112]{1,0:T(8,128)S(1)}, f32[32,112]{1,0:T(8,128)S(1)}, u32[]{:S(2)}, u32[]{:S(2)}) collective-permute-start(f32[32,112]{1,0:T(8,128)S(1)} %get-tuple-element.112.sums_own), channel_id=1, source_target_pairs={{0,1},{1,0},{2,3},{3,2},{4,5},{5,4},{6,7},{7,6},{8,9},{9,8},{10,11... | collective-permute-start | bytes 43016 | tf_op jit(solution)/shard_map/ppermute | solution.py:1043
  55.3 1.3 %collective-permute-start.13 = (f32[16,384]{1,0:T(8,128)S(1)}, f32[16,384]{1,0:T(8,128)S(1)}, u32[]{:S(2)}, u32[]{:S(2)}) collective-permute-start(f32[16,384]{1,0:T(8,128)S(1)} %get-tuple-element.120.sums_own), channel_id=1, source_target_pairs={{0,1},{1,0},{2,3},{3,2},{4,5},{5,4},{6,7},{7,6},{8,9},{9,8},{10,11... | collective-permute-start | bytes 73736 | tf_op jit(solution)/shard_map/ppermute | solution.py:1043
  65.5 6.4 %collective-permute-start.16 = (f32[224,384]{1,0:T(8,128)S(1)}, f32[224,384]{1,0:T(8,128)S(1)}, u32[]{:S(2)}, u32[]{:S(2)}) collective-permute-start(f32[224,384]{1,0:T(8,128)S(1)} %get-tuple-element.127.keep_own), channel_id=1, source_target_pairs={{0,1},{1,0},{2,3},{3,2},{4,5},{5,4},{6,7},{7,6},{8,9},{9,8},{10,11... | collective-permute-start | bytes 1032200 | tf_op jit(solution)/shard_map/ppermute | solution.py:1043
  65.8 1.5 %collective-permute-start.14 = (f32[16,384]{1,0:T(8,128)S(1)}, f32[16,384]{1,0:T(8,128)S(1)}, u32[]{:S(2)}, u32[]{:S(2)}) collective-permute-start(f32[16,384]{1,0:T(8,128)S(1)} %get-tuple-element.124.sums_own), channel_id=1, source_target_pairs={{0,1},{1,0},{2,3},{3,2},{4,5},{5,4},{6,7},{7,6},{8,9},{9,8},{10,11... | collective-permute-start | bytes 73736 | tf_op jit(solution)/shard_map/ppermute | solution.py:1043
  67.3 10.9 %copy-start.4 = (f32[28,168]{1,0:T(8,128)S(1)}, f32[28,168]{1,0:T(8,128)}, u32[]{:S(2)}) copy-start(f32[28,168]{1,0:T(8,128)} %refs_12_.1) | copy-start | bytes 56452
  67.3 10.9 %copy-start.5 = (f32[28,168]{1,0:T(8,128)S(1)}, f32[28,168]{1,0:T(8,128)}, u32[]{:S(2)}) copy-start(f32[28,168]{1,0:T(8,128)} %refs_18_.1) | copy-start | bytes 56452
  70.3 1.6 %collective-permute-start.15 = (f32[112,384]{1,0:T(8,128)S(1)}, f32[112,384]{1,0:T(8,128)S(1)}, u32[]{:S(2)}, u32[]{:S(2)}) collective-permute-start(f32[112,384]{1,0:T(8,128)S(1)} %get-tuple-element.126.expand_own), channel_id=1, source_target_pairs={{0,1},{1,0},{2,3},{3,2},{4,5},{5,4},{6,7},{7,6},{8,9},{9,8},{10,11... | collective-permute-start | bytes 516104 | tf_op jit(solution)/shard_map/ppermute | solution.py:1043
  70.6 1.3 %collective-permute-start.17 = (f32[192,112]{1,0:T(8,128)S(1)}, f32[192,112]{1,0:T(8,128)S(1)}, u32[]{:S(2)}, u32[]{:S(2)}) collective-permute-start(f32[192,112]{1,0:T(8,128)S(1)} %get-tuple-element.131.input_own), channel_id=1, source_target_pairs={{0,1},{1,0},{2,3},{3,2},{4,5},{5,4},{6,7},{7,6},{8,9},{9,8},{10,11... | collective-permute-start | bytes 258056 | tf_op jit(solution)/shard_map/ppermute | solution.py:1043
  70.8 4.1 %collective-permute-start.12 = (bf16[192,112]{1,0:T(8,128)(2,1)S(1)}, bf16[192,112]{1,0:T(8,128)(2,1)S(1)}, u32[]{:S(2)}, u32[]{:S(2)}) collective-permute-start(bf16[192,112]{1,0:T(8,128)(2,1)S(1)} %get-tuple-element.119.own_ref), channel_id=1, source_target_pairs={{0,1},{1,0},{2,3},{3,2},{4,5},{5,4},{6,7},{7,6},{8,9},{9,8},{10,11... | collective-permute-start | bytes 129032 | tf_op jit(solution)/shard_map/ppermute | solution.py:1043
  72.9 5.3 %collective-permute-start.19 = (bf16[96,112]{1,0:T(8,128)(2,1)S(1)}, bf16[96,112]{1,0:T(8,128)(2,1)S(1)}, u32[]{:S(2)}, u32[]{:S(2)}) collective-permute-start(bf16[96,112]{1,0:T(8,128)(2,1)S(1)} %get-tuple-element.138), channel_id=1, source_target_pairs={{0,2},{1,3},{2,0},{3,1},{4,6},{5,7},{6,4},{7,5},{8,10},{9,11},{10,... | collective-permute-start | bytes 64520 | tf_op jit(solution)/shard_map/ppermute | solution.py:1043
  74.5 3.7 %collective-permute-start.18 = (f32[16,128]{1,0:T(8,128)S(1)}, f32[16,128]{1,0:T(8,128)S(1)}, u32[]{:S(2)}, u32[]{:S(2)}) collective-permute-start(f32[16,128]{1,0:T(8,128)S(1)} %get-tuple-element.132.square_own), channel_id=1, source_target_pairs={{0,2},{1,3},{2,0},{3,1},{4,6},{5,7},{6,4},{7,5},{8,10},{9,11},{10,... | collective-permute-start | bytes 24584 | tf_op jit(solution)/shard_map/ppermute | solution.py:1043
  (28 other events, 305.1 us)

commit v3 on v2

--- a/solution.py
+++ b/solution.py
@@ -400,6 +400,8 @@
 
 
 def lane_tile(index, start=0):
+    if isinstance(start, int):
+        return slice(start + index * 128, start + index * 128 + 128)
     return pl.ds(pl.multiple_of(start + index * 128, 128), 128)
 
 
@@ -423,46 +425,75 @@
     return found
 
 
-def gram_kernel(x_ref, gram_ref, packed_ref):
-    blocks = x_ref.shape[0]
-    flat = x_ref[:, 0:BLOCK_ROWS, :].reshape(blocks * BLOCK_ROWS, C_IN)
-    gram_ref[0:C_IN, :] = dot(flat, flat, contract_rows)
-    ones = jnp.ones((8, flat.shape[0]), bf16)
-    gram_ref[C_IN : C_IN + 8, :] = dot(ones, flat, contract_plain)
-    packed_ref[...] = x_ref[:, BLOCK_ROWS : BLOCK_ROWS + PACKED_ROWS, :]
-
-
-def expand_kernel(
-    total_rows, gram_own, gram_other, x_ref, we_ref, stack_ref,
-    depth_ref, sums_ref, norm_ref, expanded_scr, taps_scr,
+def in_order(position, own, near, far, cross):
+    first = position % 2 == 0
+    front = position // 2 == 0
+    low, high = jnp.where(first, own, near), jnp.where(first, near, own)
+    far_low, far_high = jnp.where(first, far, cross), jnp.where(first, cross, far)
+    return (
+        jnp.where(front, low, far_low), jnp.where(front, high, far_high),
+        jnp.where(front, far_low, low), jnp.where(front, far_high, high),
+    )
+
+
+def matrix_in_order(position, refs, start, channels):
+    parts = in_order(position, *[ref[start : start + channels, :].astype(f32) for ref in refs])
+    gap = jnp.zeros((PAIR_LANES - 2 * channels, C_IN), f32)
+    return jnp.concatenate([*parts[0:2], gap, *parts[2:4], gap], axis=0).astype(bf16)
+
+
+def first_kernel(
+    index_ref, matrix_0, matrix_1, matrix_2, matrix_3, x_ref,
+    expanded_ref, sums_ref, we_ref, packed_ref,
 ):
     blocks = x_ref.shape[0]
     width = we_ref.shape[0]
-    gram = gram_own[...] + gram_other[...]
-    weights = we_ref[...].astype(f32)
-    average = highest(gram[C_IN : C_IN + 8], weights, contract_lanes) / total_rows
-    turned = highest(weights, gram[0:C_IN], contract_plain)
-    squares = highest(jnp.ones((8, C_IN), f32), turned * weights, contract_lanes) / total_rows
+    refs = (matrix_0, matrix_1, matrix_2, matrix_3)
+    we_ref[...] = matrix_in_order(index_ref[1], refs, 0, matrix_0.shape[0] // 2)
+    packed_ref[...] = x_ref[:, BLOCK_ROWS : BLOCK_ROWS + PACKED_ROWS, :]
+    for lanes in (slice(at, at + 256) for at in range(0, width, 256)):
+        total = jnp.zeros((8, 256), f32)
+        square = jnp.zeros((8, 256), f32)
+        for block in range(blocks):
+            value = dot(x_ref[block, 0:BLOCK_ROWS, :], we_ref[lanes, :], contract_lanes)
+            expanded_ref[block, :, lanes] = value
+            shaped = value.reshape(POSITIONS, 8, 256)
+            total = total + jnp.sum(shaped, axis=0)
+            square = square + jnp.sum(shaped * shaped, axis=0)
+        sums_ref[0:8, lanes] = total
+        sums_ref[8:16, lanes] = square
+
+
+def norm_factors(total_rows, sums_own, sums_other, gain, shift, norm_ref):
+    average = rows_sum(sums_own[0:8] + sums_other[0:8]) / total_rows
+    squares = rows_sum(sums_own[8:16] + sums_other[8:16]) / total_rows
     spread = lax.rsqrt(squares - average * average + norm_epsilon)
-    gain = stack_ref[ROW_EXPAND_GAINS : ROW_EXPAND_GAINS + 1, :] * spread
-    shift = stack_ref[ROW_EXPAND_GAINS + 1 : ROW_EXPAND_GAINS + 2, :] - average * gain
+    gain = gain * spread
     norm_ref[0:8, :] = 0.5 * gain
-    norm_ref[8:16, :] = 0.5 * shift
+    norm_ref[8:16, :] = 0.5 * (shift - average * gain)
     norm_ref[16:24, :] = average
     norm_ref[24:32, :] = spread
+
+
+def expand_kernel(
+    total_rows, expanded_ref, sums_own, sums_other, stack_ref, depth_ref, sums_ref, norm_ref, taps_scr
+):
+    blocks, _, width = expanded_ref.shape
+    norm_factors(
+        total_rows, sums_own, sums_other, stack_ref[ROW_EXPAND_GAINS : ROW_EXPAND_GAINS + 1, :],
+        stack_ref[ROW_EXPAND_GAINS + 1 : ROW_EXPAND_GAINS + 2, :], norm_ref,
+    )
     for tap in range(TAPS):
         taps_scr[tap] = jnp.broadcast_to(stack_ref[tap : tap + 1, :], (8, width))
     sums_ref[...] = jnp.zeros_like(sums_ref)
 
     def one_block(block, carry):
-        expanded_scr[...] = dot(x_ref[block, 0:BLOCK_ROWS, :], we_ref[...], contract_lanes)
-
-        def one_tile(tile, carry):
+        for tile in range(width // 128):
             lanes = lane_tile(tile)
             gain_half = norm_ref[0:8, lanes]
             shift_half = norm_ref[8:16, lanes]
             active = [
-                swish_of_half(expanded_scr[8 * at : 8 * at + 8, lanes] * gain_half + shift_half)
+                swish_of_half(expanded_ref[block, 8 * at : 8 * at + 8, lanes] * gain_half + shift_half)
                 for at in range(POSITIONS)
             ]
             total = jnp.zeros((8, 128), f32)
@@ -479,33 +510,23 @@
                     square = square + value * value
             sums_ref[0:8, lanes] += total
             sums_ref[8:16, lanes] += square
-            return carry
-
-        return lax.fori_loop(0, width // 128, one_tile, carry)
+        return carry
 
     lax.fori_loop(0, blocks, one_block, 0)
 
 
 def squeeze_kernel(
-    total_rows, index_ref, depth_ref, sums_own, sums_other, stack_ref, wp_ref, cot_ref, bias_ref,
-    projected_ref, scaled_ref, sums_ref, gate_ref, before_ref, pooled_ref, norm_ref,
-    active_scr, scaled_scr,
+    total_rows, depth_ref, sums_own, sums_other, stack_ref, wp_ref, cot_ref, bias_ref,
+    projected_ref, scaled_ref, sums_ref, gate_ref, before_ref, pooled_ref, norm_ref, active_ref,
 ):
-    blocks = depth_ref.shape[0]
-    width = depth_ref.shape[2]
-    own = pl.multiple_of(index_ref[1] // 2 * PAIR_LANES, 128)
-    average = rows_sum(sums_own[0:8] + sums_other[0:8]) / total_rows
-    squares = rows_sum(sums_own[8:16] + sums_other[8:16]) / total_rows
-    spread = lax.rsqrt(squares - average * average + norm_epsilon)
-    gain = stack_ref[ROW_DEPTH_GAINS : ROW_DEPTH_GAINS + 1, :] * spread
-    shift = stack_ref[ROW_DEPTH_GAINS + 1 : ROW_DEPTH_GAINS + 2, :] - average * gain
-    norm_ref[0:8, :] = 0.5 * gain
-    norm_ref[8:16, :] = 0.5 * shift
-    norm_ref[16:24, :] = average
-    norm_ref[24:32, :] = spread
+    blocks, _, width = depth_ref.shape
+    norm_factors(
+        total_rows, sums_own, sums_other, stack_ref[ROW_DEPTH_GAINS : ROW_DEPTH_GAINS + 1, :],
+        stack_ref[ROW_DEPTH_GAINS + 1 : ROW_DEPTH_GAINS + 2, :], norm_ref,
+    )
 
     def pool_block(block, carry):
-        def pool_tile(tile, carry):
+        for tile in range(width // 128):
             lanes = lane_tile(tile)
             gain_half = norm_ref[0:8, lanes]
             shift_half = norm_ref[8:16, lanes]
@@ -514,12 +535,10 @@
                 value = swish_of_half(
                     depth_ref[block, 8 * at : 8 * at + 8, lanes] * gain_half + shift_half
                 )
-                active_scr[block, 8 * at : 8 * at + 8, lanes] = value
+                active_ref[block, 8 * at : 8 * at + 8, lanes] = value
                 total = total + value
             pooled_ref[pl.ds(pl.multiple_of(block * 8, 8), 8), lanes] = total / POSITIONS
-            return carry
-
-        return lax.fori_loop(0, width // 128, pool_tile, carry)
+        return carry
 
     lax.fori_loop(0, blocks, pool_block, 0)
     squeeze = stack_ref[ROW_SQUEEZE : ROW_SQUEEZE + HIDDEN_ROWS, :]
@@ -530,31 +549,26 @@
     raised = highest(hidden, excite, contract_plain)
     raised = raised + stack_ref[ROW_EXCITE_BIAS : ROW_EXCITE_BIAS + 1, :]
     gate_ref[...] = 0.5 + 0.5 * jnp.tanh(0.5 * raised)
-    sums_ref[...] = jnp.zeros_like(sums_ref)
-
-    def scale_block(block, carry):
+    totals = [jnp.zeros((8, C_IN), f32)] * 4
+    for block in range(blocks):
         for tile in range(width // 128):
-            lanes = slice(tile * 128, tile * 128 + 128)
-            gate = gate_ref[pl.ds(pl.multiple_of(block * 8, 8), 8), lanes]
-            value = active_scr[block, :, lanes].reshape(POSITIONS, 8, 128) * gate[None]
-            scaled_scr[:, lanes] = value.reshape(POSITIONS * 8, 128).astype(bf16)
-        projected = dot(scaled_scr[...], wp_ref[...], contract_plain)
+            lanes = lane_tile(tile)
+            gate = gate_ref[8 * block : 8 * block + 8, lanes]
+            value = active_ref[block, :, lanes].reshape(POSITIONS, 8, 128) * gate[None]
+            scaled_ref[block, :, lanes] = value.reshape(BLOCK_ROWS, 128).astype(bf16)
+        projected = dot(scaled_ref[block], wp_ref[...], contract_plain)
         projected_ref[block] = projected
-        scaled_ref[block] = scaled_scr[:, pl.ds(own, PAIR_LANES)]
         shaped = projected.reshape(POSITIONS, 8, C_IN)
         upstream = cot_ref[block].astype(f32).reshape(POSITIONS, 8, C_IN)
-        sums_ref[0:8, :] += jnp.sum(shaped, axis=0)
-        sums_ref[8:16, :] += jnp.sum(shaped * shaped, axis=0)
-        sums_ref[16:24, :] += jnp.sum(shaped * upstream, axis=0)
-        sums_ref[24:32, :] += jnp.sum(upstream, axis=0)
-        return carry
-
-    lax.fori_loop(0, blocks, scale_block, 0)
+        terms = (shaped, shaped * shaped, shaped * upstream, upstream)
+        totals = [total + jnp.sum(term, axis=0) for total, term in zip(totals, terms)]
+    for at in range(4):
+        sums_ref[8 * at : 8 * at + 8, :] = totals[at]
 
 
 def gate_back_kernel(
     total_rows, index_ref, projected_ref, cot_ref, sums_own, sums_other, gains_ref, depth_ref,
-    norm_ref, stack_ref, wp_ref, gate_ref, before_ref, pooled_ref, scaled_ref, x_ref,
+    norm_ref, stack_ref, wp_ref, gate_ref, before_ref, pooled_ref, scaled_ref, active_ref, x_ref,
     two_ref, sums_ref, lanes_ref, gains_grad_ref, output_ref,
     delta_scr, grad_scr, gate_grad_scr, pooled_scr,
 ):
@@ -577,31 +591,18 @@
     ).astype(output_ref.dtype)
     outer = gain * spread
 
-    def back_block(block, carry):
+    for block in range(blocks):
         normal = (projected_ref[block] - average) * spread
         delta = outer * (
             cot_ref[block].astype(f32) - beta / total_rows - normal * (gamma / total_rows)
         )
         delta_scr[block] = delta.astype(bf16)
-        grad_scr[...] = dot(delta_scr[block], wp_ref[...], contract_lanes)
-        two_ref[block] = grad_scr[:, own_lanes]
-
-        def gate_tile(tile, carry):
-            lanes = lane_tile(tile)
-            gain_half = norm_ref[0:8, lanes]
-            shift_half = norm_ref[8:16, lanes]
-            total = jnp.zeros((8, 128), f32)
-            for at in range(POSITIONS):
-                active = swish_of_half(
-                    depth_ref[block, 8 * at : 8 * at + 8, lanes] * gain_half + shift_half
-                )
-                total = total + active * grad_scr[8 * at : 8 * at + 8, lanes]
-            gate_grad_scr[pl.ds(pl.multiple_of(block * 8, 8), 8), lanes] = total
-            return carry
-
-        return lax.fori_loop(0, width // 128, gate_tile, carry)
-
-    lax.fori_loop(0, blocks, back_block, 0)
+    for block in range(blocks):
+        for lanes in (slice(at, at + 256) for at in range(0, width, 256)):
+            value = dot(delta_scr[block], wp_ref[lanes, :], contract_lanes)
+            grad_scr[block, :, lanes] = value
+            value = (value * active_ref[block, :, lanes]).reshape(POSITIONS, 8, 256)
+            gate_grad_scr[8 * block : 8 * block + 8, lanes] = jnp.sum(value, axis=0)
     excite = stack_ref[ROW_EXCITE : ROW_EXCITE + HIDDEN_ROWS, :]
     gate = gate_ref[...]
     gate_grad_scr[...] = gate_grad_scr[...] * gate * (1.0 - gate)
@@ -620,42 +621,40 @@
 
     def two_block(block, carry):
         rows = pl.ds(pl.multiple_of(block * 8, 8), 8)
-
-        def two_tile(tile, carry):
+        for tile in range(PAIR_LANES // 128):
             lanes = lane_tile(tile)
             whole = lane_tile(tile, own)
             gain_half = norm_ref[0:8, whole]
             shift_half = norm_ref[8:16, whole]
             average = norm_ref[16:24, whole]
-            gate = gate_ref[rows, whole]
-            pooled_grad = pooled_scr[rows, lanes]
+            gate = 0.5 * gate_ref[rows, whole]
+            pooled_grad = 0.5 * pooled_scr[rows, lanes]
             total = jnp.zeros((8, 128), f32)
             product = jnp.zeros((8, 128), f32)
             for at in range(POSITIONS):
                 spot = slice(8 * at, 8 * at + 8)
                 depth = depth_ref[block, spot, whole]
-                value = two_ref[block, spot, lanes] * gate + pooled_grad
-                value = value * slope_of_half(depth * gain_half + shift_half)
+                bent = jnp.tanh(depth * gain_half + shift_half)
+                slope = (1.0 + bent) + active_ref[block, spot, whole] * (1.0 - bent)
+                value = (grad_scr[block, spot, whole] * gate + pooled_grad) * slope
                 two_ref[block, spot, lanes] = value
                 total = total + value
                 product = product + value * (depth - average)
             sums_ref[0:8, lanes] += total
             sums_ref[8:16, lanes] += product
-            return carry
-
-        return lax.fori_loop(0, PAIR_LANES // 128, two_tile, carry)
+        return carry
 
     lax.fori_loop(0, blocks, two_block, 0)
     rows = blocks * POSITIONS * 8
     lanes_ref[KEEP_PROJECT : KEEP_PROJECT + C_IN, :] = dot(
-        delta_scr[...].reshape(rows, C_IN), scaled_ref[...].reshape(rows, PAIR_LANES), contract_rows
+        delta_scr[...].reshape(rows, C_IN), scaled_ref[:, :, own_lanes].reshape(rows, PAIR_LANES), contract_rows
     )
 
 
 def depth_back_kernel(
-    total_rows, index_ref, sums_own, sums_other, two_ref, depth_ref, x_ref, we_ref, stack_ref, lanes_ref,
+    total_rows, index_ref, sums_own, sums_other, two_ref, depth_ref, expanded_ref, stack_ref, lanes_ref,
     norm_one_ref, norm_two_ref,
-    one_ref, sums_ref, kernel_ref, gains_grad_ref, expanded_scr, taps_scr, kernel_scr, factors_scr,
+    one_ref, sums_ref, kernel_ref, gains_grad_ref, taps_scr, kernel_scr, factors_scr,
 ):
     blocks = depth_ref.shape[0]
     own = pl.multiple_of(index_ref[1] // 2 * PAIR_LANES, 128)
@@ -675,12 +674,9 @@
         taps_scr[tap] = jnp.broadcast_to(stack_ref[tap : tap + 1, own_lanes], (8, PAIR_LANES))
     sums_ref[...] = jnp.zeros_like(sums_ref)
     kernel_scr[...] = jnp.zeros_like(kernel_scr)
-    own_weights = we_ref[own_lanes, :]
 
     def one_block(block, carry):
-        expanded_scr[...] = dot(x_ref[block, 0:BLOCK_ROWS, :], own_weights, contract_lanes)
-
-        def one_tile(tile, carry):
+        for tile in range(PAIR_LANES // 128):
             lanes = lane_tile(tile)
             whole = lane_tile(tile, own)
             gain_half = norm_one_ref[0:8, whole]
@@ -699,7 +695,7 @@
                     - level
                     - slope * (depth_ref[block, spot, whole] - average_two)
                 )
-                active.append(swish_of_half(expanded_scr[spot, lanes] * gain_half + shift_half))
+                active.append(swish_of_half(expanded_ref[block, spot, whole] * gain_half + shift_half))
             pairs = {}
             for row in range(HT):
                 for col in range(WD):
@@ -723,16 +719,14 @@
                 for tap, target in back[at]:
                     term = taps_scr[tap, :, lanes] * grads[target]
                     value = term if value is None else value + term
-                expanded = expanded_scr[spot, lanes]
+                expanded = expanded_ref[block, spot, whole]
                 value = value * slope_of_half(expanded * gain_half + shift_half)
                 one_ref[block, spot, lanes] = value
                 total = total + value
                 product = product + value * (expanded - average_one)
             sums_ref[0:8, lanes] += total
             sums_ref[8:16, lanes] += product
-            return carry
-
-        return lax.fori_loop(0, PAIR_LANES // 128, one_tile, carry)
+        return carry
 
     lax.fori_loop(0, blocks, one_block, 0)
     kernel_ref[0:KEEP_KERNEL, :] = lanes_ref[...]
@@ -743,7 +737,7 @@
 
 
 def expand_back_kernel(
-    total_rows, index_ref, sums_own, sums_other, one_ref, x_ref, we_ref, stack_ref, norm_ref,
+    total_rows, index_ref, sums_own, sums_other, one_ref, expanded_ref, x_ref, we_ref, stack_ref, norm_ref,
     expand_ref, input_ref, gains_grad_ref, delta_scr,
 ):
     blocks = x_ref.shape[0]
@@ -760,13 +754,10 @@
     level = outer * (beta[0:1] / total_rows)
     own_weights = we_ref[own_lanes, :]
 
-    def one_block(block, carry):
-        expanded = dot(x_ref[block, 0:BLOCK_ROWS, :], own_weights, contract_lanes)
-        delta = outer * one_ref[block] - level - slope * (expanded - average)
+    for block in range(blocks):
+        centred = expanded_ref[block, :, own_lanes] - average
+        delta = outer * one_ref[block] - level - slope * centred
         delta_scr[block] = delta.astype(bf16)
-        return carry
-
-    lax.fori_loop(0, blocks, one_block, 0)
     rows = blocks * POSITIONS * 8
     expand_ref[...] = dot(
         x_ref[:, 0:BLOCK_ROWS, :].reshape(rows, C_IN), delta_scr[...].reshape(rows, PAIR_LANES), contract_rows
@@ -848,23 +839,11 @@
 
 def assemble_kernel(
     index_ref, stack_0, stack_1, stack_2, stack_3, matrix_0, matrix_1, matrix_2, matrix_3,
-    x_ref, stack_ref, expand_ref, project_ref, gains_ref,
+    after_ref, stack_ref, project_ref, gains_ref,
 ):
-    position = index_ref[1]
-    first = position % 2 == 0
-    front = position // 2 == 0
     channels = stack_0.shape[1]
     narrow = C_IN // 4
-
-    def ordered(own, near, far, cross):
-        low, high = jnp.where(first, own, near), jnp.where(first, near, own)
-        far_low, far_high = jnp.where(first, far, cross), jnp.where(first, cross, far)
-        return (
-            jnp.where(front, low, far_low), jnp.where(front, high, far_high),
-            jnp.where(front, far_low, low), jnp.where(front, far_high, high),
-        )
-
-    stacks = ordered(stack_0[...], stack_1[...], stack_2[...], stack_3[...])
+    stacks = in_order(index_ref[1], stack_0[...], stack_1[...], stack_2[...], stack_3[...])
     stack_ref[...] = jnp.zeros_like(stack_ref)
     for place in range(4):
         start = place // 2 * PAIR_LANES + place % 2 * channels
@@ -872,11 +851,8 @@
         gains_ref[:, place * narrow : (place + 1) * narrow] = stacks[place][
             ROW_PROJECT_GAINS : ROW_PROJECT_GAINS + 2, 0:narrow
         ]
-    matrices = ordered(*[ref[...].astype(f32) for ref in (matrix_0, matrix_1, matrix_2, matrix_3)])
-    gap = jnp.zeros((PAIR_LANES - 2 * channels, C_IN), f32)
-    for ref, start in ((expand_ref, 0), (project_ref, channels)):
-        parts = [matrix[start : start + channels] for matrix in matrices]
-        ref[...] = jnp.concatenate(parts[0:2] + [gap] + parts[2:4] + [gap], axis=0).astype(bf16)
+    refs = (matrix_0, matrix_1, matrix_2, matrix_3)
+    project_ref[...] = matrix_in_order(index_ref[1], refs, channels, channels)
 
 
 def settle_kernel(
@@ -1069,20 +1045,20 @@
         stack, swap(stack, 1), stack_far, swap(stack_far, 1),
         matrix, swap(matrix, 1), matrix_far, swap(matrix_far, 1),
     ]
-    gram, packed = call(
-        gram_kernel,
-        [((C_IN + 8, C_IN), f32), ((shards, PACKED_ROWS, C_IN), bf16)],
-        [x],
-        name="gram",
-    )
-    stack_all, expand_all, project_all, gains_all = call(
+    expanded, sums_one, expand_all, packed = call(
+        first_kernel,
+        [
+            ((shards, rows, width), f32),
+            ((16, width), f32),
+            ((width, C_IN), bf16),
+            ((shards, PACKED_ROWS, C_IN), bf16),
+        ],
+        [index, *pieces[4:], x],
+        name="first",
+    )
+    stack_all, project_all, gains_all = call(
         assemble_kernel,
-        [
-            ((STACK_ROWS, width), f32),
-            ((width, C_IN), bf16),
-            ((width, C_IN), bf16),
-            ((2, C_IN), f32),
-        ],
+        [((STACK_ROWS, width), f32), ((width, C_IN), bf16), ((2, C_IN), f32)],
         [index, *pieces, packed],
         name="assemble",
     )
@@ -1097,23 +1073,23 @@
     depth, sums, norm_one = call(
         functools.partial(expand_kernel, total_rows),
         [((shards, rows, width), f32), ((16, width), f32), ((32, width), f32)],
-        [gram, swap(gram, 1), x, expand_all, stack_all],
-        [((rows, width), f32), ((TAPS, 8, width), f32)],
+        [expanded, sums_one, swap(sums_one, 1), stack_all],
+        [((TAPS, 8, width), f32)],
         name="expand",
     )
-    projected, scaled, sums, gate, before, pooled, norm_two = call(
+    projected, scaled, sums, gate, before, pooled, norm_two, active = call(
         functools.partial(squeeze_kernel, total_rows),
         [
             ((shards, rows, C_IN), f32),
-            ((shards, rows, PAIR_LANES), bf16),
+            ((shards, rows, width), bf16),
             ((32, C_IN), f32),
             ((shards * 8, width), f32),
             ((shards * 8, HIDDEN_ROWS), f32),
             ((shards * 8, width), f32),
             ((32, width), f32),
+            ((shards, rows, width), f32),
         ],
-        [index, depth, sums, swap(sums, 1), stack_all, project_all, cot, bias_row],
-        [((shards, rows, width), f32), ((rows, width), bf16)],
+        [depth, sums, swap(sums, 1), stack_all, project_all, cot, bias_row],
         name="squeeze",
     )
     two, sums, lanes_grad, three_grad, output = call(
@@ -1127,11 +1103,11 @@
         ],
         [
             index, projected, cot, sums, swap(sums, 1), gains_all, depth, norm_two, stack_all,
-            project_all, gate, before, pooled, scaled, x,
+            project_all, gate, before, pooled, scaled, active, x,
         ],
         [
             ((shards, rows, C_IN), bf16),
-            ((rows, width), f32),
+            ((shards, rows, width), f32),
             ((shards * 8, width), f32),
             ((shards * 8, PAIR_LANES), f32),
         ],
@@ -1146,11 +1122,10 @@
             ((2, PAIR_LANES), f32),
         ],
         [
-            index, sums, swap(sums, 1), two, depth, x, expand_all, stack_all, lanes_grad,
+            index, sums, swap(sums, 1), two, depth, expanded, stack_all, lanes_grad,
             norm_one, norm_two,
         ],
         [
-            ((rows, PAIR_LANES), f32),
             ((TAPS, 8, PAIR_LANES), f32),
             ((TAPS, 8, PAIR_LANES), f32),
             ((24, PAIR_LANES), f32),
@@ -1160,7 +1135,7 @@
     expand_grad, input_part, one_grad = call(
         functools.partial(expand_back_kernel, total_rows),
         [((C_IN, PAIR_LANES), f32), ((rows, C_IN), f32), ((2, PAIR_LANES), f32)],
-        [index, sums, swap(sums, 1), one, x, expand_all, stack_all, norm_one],
+        [index, sums, swap(sums, 1), one, expanded, x, expand_all, stack_all, norm_one],
         [((shards, rows, PAIR_LANES), bf16)],
         name="expand_back",
     )

time: 80.6 us -> 69 us (0.86)
  Pallas kernels: 43.3 us -> 31.2 us
    pallas_call x13, Pallas kernels: 43.3 us -> 31.2 us  [call(): pl.pallas_call(kernel, out_shape=[made(shape, dtype) for shape, dtype in...]
  transfers between devices with their start and end apart: 21 -> 21, of which waited for: 8 -> 10; matrix products, arithmetic and copies ran while one was open for 0% -> 0% of each run, Pallas kernels for 22% -> 20%
where the time goes in v3:
time: 69 us; the launch traced here: 68.7 us
  Pallas kernels  31.2 us (45%)
  waiting for transfers between devices  18.9 us (27%)
  starting transfers between devices  17.2 us (25%)
  between operations  1.22 us (2%)
    pallas_call x13, Pallas kernels, call(): pl.pallas_call(kernel, out_shape=[made(shape, dtype) for shape, dtype in...  31.2 us
    ppermute x20, waiting for transfers between devices, swap(): return lax.ppermute(values, 'chan', [(at, at ^ mask) for at in range(4)])  10 us
    ppermute x20, starting transfers between devices, swap(): return lax.ppermute(values, 'chan', [(at, at ^ mask) for at in range(4)])  9.88 us
    all_to_all x1, waiting for transfers between devices, on_device_paired(): x = lax.all_to_all(copies, 'dp', 0, 0)  8.82 us
    all_to_all x1, starting transfers between devices, on_device_paired(): x = lax.all_to_all(copies, 'dp', 0, 0)  7.28 us
  transfers between devices with their start and end apart: 21, of which 10 were waited for; matrix products, arithmetic and copies ran while one was open for 0% of the time, Pallas kernels for 20%

profile of v3, /device:TPU:0, one launch (start us, length us, event | category | flops | bytes accessed | tf_op | source)
XLA Modules:
  0.0 68.7 jit_solution(18293299775908654249)
XLA Ops:
  0.8 1.9 %copies.1 = bf16[8,288,112]{2,1,0:T(8,128)(2,1)} custom-call(s32[2]{0:T(128)S(1)} %pad_add_fusion.index_ref, bf16[24,16,112]{2,1,0:T(8,128)(2,1)} %bitcast.48, bf16[24,16,28]{2,1,0:T(8,128)(2,1)} %bitcast.33), custom_call_target="tpu_custom_call" | custom-call | tf_op jit(solution)/shard_map/copies/pallas_call | solution.py:985
  2.7 7.3 %all-to-all-start = ((bf16[8,288,112]{2,1,0:T(8,128)(2,1)}), bf16[8,288,112]{2,1,0:T(8,128)(2,1)S(1)}, u32[]{:S(2)}, u32[]{:S(2)}) async-start(bf16[8,288,112]{2,1,0:T(8,128)(2,1)} %copies.1), calls=%async_computation | async-start | bytes 1179648 | tf_op jit(solution)/shard_map/all_to_all | solution.py:1031
  10.0 1.0 %pack.1 = (f32[104,168]{1,0:T(8,128)S(1)}, bf16[336,112]{1,0:T(8,128)(2,1)S(1)}) custom-call(f32[168,112]{1,0:T(8,128)} %refs_0_.1, f32[168,112]{1,0:T(8,128)} %bitcast.35, f32[25,168]{1,0:T(8,128)} %refs_6_.1, f32[28,168]{1,0:T(8,128)} %refs_12_.1, f32[28,168]{1,0:T(8,128)} %refs_18_.1, f32[1,168]{1,0:T(1,128)} %bitcast.39, f32[2,168]{1,0:T(2,128)} %refs_3_.1, ...), custom_call_target="tpu_custom_call" | custom-call | tf_op jit(solution)/shard_map/pack/pallas_call | solution.py:985
  11.0 1.6 %collective-permute-start.1 = (bf16[336,112]{1,0:T(8,128)(2,1)S(1)}, bf16[336,112]{1,0:T(8,128)(2,1)S(1)}, u32[]{:S(2)}, u32[]{:S(2)}) collective-permute-start(bf16[336,112]{1,0:T(8,128)(2,1)S(1)} %get-tuple-element.104.matrix_0), channel_id=1, source_target_pairs={{0,2},{1,3},{2,0},{3,1},{4,6},{5,7},{6,4},{7,5},{8,10},{9,11},{10,... | collective-permute-start | bytes 225800 | tf_op jit(solution)/shard_map/ppermute | solution.py:1019
  12.6 3.0 %collective-permute-done.1.matrix_2 = bf16[336,112]{1,0:T(8,128)(2,1)S(1)} collective-permute-done((bf16[336,112]{1,0:T(8,128)(2,1)S(1)}, bf16[336,112]{1,0:T(8,128)(2,1)S(1)}, u32[]{:S(2)}, u32[]{:S(2)}) %collective-permute-start.1) | collective-permute-done | bytes 75296 | tf_op jit(solution)/shard_map/ppermute | solution.py:1019
  15.6 1.5 %collective-permute-start.5 = (f32[104,168]{1,0:T(8,128)S(1)}, f32[104,168]{1,0:T(8,128)S(1)}, u32[]{:S(2)}, u32[]{:S(2)}) collective-permute-start(f32[104,168]{1,0:T(8,128)S(1)} %get-tuple-element.107.stack_0), channel_id=1, source_target_pairs={{0,2},{1,3},{2,0},{3,1},{4,6},{5,7},{6,4},{7,5},{8,10},{9,11},{10,... | collective-permute-start | bytes 209672 | tf_op jit(solution)/shard_map/ppermute | solution.py:1019
  17.1 8.8 %all-to-all-done.x_ref = bf16[8,288,112]{2,1,0:T(8,128)(2,1)S(1)} async-done(((bf16[8,288,112]{2,1,0:T(8,128)(2,1)}), bf16[8,288,112]{2,1,0:T(8,128)(2,1)S(1)}, u32[]{:S(2)}, u32[]{:S(2)}) %all-to-all-start) | async-done | bytes 516128 | tf_op jit(solution)/shard_map/all_to_all | solution.py:1031
  25.9 1.4 %first.1 = (f32[8,192,768]{2,1,0:T(8,128)S(1)}, f32[16,768]{1,0:T(8,128)S(1)}, bf16[768,112]{1,0:T(8,128)(2,1)S(1)}, bf16[8,96,112]{2,1,0:T(8,128)(2,1)S(1)}) custom-call(s32[2]{0:T(128)S(1)} %pad_add_fusion.index_ref, bf16[336,112]{1,0:T(8,128)(2,1)S(1)} %get-tuple-element.104.matrix_0, bf16[336,112]{1,0:T(8,128)(2,1)S(1)} %collective-permute-done.matrix_1, ...), custom_call_target="tpu_custom_call" | custom-call | tf_op jit(solution)/shard_map/first/pallas_call | solution.py:985
  27.4 1.6 %collective-permute-start.9 = (bf16[8,96,112]{2,1,0:T(8,128)(2,1)S(1)}, bf16[8,96,112]{2,1,0:T(8,128)(2,1)S(1)}, u32[]{:S(2)}, u32[]{:S(2)}) collective-permute-start(bf16[8,96,112]{2,1,0:T(8,128)(2,1)S(1)} %get-tuple-element.108.after_ref.own_ref), channel_id=1, source_target_pairs={{0,2},{1,3},{2,0},{3,1},{4,6},{5,7},{6,4},{7,5},{8,10},{9,11},{10,... | collective-permute-start | bytes 516104 | tf_op jit(solution)/shard_map/ppermute | solution.py:1019
  31.8 5.6 %expand.1 = (f32[8,192,768]{2,1,0:T(8,128)S(1)}, f32[16,768]{1,0:T(8,128)S(1)}, f32[32,768]{1,0:T(8,128)S(1)}) custom-call(f32[8,192,768]{2,1,0:T(8,128)S(1)} %get-tuple-element.105.expanded_ref, f32[16,768]{1,0:T(8,128)S(1)} %get-tuple-element.106.sums_own, f32[16,768]{1,0:T(8,128)S(1)} %collective-permute-done.3.sums_other, ...), custom_call_target="tpu_custom_call" | custom-call | tf_op jit(solution)/shard_map/expand/pallas_call | solution.py:985
  37.7 1.0 %collective-permute-done.9.far_ref = bf16[8,96,112]{2,1,0:T(8,128)(2,1)S(1)} collective-permute-done((bf16[8,96,112]{2,1,0:T(8,128)(2,1)S(1)}, bf16[8,96,112]{2,1,0:T(8,128)(2,1)S(1)}, u32[]{:S(2)}, u32[]{:S(2)}) %collective-permute-start.9) | collective-permute-done | bytes 172064 | tf_op jit(solution)/shard_map/ppermute | solution.py:1019
  38.8 1.5 %cot.1.cot_ref = bf16[8,192,112]{2,1,0:T(8,128)(2,1)S(1)} custom-call(s32[2]{0:T(128)S(1)} %pad_add_fusion.index_ref, bf16[8,96,112]{2,1,0:T(8,128)(2,1)S(1)} %get-tuple-element.108.after_ref.own_ref, bf16[8,96,112]{2,1,0:T(8,128)(2,1)S(1)} %collective-permute-done.8.near_ref, bf16[8,96,112]{2,1,0:T(8,128)(2,1)S(1)} %collective-permute-done.9.far_ref, ...), custom_call_target="tpu_custom_call" | custom-call | tf_op jit(solution)/shard_map/cot/pallas_call | solution.py:985
  40.3 2.7 %squeeze.29 = (f32[8,192,112]{2,1,0:T(8,128)S(1)}, bf16[8,192,768]{2,1,0:T(8,128)(2,1)S(1)}, f32[32,112]{1,0:T(8,128)S(1)}, f32[64,768]{1,0:T(8,128)S(1)}, f32[6...) custom-call(f32[8,192,768]{2,1,0:T(8,128)S(1)} %get-tuple-element.110.depth_ref, ...), custom_call_target="tpu_custom_call" | custom-call | tf_op jit(solution)/shard_map/squeeze/pallas_call | solution.py:985
  43.1 1.1 %collective-permute-done.11.sums_other = f32[32,112]{1,0:T(8,128)S(1)} collective-permute-done((f32[32,112]{1,0:T(8,128)S(1)}, f32[32,112]{1,0:T(8,128)S(1)}, u32[]{:S(2)}, u32[]{:S(2)}) %collective-permute-start.11) | collective-permute-done | bytes 14368 | tf_op jit(solution)/shard_map/ppermute | solution.py:1019
  44.2 3.8 %gate_back.1 = (f32[8,192,384]{2,1,0:T(8,128)S(1)}, f32[16,384]{1,0:T(8,128)S(1)}, f32[192,384]{1,0:T(8,128)S(1)}, f32[2,112]{1,0:T(2,128)S(1)}, bf16[192,112]{1,0:T(8,128)(2,1)S(1)}) custom-call(s32[2]{0:T(128)S(1)} %pad_add_fusion.index_ref, f32[8,192,112]{2,1,0:T(8,128)S(1)} %get-tuple-element.113.projected_ref, bf16[8,192,112]{2,1,0:T(8,128)(2,1)S(1)} %cot.1.cot_ref, ...), custom_call_target="tpu_custom_call" | custom-call | tf_op jit(solution)/shard_map/gate_back/pallas_call | solution.py:985
  48.3 1.0 %collective-permute-done.13.sums_other = f32[16,384]{1,0:T(8,128)S(1)} collective-permute-done((f32[16,384]{1,0:T(8,128)S(1)}, f32[16,384]{1,0:T(8,128)S(1)}, u32[]{:S(2)}, u32[]{:S(2)}) %collective-permute-start.13) | collective-permute-done | bytes 24608 | tf_op jit(solution)/shard_map/ppermute | solution.py:1019
  49.3 6.9 %depth_back.1 = (f32[8,192,384]{2,1,0:T(8,128)S(1)}, f32[16,384]{1,0:T(8,128)S(1)}, f32[224,384]{1,0:T(8,128)S(1)}, f32[2,384]{1,0:T(2,128)S(1)}) custom-call(s32[2]{0:T(128)S(1)} %pad_add_fusion.index_ref, f32[16,384]{1,0:T(8,128)S(1)} %get-tuple-element.123.sums_own, f32[16,384]{1,0:T(8,128)S(1)} %collective-permute-done.13.sums_other, ...), custom_call_target="tpu_custom_call" | custom-call | tf_op jit(solution)/shard_map/depth_back/pallas_call | solution.py:985
  56.9 1.2 %collective-permute-done.14.sums_other = f32[16,384]{1,0:T(8,128)S(1)} collective-permute-done((f32[16,384]{1,0:T(8,128)S(1)}, f32[16,384]{1,0:T(8,128)S(1)}, u32[]{:S(2)}, u32[]{:S(2)}) %collective-permute-start.14) | collective-permute-done | bytes 24608 | tf_op jit(solution)/shard_map/ppermute | solution.py:1019
  58.4 1.4 %expand_back.1 = (f32[112,384]{1,0:T(8,128)S(1)}, f32[192,112]{1,0:T(8,128)S(1)}, f32[2,384]{1,0:T(2,128)S(1)}) custom-call(s32[2]{0:T(128)S(1)} %pad_add_fusion.index_ref, f32[16,384]{1,0:T(8,128)S(1)} %get-tuple-element.127.sums_own, f32[16,384]{1,0:T(8,128)S(1)} %collective-permute-done.14.sums_other, f32[8,192,384]{2,1,0:T(8,128)S(1)} %get-tuple-element.128.one_ref, ...), custom_call_target="tpu_custom_call" | custom-call | tf_op jit(solution)/shard_map/expand_back/pallas_call | solution.py:985
  60.5 0.9 %collective-permute-done.17.input_other = f32[192,112]{1,0:T(8,128)S(1)} collective-permute-done((f32[192,112]{1,0:T(8,128)S(1)}, f32[192,112]{1,0:T(8,128)S(1)}, u32[]{:S(2)}, u32[]{:S(2)}) %collective-permute-start.17) | collective-permute-done | bytes 86048 | tf_op jit(solution)/shard_map/ppermute | solution.py:1019
  61.4 1.0 %settle.1 = (f32[168,112]{1,0:T(8,128)S(1)}, f32[168,112]{1,0:T(8,128)S(1)}, f32[104,168]{1,0:T(8,128)S(1)}, f32[1,32]{1,0:T(1,128)S(1)}, f32[16,128]{1,0:T(8,12...) custom-call(s32[2]{0:T(128)S(1)} %pad_add_fusion.index_ref, ...), custom_call_target="tpu_custom_call" | custom-call | tf_op jit(solution)/shard_map/settle/pallas_call | solution.py:985
  62.9 1.5 %collective-permute-start.18 = (f32[16,128]{1,0:T(8,128)S(1)}, f32[16,128]{1,0:T(8,128)S(1)}, u32[]{:S(2)}, u32[]{:S(2)}) collective-permute-start(f32[16,128]{1,0:T(8,128)S(1)} %get-tuple-element.136.square_own), channel_id=1, source_target_pairs={{0,2},{1,3},{2,0},{3,1},{4,6},{5,7},{6,4},{7,5},{8,10},{9,11},{10,... | collective-permute-start | bytes 24584 | tf_op jit(solution)/shard_map/ppermute | solution.py:1019
  64.4 1.4 %output.1 = bf16[24,16,28]{2,1,0:T(8,128)(2,1)} custom-call(s32[2]{0:T(128)S(1)} %pad_add_fusion.index_ref, bf16[192,112]{1,0:T(8,128)(2,1)S(1)} %get-tuple-element.122.own_ref, bf16[192,112]{1,0:T(8,128)(2,1)S(1)} %collective-permute-done.12.other_ref), custom_call_target="tpu_custom_call" | custom-call | tf_op jit(solution)/shard_map/output/pallas_call | solution.py:985
  66.8 1.9 %adam.1 = (f32[24,16,28]{2,1,0:T(8,128)}, f32[168,112]{1,0:T(8,128)}, f32[168,112]{1,0:T(8,128)}, f32[168,112]{1,0:T(8,128)}, f32[2,168]{1,0:T(2,128)}, /*index=...) custom-call(s32[2]{0:T(128)S(1)} %pad_add_fusion.index_ref, ...), custom_call_target="tpu_custom_call" | custom-call | tf_op jit(solution)/shard_map/adam/pallas_call | solution.py:985
  (95 shorter events, 6.5 us)
Async XLA Ops:
  0.7 37.0 %copy-start.28 = (f32[28]{0:T(128)S(1)}, f32[28]{0:T(128)}, u32[]{:S(2)}) copy-start(f32[28]{0:T(128)} %param.49) | copy-start | bytes 340
  2.7 23.2 %all-to-all-start = ((bf16[8,288,112]{2,1,0:T(8,128)(2,1)}), bf16[8,288,112]{2,1,0:T(8,128)(2,1)S(1)}, u32[]{:S(2)}, u32[]{:S(2)}) async-start(bf16[8,288,112]{2,1,0:T(8,128)(2,1)} %copies.1), calls=%async_computation | async-start | bytes 1179648 | tf_op jit(solution)/shard_map/all_to_all | solution.py:1031
  11.0 4.6 %collective-permute-start.1 = (bf16[336,112]{1,0:T(8,128)(2,1)S(1)}, bf16[336,112]{1,0:T(8,128)(2,1)S(1)}, u32[]{:S(2)}, u32[]{:S(2)}) collective-permute-start(bf16[336,112]{1,0:T(8,128)(2,1)S(1)} %get-tuple-element.104.matrix_0), channel_id=1, source_target_pairs={{0,2},{1,3},{2,0},{3,1},{4,6},{5,7},{6,4},{7,5},{8,10},{9,11},{10,... | collective-permute-start | bytes 225800 | tf_op jit(solution)/shard_map/ppermute | solution.py:1019
  12.6 4.5 %collective-permute-start = (bf16[336,112]{1,0:T(8,128)(2,1)S(1)}, bf16[336,112]{1,0:T(8,128)(2,1)S(1)}, u32[]{:S(2)}, u32[]{:S(2)}) collective-permute-start(bf16[336,112]{1,0:T(8,128)(2,1)S(1)} %get-tuple-element.104.matrix_0), channel_id=1, source_target_pairs={{0,1},{1,0},{2,3},{3,2},{4,5},{5,4},{6,7},{7,6},{8,9},{9,8},{10,11... | collective-permute-start | bytes 225800 | tf_op jit(solution)/shard_map/ppermute | solution.py:1019
  15.6 1.5 %collective-permute-start.2 = (bf16[336,112]{1,0:T(8,128)(2,1)S(1)}, bf16[336,112]{1,0:T(8,128)(2,1)S(1)}, u32[]{:S(2)}, u32[]{:S(2)}) collective-permute-start(bf16[336,112]{1,0:T(8,128)(2,1)S(1)} %collective-permute-done.1.matrix_2), channel_id=1, source_target_pairs={{0,1},{1,0},{2,3},{3,2},{4,5},{5,4},{6,7},{7,6},{8,9},{9,8},{10,11... | collective-permute-start | bytes 225800 | tf_op jit(solution)/shard_map/ppermute | solution.py:1019
  15.6 13.9 %collective-permute-start.5 = (f32[104,168]{1,0:T(8,128)S(1)}, f32[104,168]{1,0:T(8,128)S(1)}, u32[]{:S(2)}, u32[]{:S(2)}) collective-permute-start(f32[104,168]{1,0:T(8,128)S(1)} %get-tuple-element.107.stack_0), channel_id=1, source_target_pairs={{0,2},{1,3},{2,0},{3,1},{4,6},{5,7},{6,4},{7,5},{8,10},{9,11},{10,... | collective-permute-start | bytes 209672 | tf_op jit(solution)/shard_map/ppermute | solution.py:1019
  27.3 10.4 %collective-permute-start.10 = (bf16[8,96,112]{2,1,0:T(8,128)(2,1)S(1)}, bf16[8,96,112]{2,1,0:T(8,128)(2,1)S(1)}, u32[]{:S(2)}, u32[]{:S(2)}) collective-permute-start(bf16[8,96,112]{2,1,0:T(8,128)(2,1)S(1)} %get-tuple-element.108.after_ref.own_ref), channel_id=1, source_target_pairs={{0,3},{1,2},{2,1},{3,0},{4,7},{5,6},{6,5},{7,4},{8,11},{9,10},{10,... | collective-permute-start | bytes 516104 | tf_op jit(solution)/shard_map/ppermute | solution.py:1019
  27.4 11.4 %collective-permute-start.9 = (bf16[8,96,112]{2,1,0:T(8,128)(2,1)S(1)}, bf16[8,96,112]{2,1,0:T(8,128)(2,1)S(1)}, u32[]{:S(2)}, u32[]{:S(2)}) collective-permute-start(bf16[8,96,112]{2,1,0:T(8,128)(2,1)S(1)} %get-tuple-element.108.after_ref.own_ref), channel_id=1, source_target_pairs={{0,2},{1,3},{2,0},{3,1},{4,6},{5,7},{6,4},{7,5},{8,10},{9,11},{10,... | collective-permute-start | bytes 516104 | tf_op jit(solution)/shard_map/ppermute | solution.py:1019
  28.9 9.8 %collective-permute-start.8 = (bf16[8,96,112]{2,1,0:T(8,128)(2,1)S(1)}, bf16[8,96,112]{2,1,0:T(8,128)(2,1)S(1)}, u32[]{:S(2)}, u32[]{:S(2)}) collective-permute-start(bf16[8,96,112]{2,1,0:T(8,128)(2,1)S(1)} %get-tuple-element.108.after_ref.own_ref), channel_id=1, source_target_pairs={{0,1},{1,0},{2,3},{3,2},{4,5},{5,4},{6,7},{7,6},{8,9},{9,8},{10,11... | collective-permute-start | bytes 516104 | tf_op jit(solution)/shard_map/ppermute | solution.py:1019
  29.2 1.3 %collective-permute-start.4 = (f32[104,168]{1,0:T(8,128)S(1)}, f32[104,168]{1,0:T(8,128)S(1)}, u32[]{:S(2)}, u32[]{:S(2)}) collective-permute-start(f32[104,168]{1,0:T(8,128)S(1)} %get-tuple-element.107.stack_0), channel_id=1, source_target_pairs={{0,1},{1,0},{2,3},{3,2},{4,5},{5,4},{6,7},{7,6},{8,9},{9,8},{10,11... | collective-permute-start | bytes 209672 | tf_op jit(solution)/shard_map/ppermute | solution.py:1019
  29.4 1.4 %collective-permute-start.6 = (f32[104,168]{1,0:T(8,128)S(1)}, f32[104,168]{1,0:T(8,128)S(1)}, u32[]{:S(2)}, u32[]{:S(2)}) collective-permute-start(f32[104,168]{1,0:T(8,128)S(1)} %collective-permute-done.5.stack_2), channel_id=1, source_target_pairs={{0,1},{1,0},{2,3},{3,2},{4,5},{5,4},{6,7},{7,6},{8,9},{9,8},{10,11... | collective-permute-start | bytes 209672 | tf_op jit(solution)/shard_map/ppermute | solution.py:1019
  30.5 1.2 %collective-permute-start.3 = (f32[16,768]{1,0:T(8,128)S(1)}, f32[16,768]{1,0:T(8,128)S(1)}, u32[]{:S(2)}, u32[]{:S(2)}) collective-permute-start(f32[16,768]{1,0:T(8,128)S(1)} %get-tuple-element.106.sums_own), channel_id=1, source_target_pairs={{0,1},{1,0},{2,3},{3,2},{4,5},{5,4},{6,7},{7,6},{8,9},{9,8},{10,11... | collective-permute-start | bytes 147464 | tf_op jit(solution)/shard_map/ppermute | solution.py:1019
  37.4 2.9 %collective-permute-start.7 = (f32[16,768]{1,0:T(8,128)S(1)}, f32[16,768]{1,0:T(8,128)S(1)}, u32[]{:S(2)}, u32[]{:S(2)}) collective-permute-start(f32[16,768]{1,0:T(8,128)S(1)} %get-tuple-element.111.sums_own), channel_id=1, source_target_pairs={{0,1},{1,0},{2,3},{3,2},{4,5},{5,4},{6,7},{7,6},{8,9},{9,8},{10,11... | collective-permute-start | bytes 147464 | tf_op jit(solution)/shard_map/ppermute | solution.py:1019
  43.0 1.2 %collective-permute-start.11 = (f32[32,112]{1,0:T(8,128)S(1)}, f32[32,112]{1,0:T(8,128)S(1)}, u32[]{:S(2)}, u32[]{:S(2)}) collective-permute-start(f32[32,112]{1,0:T(8,128)S(1)} %get-tuple-element.114.sums_own), channel_id=1, source_target_pairs={{0,1},{1,0},{2,3},{3,2},{4,5},{5,4},{6,7},{7,6},{8,9},{9,8},{10,11... | collective-permute-start | bytes 43016 | tf_op jit(solution)/shard_map/ppermute | solution.py:1019
  48.1 1.3 %collective-permute-start.13 = (f32[16,384]{1,0:T(8,128)S(1)}, f32[16,384]{1,0:T(8,128)S(1)}, u32[]{:S(2)}, u32[]{:S(2)}) collective-permute-start(f32[16,384]{1,0:T(8,128)S(1)} %get-tuple-element.123.sums_own), channel_id=1, source_target_pairs={{0,1},{1,0},{2,3},{3,2},{4,5},{5,4},{6,7},{7,6},{8,9},{9,8},{10,11... | collective-permute-start | bytes 73736 | tf_op jit(solution)/shard_map/ppermute | solution.py:1019
  56.3 5.1 %collective-permute-start.16 = (f32[224,384]{1,0:T(8,128)S(1)}, f32[224,384]{1,0:T(8,128)S(1)}, u32[]{:S(2)}, u32[]{:S(2)}) collective-permute-start(f32[224,384]{1,0:T(8,128)S(1)} %get-tuple-element.131.keep_own), channel_id=1, source_target_pairs={{0,1},{1,0},{2,3},{3,2},{4,5},{5,4},{6,7},{7,6},{8,9},{9,8},{10,11... | collective-permute-start | bytes 1032200 | tf_op jit(solution)/shard_map/ppermute | solution.py:1019
  56.5 1.5 %collective-permute-start.14 = (f32[16,384]{1,0:T(8,128)S(1)}, f32[16,384]{1,0:T(8,128)S(1)}, u32[]{:S(2)}, u32[]{:S(2)}) collective-permute-start(f32[16,384]{1,0:T(8,128)S(1)} %get-tuple-element.127.sums_own), channel_id=1, source_target_pairs={{0,1},{1,0},{2,3},{3,2},{4,5},{5,4},{6,7},{7,6},{8,9},{9,8},{10,11... | collective-permute-start | bytes 73736 | tf_op jit(solution)/shard_map/ppermute | solution.py:1019
  58.0 8.5 %copy-start.4 = (f32[28,168]{1,0:T(8,128)S(1)}, f32[28,168]{1,0:T(8,128)}, u32[]{:S(2)}) copy-start(f32[28,168]{1,0:T(8,128)} %refs_12_.1) | copy-start | bytes 56452
  58.1 8.5 %copy-start.5 = (f32[28,168]{1,0:T(8,128)S(1)}, f32[28,168]{1,0:T(8,128)}, u32[]{:S(2)}) copy-start(f32[28,168]{1,0:T(8,128)} %refs_18_.1) | copy-start | bytes 56452
  59.8 1.6 %collective-permute-start.15 = (f32[112,384]{1,0:T(8,128)S(1)}, f32[112,384]{1,0:T(8,128)S(1)}, u32[]{:S(2)}, u32[]{:S(2)}) collective-permute-start(f32[112,384]{1,0:T(8,128)S(1)} %get-tuple-element.130.expand_own), channel_id=1, source_target_pairs={{0,1},{1,0},{2,3},{3,2},{4,5},{5,4},{6,7},{7,6},{8,9},{9,8},{10,11... | collective-permute-start | bytes 516104 | tf_op jit(solution)/shard_map/ppermute | solution.py:1019
  60.0 1.4 %collective-permute-start.17 = (f32[192,112]{1,0:T(8,128)S(1)}, f32[192,112]{1,0:T(8,128)S(1)}, u32[]{:S(2)}, u32[]{:S(2)}) collective-permute-start(f32[192,112]{1,0:T(8,128)S(1)} %get-tuple-element.135.input_own), channel_id=1, source_target_pairs={{0,1},{1,0},{2,3},{3,2},{4,5},{5,4},{6,7},{7,6},{8,9},{9,8},{10,11... | collective-permute-start | bytes 258056 | tf_op jit(solution)/shard_map/ppermute | solution.py:1019
  60.3 4.1 %collective-permute-start.12 = (bf16[192,112]{1,0:T(8,128)(2,1)S(1)}, bf16[192,112]{1,0:T(8,128)(2,1)S(1)}, u32[]{:S(2)}, u32[]{:S(2)}) collective-permute-start(bf16[192,112]{1,0:T(8,128)(2,1)S(1)} %get-tuple-element.122.own_ref), channel_id=1, source_target_pairs={{0,1},{1,0},{2,3},{3,2},{4,5},{5,4},{6,7},{7,6},{8,9},{9,8},{10,11... | collective-permute-start | bytes 129032 | tf_op jit(solution)/shard_map/ppermute | solution.py:1019
  62.4 4.2 %collective-permute-start.19 = (bf16[96,112]{1,0:T(8,128)(2,1)S(1)}, bf16[96,112]{1,0:T(8,128)(2,1)S(1)}, u32[]{:S(2)}, u32[]{:S(2)}) collective-permute-start(bf16[96,112]{1,0:T(8,128)(2,1)S(1)} %get-tuple-element.142), channel_id=1, source_target_pairs={{0,2},{1,3},{2,0},{3,1},{4,6},{5,7},{6,4},{7,5},{8,10},{9,11},{10,... | collective-permute-start | bytes 64520 | tf_op jit(solution)/shard_map/ppermute | solution.py:1019
  62.9 3.7 %collective-permute-start.18 = (f32[16,128]{1,0:T(8,128)S(1)}, f32[16,128]{1,0:T(8,128)S(1)}, u32[]{:S(2)}, u32[]{:S(2)}) collective-permute-start(f32[16,128]{1,0:T(8,128)S(1)} %get-tuple-element.136.square_own), channel_id=1, source_target_pairs={{0,2},{1,3},{2,0},{3,1},{4,6},{5,7},{6,4},{7,5},{8,10},{9,11},{10,... | collective-permute-start | bytes 24584 | tf_op jit(solution)/shard_map/ppermute | solution.py:1019
  (28 other events, 238.4 us)

commit v4 on v3

--- a/solution.py
+++ b/solution.py
@@ -377,10 +377,12 @@
 STACK_ROWS = 104
 KEEP_BIASES = 64
 KEEP_PROJECT = 80
-KEEP_KERNEL = 192
-KEEP_ROWS = 224
+KEEP_ROWS = 192
 PACKED_ROWS = 96
 BLOCK_ROWS = POSITIONS * 8
+SENT_ROWS = 256
+TAIL_ROWS = BLOCK_ROWS + PACKED_ROWS - SENT_ROWS
+TAIL_LANES = 128 - C_IN
 PAIRED_ROWS_LIMIT = 3072
 contract_lanes = (((1,), (1,)), ((), ()))
 f32 = jnp.float32
@@ -415,14 +417,76 @@
     return 0.5 * up * (1.0 + half * (1.0 - bent))
 
 
-def taps_of(row, col):
-    found = []
+PRODUCTS = 9
+FILTER_SIGNS = (
+    ((2, 1),),
+    ((3, 1), (2, -1)),
+    ((1, 1), (2, -1)),
+    ((4, 1), (2, -1)),
+    ((2, 1), (3, -1), (4, -1)),
+    ((2, 1), (3, 1), (1, -1), (4, -1)),
+    ((0, 1), (2, -1)),
+    ((2, 1), (1, 1), (3, -1), (0, -1)),
+    ((2, 1), (1, -1), (0, -1)),
+)
+
+
+def signed(terms):
+    total = None
+    for value, sign in terms:
+        if total is None:
+            total = value if sign > 0 else -value
+        else:
+            total = total + value if sign > 0 else total - value
+    return total
+
+
+def product_filters(taps, out_ref):
     for i in range(KS):
-        for j in range(KS):
-            r, c = row + i - HALF_KS, col + j - HALF_KS
-            if 0 <= r < HT and 0 <= c < WD:
-                found.append((i * KS + j, r * WD + c))
-    return found
+        for at, signs in enumerate(FILTER_SIGNS):
+            value = signed([(taps(i, column), sign) for column, sign in signs])
+            out_ref[i * PRODUCTS + at] = jnp.broadcast_to(value, out_ref.shape[1:])
+
+
+def product_inputs(field):
+    rows = []
+    for row in range(HT):
+        x0, x1, x2, x3 = field[row * WD : row * WD + WD]
+        even, odd = x0 + x2, x1 + x3
+        rows.append((even + odd, odd, even, x2 + x3, x3, x2, x0 + x1, x1, x0))
+    return list(zip(*rows))
+
+
+def product_targets(inputs):
+    both, odd, even, right, x3, x2, left, x1, x0 = inputs
+    return (both, even, odd, left, x0, x1, right, x2, x3)
+
+
+def rows_of(row):
+    return [(i, row + i - HALF_KS) for i in range(KS) if 0 <= row + i - HALF_KS < HT]
+
+
+def product_sum(filters, inputs):
+    sums = []
+    for at in range(PRODUCTS):
+        weights = [filters(i * PRODUCTS + at) for i in range(KS)]
+        found = []
+        for row in range(HT):
+            value = None
+            for i, source in rows_of(row):
+                term = weights[i] * inputs[at][source]
+                value = term if value is None else value + term
+            found.append(value)
+        sums.append(found)
+    return sums
+
+
+def product_outputs(sums, row):
+    q = [found[row] for found in sums]
+    near_0, near_1 = q[0] + q[1], q[0] + q[2]
+    return (
+        near_0 + (q[3] + q[4]), near_1 + (q[3] + q[5]), near_0 + (q[6] + q[7]), near_1 + (q[6] + q[8])
+    )
 
 
 def in_order(position, own, near, far, cross):
@@ -443,19 +507,38 @@
 
 
 def first_kernel(
-    index_ref, matrix_0, matrix_1, matrix_2, matrix_3, x_ref,
-    expanded_ref, sums_ref, we_ref, packed_ref,
+    index_ref, matrix_0, matrix_1, matrix_2, matrix_3, x_ref, _after_ref,
+    expanded_ref, sums_ref, we_ref, keep_ref, send_ref,
 ):
     blocks = x_ref.shape[0]
     width = we_ref.shape[0]
     refs = (matrix_0, matrix_1, matrix_2, matrix_3)
     we_ref[...] = matrix_in_order(index_ref[1], refs, 0, matrix_0.shape[0] // 2)
-    packed_ref[...] = x_ref[:, BLOCK_ROWS : BLOCK_ROWS + PACKED_ROWS, :]
+    tail = None
+    for piece in range(C_IN // TAIL_LANES):
+        rows = x_ref[:, piece * TAIL_ROWS : (piece + 1) * TAIL_ROWS, :].reshape(-1, 128)
+        move = one_hot(
+            128, C_IN, lambda r, c: (r - C_IN == c - piece * TAIL_LANES) & (r >= C_IN)
+        ).astype(bf16)
+        part = dot(rows, move, contract_plain)
+        tail = part if tail is None else tail + part
+    packed = jnp.concatenate(
+        [
+            x_ref[:, BLOCK_ROWS:SENT_ROWS, 0:C_IN].astype(f32),
+            tail.reshape(blocks, TAIL_ROWS, C_IN),
+        ],
+        axis=1,
+    )
+    packed = packed.reshape(blocks * PACKED_ROWS // 16, 2, 8, C_IN)
+    first = index_ref[1] % 2 == 0
+    for ref, at in ((keep_ref, 0), (send_ref, 1)):
+        half = jnp.where(first, packed[:, at], packed[:, 1 - at])
+        ref[...] = half.reshape(blocks, PACKED_ROWS // 2, C_IN).astype(bf16)
     for lanes in (slice(at, at + 256) for at in range(0, width, 256)):
         total = jnp.zeros((8, 256), f32)
         square = jnp.zeros((8, 256), f32)
         for block in range(blocks):
-            value = dot(x_ref[block, 0:BLOCK_ROWS, :], we_ref[lanes, :], contract_lanes)
+            value = dot(x_ref[block, 0:BLOCK_ROWS, 0:C_IN], we_ref[lanes, :], contract_lanes)
             expanded_ref[block, :, lanes] = value
             shaped = value.reshape(POSITIONS, 8, 256)
             total = total + jnp.sum(shaped, axis=0)
@@ -483,8 +566,7 @@
         total_rows, sums_own, sums_other, stack_ref[ROW_EXPAND_GAINS : ROW_EXPAND_GAINS + 1, :],
         stack_ref[ROW_EXPAND_GAINS + 1 : ROW_EXPAND_GAINS + 2, :], norm_ref,
     )
-    for tap in range(TAPS):
-        taps_scr[tap] = jnp.broadcast_to(stack_ref[tap : tap + 1, :], (8, width))
+    product_filters(lambda i, j: stack_ref[i * KS + j : i * KS + j + 1, :], taps_scr)
     sums_ref[...] = jnp.zeros_like(sums_ref)
 
     def one_block(block, carry):
@@ -498,13 +580,10 @@
             ]
             total = jnp.zeros((8, 128), f32)
             square = jnp.zeros((8, 128), f32)
+            sums = product_sum(lambda at: taps_scr[at, :, lanes], product_inputs(active))
             for row in range(HT):
-                for col in range(WD):
+                for col, value in enumerate(product_outputs(sums, row)):
                     at = row * WD + col
-                    value = None
-                    for tap, source in taps_of(row, col):
-                        term = taps_scr[tap, :, lanes] * active[source]
-                        value = term if value is None else value + term
                     depth_ref[block, 8 * at : 8 * at + 8, lanes] = value
                     total = total + value
                     square = square + value * value
@@ -587,7 +666,7 @@
     shift = gains_ref[1:2, :]
     mine = index_ref[0]
     output_ref[...] = (
-        x_ref[mine, 0:BLOCK_ROWS, :].astype(f32) + (projected_ref[mine] - average) * spread * gain + shift
+        x_ref[mine, 0:BLOCK_ROWS, 0:C_IN].astype(f32) + (projected_ref[mine] - average) * spread * gain + shift
     ).astype(output_ref.dtype)
     outer = gain * spread
 
@@ -652,9 +731,9 @@
 
 
 def depth_back_kernel(
-    total_rows, index_ref, sums_own, sums_other, two_ref, depth_ref, expanded_ref, stack_ref, lanes_ref,
+    total_rows, index_ref, sums_own, sums_other, two_ref, depth_ref, expanded_ref, stack_ref,
     norm_one_ref, norm_two_ref,
-    one_ref, sums_ref, kernel_ref, gains_grad_ref, taps_scr, kernel_scr, factors_scr,
+    one_ref, sums_ref, gains_grad_ref, taps_scr, kernel_scr, factors_scr,
 ):
     blocks = depth_ref.shape[0]
     own = pl.multiple_of(index_ref[1] // 2 * PAIR_LANES, 128)
@@ -670,8 +749,9 @@
     factors_scr[0:8, :] = outer
     factors_scr[8:16, :] = slope
     factors_scr[16:24, :] = outer * (beta / total_rows)
-    for tap in range(TAPS):
-        taps_scr[tap] = jnp.broadcast_to(stack_ref[tap : tap + 1, own_lanes], (8, PAIR_LANES))
+    product_filters(
+        lambda i, j: stack_ref[TAPS - 1 - i * KS - j : TAPS - i * KS - j, own_lanes], taps_scr
+    )
     sums_ref[...] = jnp.zeros_like(sums_ref)
     kernel_scr[...] = jnp.zeros_like(kernel_scr)
 
@@ -696,48 +776,49 @@
                     - slope * (depth_ref[block, spot, whole] - average_two)
                 )
                 active.append(swish_of_half(expanded_ref[block, spot, whole] * gain_half + shift_half))
-            pairs = {}
-            for row in range(HT):
-                for col in range(WD):
-                    for tap, source in taps_of(row, col):
-                        pairs.setdefault(tap, []).append((row * WD + col, source))
-            for tap in range(TAPS):
-                value = None
-                for target, source in pairs[tap]:
-                    term = grads[target] * active[source]
-                    value = term if value is None else value + term
-                kernel_scr[tap, :, lanes] += value
-            back = {}
-            for tap in range(TAPS):
-                for target, source in pairs[tap]:
-                    back.setdefault(source, []).append((tap, target))
+            sources = product_inputs(active)
+            inputs = product_inputs(grads)
+            targets = product_targets(inputs)
+            for at in range(PRODUCTS):
+                for i in range(KS):
+                    value = None
+                    for row in range(HT):
+                        if 0 <= row + i - HALF_KS < HT:
+                            term = targets[at][row] * sources[at][row + i - HALF_KS]
+                            value = term if value is None else value + term
+                    kernel_scr[i * PRODUCTS + at, :, lanes] += value
+            sums = product_sum(lambda at: taps_scr[at, :, lanes], inputs)
             total = jnp.zeros((8, 128), f32)
             product = jnp.zeros((8, 128), f32)
-            for at in range(POSITIONS):
-                spot = slice(8 * at, 8 * at + 8)
-                value = None
-                for tap, target in back[at]:
-                    term = taps_scr[tap, :, lanes] * grads[target]
-                    value = term if value is None else value + term
-                expanded = expanded_ref[block, spot, whole]
-                value = value * slope_of_half(expanded * gain_half + shift_half)
-                one_ref[block, spot, lanes] = value
-                total = total + value
-                product = product + value * (expanded - average_one)
+            for row in range(HT):
+                for col, value in enumerate(product_outputs(sums, row)):
+                    at = row * WD + col
+                    spot = slice(8 * at, 8 * at + 8)
+                    expanded = expanded_ref[block, spot, whole]
+                    value = value * slope_of_half(expanded * gain_half + shift_half)
+                    one_ref[block, spot, lanes] = value
+                    total = total + value
+                    product = product + value * (expanded - average_one)
             sums_ref[0:8, lanes] += total
             sums_ref[8:16, lanes] += product
         return carry
 
     lax.fori_loop(0, blocks, one_block, 0)
-    kernel_ref[0:KEEP_KERNEL, :] = lanes_ref[...]
-    kernel_ref[KEEP_KERNEL : KEEP_KERNEL + 32, :] = jnp.zeros((32, PAIR_LANES), f32)
-    for tap in range(TAPS):
-        row = KEEP_KERNEL + tap
-        kernel_ref[row : row + 1, :] = jnp.sum(kernel_scr[tap], axis=0, keepdims=True)
+    for i in range(KS):
+        for j in range(KS):
+            terms = [
+                (jnp.sum(kernel_scr[i * PRODUCTS + at], axis=0, keepdims=True), sign)
+                for at, signs in enumerate(FILTER_SIGNS)
+                for column, sign in signs
+                if column == j
+            ]
+            row = 16 + i * KS + j
+            sums_ref[row : row + 1, :] = signed(terms)
 
 
 def expand_back_kernel(
     total_rows, index_ref, sums_own, sums_other, one_ref, expanded_ref, x_ref, we_ref, stack_ref, norm_ref,
+    _output_ref, _lanes_ref,
     expand_ref, input_ref, gains_grad_ref, delta_scr,
 ):
     blocks = x_ref.shape[0]
@@ -760,7 +841,7 @@
         delta_scr[block] = delta.astype(bf16)
     rows = blocks * POSITIONS * 8
     expand_ref[...] = dot(
-        x_ref[:, 0:BLOCK_ROWS, :].reshape(rows, C_IN), delta_scr[...].reshape(rows, PAIR_LANES), contract_rows
+        x_ref[:, 0:BLOCK_ROWS, 0:C_IN].reshape(rows, C_IN), delta_scr[...].reshape(rows, PAIR_LANES), contract_rows
     )
     input_ref[...] = dot(delta_scr[index_ref[0]], own_weights, contract_plain)
 
@@ -775,7 +856,7 @@
 def copies_kernel(index_ref, rows_ref, cot_ref, copies_ref):
     whole = rows_ref[...].astype(f32)
     half = jnp.where(index_ref[1] % 2 == 0, whole[:, 0:8, :], whole[:, 8:16, :])
-    half = half.reshape(BLOCK_ROWS, C_IN).astype(bf16)
+    half = half.reshape(BLOCK_ROWS, C_IN)
     narrow = cot_ref.shape[2]
     rows = cot_ref[...].reshape(4 * PACKED_ROWS, narrow)
     packed = None
@@ -783,19 +864,26 @@
         place = one_hot(narrow, C_IN, lambda r, c: c == r + group * narrow).astype(bf16)
         part = dot(rows[group * PACKED_ROWS : (group + 1) * PACKED_ROWS], place, contract_plain)
         packed = part if packed is None else packed + part
-    packed = packed.astype(bf16)
+    value = jnp.concatenate([half, packed], axis=0).astype(bf16)
+    widen = one_hot(C_IN, 128, lambda r, c: r == c).astype(bf16)
+    dense = dot(value[0:SENT_ROWS], widen, contract_plain)
+    parts = []
+    for piece in range(SENT_ROWS // TAIL_ROWS):
+        move = one_hot(
+            C_IN, 128, lambda r, c: (c - C_IN == r - piece * TAIL_LANES) & (c >= C_IN)
+        ).astype(bf16)
+        parts.append(dot(value[SENT_ROWS:], move, contract_plain))
+    dense = (dense + jnp.concatenate(parts, axis=0)).astype(bf16)
     for at in range(copies_ref.shape[0]):
-        copies_ref[at, 0:BLOCK_ROWS, :] = half
-        copies_ref[at, BLOCK_ROWS : BLOCK_ROWS + PACKED_ROWS, :] = packed
+        copies_ref[at] = dense
 
 
 def cot_kernel(index_ref, own_ref, near_ref, far_ref, cross_ref, cot_ref):
     position = index_ref[1]
-    first = position % 2 == 0
     near = position + 1 - position % 2 * 2
     blocks = cot_ref.shape[0]
     narrow = C_IN // 4
-    rows = blocks * PACKED_ROWS
+    rows = blocks * PACKED_ROWS // 2
     pieces = (
         (own_ref, position), (near_ref, near), (far_ref, (position + 2) % 4),
         (cross_ref, (near + 2) % 4),
@@ -811,9 +899,7 @@
             ).astype(bf16)
             part = dot(ref[...].reshape(rows, C_IN), move, contract_plain)
             total = part if total is None else total + part
-        total = total.reshape(rows // 16, 16, C_IN)
-        half = jnp.where(first, total[:, 0:8, :], total[:, 8:16, :])
-        half = half.reshape(blocks, PACKED_ROWS // 2, C_IN).astype(bf16)
+        half = total.reshape(blocks, PACKED_ROWS // 2, C_IN).astype(bf16)
         start = group * (PACKED_ROWS // 2)
         cot_ref[:, start : start + PACKED_ROWS // 2, :] = half
 
@@ -839,7 +925,7 @@
 
 def assemble_kernel(
     index_ref, stack_0, stack_1, stack_2, stack_3, matrix_0, matrix_1, matrix_2, matrix_3,
-    after_ref, stack_ref, project_ref, gains_ref,
+    stack_ref, project_ref, gains_ref,
 ):
     channels = stack_0.shape[1]
     narrow = C_IN // 4
@@ -855,52 +941,44 @@
     project_ref[...] = matrix_in_order(index_ref[1], refs, channels, channels)
 
 
+def kept_sums(keep_own, keep_other, sums_own, sums_other):
+    def both(start, stop):
+        return keep_own[start:stop, :] + keep_other[start:stop, :]
+
+    return (
+        both(KEEP_PROJECT, KEEP_PROJECT + C_IN), both(0, 2 * HIDDEN_ROWS),
+        sums_own[16 : 16 + TAPS, :] + sums_other[16 : 16 + TAPS, :],
+        both(KEEP_BIASES, KEEP_BIASES + 1), both(KEEP_BIASES + 8, KEEP_BIASES + 9)[:, 0:HIDDEN_ROWS],
+    )
+
+
+def both_halves(first, own, other):
+    own = own.reshape(POSITIONS, 8, own.shape[-1])
+    other = other.reshape(POSITIONS, 8, other.shape[-1])
+    return jnp.concatenate(
+        [jnp.where(first, own, other), jnp.where(first, other, own)], axis=1
+    )
+
+
 def settle_kernel(
-    index_ref, expand_own, expand_other, keep_own, keep_other, three_ref, two_ref, one_ref,
-    input_own, input_other,
-    expand_ref, project_ref, lanes_ref, bias_ref, square_ref, input_ref, packed_ref,
+    index_ref, expand_own, expand_other, keep_own, keep_other, sums_own, sums_other, three_ref, two_ref, one_ref,
+    input_own, input_other, square_ref, packed_ref,
 ):
     position = index_ref[1]
-    first = position % 2 == 0
-    channels = expand_ref.shape[0]
     narrow = C_IN // 4
 
     def squared(values):
         return jnp.sum(jnp.sum(values * values, axis=0, keepdims=True), axis=1, keepdims=True)
 
-    def mine(values):
-        return jnp.where(first, values[:, 0:channels], values[:, channels : 2 * channels])
-
-    def both(start, stop):
-        return keep_own[start:stop, :] + keep_other[start:stop, :]
-
-    expand = expand_own[...] + expand_other[...]
-    project = both(KEEP_PROJECT, KEEP_PROJECT + C_IN)
-    hidden = both(0, 2 * HIDDEN_ROWS)
-    excite_bias = both(KEEP_BIASES, KEEP_BIASES + 1)
-    kernel = both(KEEP_KERNEL, KEEP_KERNEL + 32)
-    total = squared(expand) + squared(project) + squared(hidden) + squared(kernel)
-    total = total + squared(excite_bias) + squared(one_ref[...]) + squared(two_ref[...])
-    bias = both(KEEP_BIASES + 8, KEEP_BIASES + 9)[:, 0:HIDDEN_ROWS]
+    project, hidden, kernel, excite_bias, bias = kept_sums(keep_own, keep_other, sums_own, sums_other)
+    total = squared(expand_own[...] + expand_other[...]) + squared(project) + squared(hidden)
+    total = total + squared(kernel) + squared(excite_bias)
+    total = total + squared(one_ref[...]) + squared(two_ref[...])
     square_ref[0:8, :] = jnp.broadcast_to(total, (8, 128))
     square_ref[8:16, :] = jnp.broadcast_to(squared(bias) + squared(three_ref[...]), (8, 128))
-    bias_ref[...] = bias
-    expand_ref[...] = jnp.transpose(mine(expand))
-    project_ref[...] = jnp.transpose(mine(project))
-    lanes_ref[0:32, :] = mine(kernel)
-    lanes_ref[ROW_SQUEEZE : ROW_SQUEEZE + 2 * HIDDEN_ROWS, :] = mine(hidden)
-    lanes_ref[ROW_EXCITE_BIAS : ROW_EXCITE_BIAS + 1, :] = mine(excite_bias)
-    lanes_ref[ROW_EXPAND_GAINS : ROW_EXPAND_GAINS + 2, :] = mine(one_ref[...])
-    lanes_ref[ROW_DEPTH_GAINS : ROW_DEPTH_GAINS + 2, :] = mine(two_ref[...])
-    own = input_own[...].reshape(POSITIONS, 8, C_IN)
-    other = input_other[...].reshape(POSITIONS, 8, C_IN)
-    whole = jnp.concatenate(
-        [jnp.where(first, own, other), jnp.where(first, other, own)], axis=1
-    ).reshape(4 * PACKED_ROWS, C_IN)
-    pick = one_hot(C_IN, narrow, lambda r, c: r == c + position * narrow).astype(f32)
-    input_ref[...] = highest(whole, pick, contract_plain).reshape(POSITIONS, 16, narrow)
+    whole = both_halves(position % 2 == 0, input_own[...], input_other[...])
+    whole = whole.reshape(4 * PACKED_ROWS, C_IN).astype(bf16)
     across = position + 2 - position // 2 * 4
-    low = whole.astype(bf16)
     packed = None
     for group in range(4):
         move = one_hot(
@@ -909,36 +987,66 @@
             lambda r, c: (r - across * narrow == c - group * narrow)
             & (c >= group * narrow) & (c < (group + 1) * narrow),
         ).astype(bf16)
-        part = dot(low[group * PACKED_ROWS : (group + 1) * PACKED_ROWS], move, contract_plain)
+        part = dot(whole[group * PACKED_ROWS : (group + 1) * PACKED_ROWS], move, contract_plain)
         packed = part if packed is None else packed + part
-    packed_ref[...] = packed.astype(bf16)
-
-
-def output_kernel(index_ref, own_ref, other_ref, output_ref):
-    first = index_ref[1] % 2 == 0
-    narrow = output_ref.shape[2]
-    pick = one_hot(C_IN, narrow, lambda r, c: r == c + index_ref[1] * narrow).astype(bf16)
-    own = dot(own_ref[...], pick, contract_plain).reshape(POSITIONS, 8, narrow)
-    other = dot(other_ref[...], pick, contract_plain).reshape(POSITIONS, 8, narrow)
-    output_ref[...] = jnp.concatenate(
-        [jnp.where(first, own, other), jnp.where(first, other, own)], axis=1
-    ).astype(bf16)
+    packed_ref[0:PACKED_ROWS, :] = packed.astype(bf16)
+    rest = jnp.broadcast_to(total, (16, C_IN))
+    parts = jnp.zeros((16, C_IN), f32)
+    row = lax.broadcasted_iota(jnp.int32, (16, C_IN), 0)
+    for at in range(3):
+        part = rest.astype(bf16).astype(f32)
+        rest = rest - part
+        parts = jnp.where(row == at, part, parts)
+    packed_ref[PACKED_ROWS : PACKED_ROWS + 16, :] = parts.astype(bf16)
+
+
+def own_kernel(
+    index_ref, expand_own, expand_other, keep_own, keep_other, sums_own, sums_other, two_ref, one_ref,
+    input_own, input_other, output_own, output_other,
+    expand_ref, project_ref, lanes_ref, bias_ref, input_ref, output_ref,
+):
+    position = index_ref[1]
+    first = position % 2 == 0
+    channels = expand_ref.shape[0]
+    narrow = C_IN // 4
+
+    def mine(values):
+        return jnp.where(first, values[:, 0:channels], values[:, channels : 2 * channels])
+
+    project, hidden, kernel, excite_bias, bias = kept_sums(keep_own, keep_other, sums_own, sums_other)
+    bias_ref[...] = bias
+    expand_ref[...] = jnp.transpose(mine(expand_own[...] + expand_other[...]))
+    project_ref[...] = jnp.transpose(mine(project))
+    lanes_ref[0:TAPS, :] = mine(kernel)
+    lanes_ref[ROW_SQUEEZE : ROW_SQUEEZE + 2 * HIDDEN_ROWS, :] = mine(hidden)
+    lanes_ref[ROW_EXCITE_BIAS : ROW_EXCITE_BIAS + 1, :] = mine(excite_bias)
+    lanes_ref[ROW_EXPAND_GAINS : ROW_EXPAND_GAINS + 2, :] = mine(one_ref[...])
+    lanes_ref[ROW_DEPTH_GAINS : ROW_DEPTH_GAINS + 2, :] = mine(two_ref[...])
+    pick = one_hot(C_IN, narrow, lambda r, c: r == c + position * narrow)
+    halves = [
+        highest(ref[...], pick.astype(f32), contract_plain) for ref in (input_own, input_other)
+    ]
+    input_ref[...] = both_halves(first, *halves)
+    halves = [dot(ref[...], pick.astype(bf16), contract_plain) for ref in (output_own, output_other)]
+    output_ref[...] = both_halves(first, *halves).astype(bf16)
 
 
 def adam_kernel(
-    index_ref, square_own, square_other, expand_grad, project_grad, lanes_grad, bias_grad, three_grad,
+    index_ref, square_ref, expand_grad, project_grad, lanes_grad, bias_grad, three_grad,
     input_own, packed_other, cot_ref, *refs,
 ):
     params, outs = refs[:30], refs[30:]
     narrow = cot_ref.shape[2]
-    total = square_own[0:1, 0:1] + square_other[0:1, 0:1] + square_own[8:9, 0:1]
+    parts = packed_other[PACKED_ROWS : PACKED_ROWS + 16, :].astype(f32)
+    other = (parts[0:1, 0:1] + parts[1:2, 0:1]) + parts[2:3, 0:1]
+    total = square_ref[0:1, 0:1] + other + square_ref[8:9, 0:1]
     grad_norm = jnp.sqrt(total)
     factor = clip_limit / jnp.maximum(grad_norm, clip_limit)
     outs[31][...] = grad_norm
     groups = []
     for group in range(4):
         pick = one_hot(C_IN, narrow, lambda r, c: r == c + group * narrow).astype(bf16)
-        groups.append(dot(packed_other[...], pick, contract_plain))
+        groups.append(dot(packed_other[0:PACKED_ROWS, :], pick, contract_plain))
     crossed = jnp.concatenate(groups, axis=0).reshape(POSITIONS, 16, narrow)
     outs[0][...] = input_own[...] + crossed + cot_ref[...].astype(f32)
     pick = one_hot(C_IN, narrow, lambda r, c: r == c + index_ref[1] * narrow).astype(f32)
@@ -967,24 +1075,27 @@
             outs[1 + 3 * entry + part][...] = updated[part]
 
 
-def call(kernel, outs, operands, scratch=(), name=None, keep=True, place=True):
+def call(kernel, outs, operands, scratch=(), name=None, keep=True, place=True, after=()):
     spaces = [
         pl.BlockSpec(memory_space=pltpu.SMEM)
         if operand.dtype == jnp.int32
         else pl.BlockSpec(memory_space=pltpu.VMEM)
         for operand in operands
     ]
+    spaces += [pl.BlockSpec(memory_space=pl.ANY)] * len(after)
     operands = [
         operand
         if operand.dtype == jnp.int32
         else pltpu.with_memory_space_constraint(operand, pltpu.VMEM if place else pltpu.HBM)
         for operand in operands
-    ]
+    ] + [pltpu.with_memory_space_constraint(operand, pltpu.HBM) for operand in after]
     limit = 4 * 1024 * 1024 + sum(4 * math.prod(shape) for shape, _ in scratch)
     made = pltpu.VMEM if keep else jax.ShapeDtypeStruct
     return pl.pallas_call(
         kernel,
-        out_shape=[made(shape, dtype) for shape, dtype in outs],
+        out_shape=[
+            (jax.ShapeDtypeStruct if out[2:] else made)(out[0], out[1]) for out in outs
+        ],
         in_specs=spaces,
         out_specs=[pl.BlockSpec(memory_space=pltpu.VMEM)] * len(outs),
         scratch_shapes=[pltpu.VMEM(shape, dtype) for shape, dtype in scratch],
@@ -1022,7 +1133,7 @@
     cot_rows = jnp.transpose(cotangent, (1, 2, 3, 0)).reshape(POSITIONS, segments, narrow)
     (copies,) = call(
         copies_kernel,
-        [((shards, rows + PACKED_ROWS, C_IN), bf16)],
+        [((shards, SENT_ROWS, 128), bf16)],
         [index, input_rows, cot_rows],
         name="copies",
         keep=False,
@@ -1045,27 +1156,30 @@
         stack, swap(stack, 1), stack_far, swap(stack_far, 1),
         matrix, swap(matrix, 1), matrix_far, swap(matrix_far, 1),
     ]
-    expanded, sums_one, expand_all, packed = call(
+    stack_all, project_all, gains_all = call(
+        assemble_kernel,
+        [((STACK_ROWS, width), f32), ((width, C_IN), bf16), ((2, C_IN), f32)],
+        [index, *pieces],
+        name="assemble",
+        keep=False,
+    )
+    expanded, sums_one, expand_all, kept, sent = call(
         first_kernel,
         [
             ((shards, rows, width), f32),
             ((16, width), f32),
             ((width, C_IN), bf16),
-            ((shards, PACKED_ROWS, C_IN), bf16),
+            ((shards, PACKED_ROWS // 2, C_IN), bf16),
+            ((shards, PACKED_ROWS // 2, C_IN), bf16),
         ],
         [index, *pieces[4:], x],
         name="first",
-    )
-    stack_all, project_all, gains_all = call(
-        assemble_kernel,
-        [((STACK_ROWS, width), f32), ((width, C_IN), bf16), ((2, C_IN), f32)],
-        [index, *pieces, packed],
-        name="assemble",
+        after=[gains_all],
     )
     (cot,) = call(
         cot_kernel,
         [((shards, rows, C_IN), bf16)],
-        [index, packed, swap(packed, 1), swap(packed, 2), swap(packed, 3)],
+        [index, kept, swap(sent, 1), swap(kept, 2), swap(sent, 3)],
         name="cot",
     )
     bias_row = jnp.pad(squeeze_bias, ((0, 0), (0, HIDDEN_ROWS - squeeze_bias.shape[1])))
@@ -1074,7 +1188,7 @@
         functools.partial(expand_kernel, total_rows),
         [((shards, rows, width), f32), ((16, width), f32), ((32, width), f32)],
         [expanded, sums_one, swap(sums_one, 1), stack_all],
-        [((TAPS, 8, width), f32)],
+        [((KS * PRODUCTS, 8, width), f32)],
         name="expand",
     )
     projected, scaled, sums, gate, before, pooled, norm_two, active = call(
@@ -1097,7 +1211,7 @@
         [
             ((shards, rows, PAIR_LANES), f32),
             ((16, PAIR_LANES), f32),
-            ((KEEP_KERNEL, PAIR_LANES), f32),
+            ((KEEP_ROWS, PAIR_LANES), f32),
             ((2, C_IN), f32),
             ((rows, C_IN), bf16),
         ],
@@ -1113,55 +1227,57 @@
         ],
         name="gate_back",
     )
-    one, sums, keep, two_grad = call(
+    output_other = swap(output, 1)
+    lanes_other = swap(lanes_grad, 1)
+    one, sums, two_grad = call(
         functools.partial(depth_back_kernel, total_rows),
         [
             ((shards, rows, PAIR_LANES), f32),
-            ((16, PAIR_LANES), f32),
-            ((KEEP_ROWS, PAIR_LANES), f32),
+            ((48, PAIR_LANES), f32),
             ((2, PAIR_LANES), f32),
         ],
         [
-            index, sums, swap(sums, 1), two, depth, expanded, stack_all, lanes_grad,
-            norm_one, norm_two,
+            index, sums, swap(sums, 1), two, depth, expanded, stack_all, norm_one, norm_two,
         ],
         [
-            ((TAPS, 8, PAIR_LANES), f32),
-            ((TAPS, 8, PAIR_LANES), f32),
+            ((KS * PRODUCTS, 8, PAIR_LANES), f32),
+            ((KS * PRODUCTS, 8, PAIR_LANES), f32),
             ((24, PAIR_LANES), f32),
         ],
         name="depth_back",
     )
+    sums_other = swap(sums, 1)
     expand_grad, input_part, one_grad = call(
         functools.partial(expand_back_kernel, total_rows),
         [((C_IN, PAIR_LANES), f32), ((rows, C_IN), f32), ((2, PAIR_LANES), f32)],
-        [index, sums, swap(sums, 1), one, expanded, x, expand_all, stack_all, norm_one],
+        [
+            index, sums, sums_other, one, expanded, x, expand_all, stack_all, norm_one,
+            output_other, lanes_other,
+        ],
         [((shards, rows, PAIR_LANES), bf16)],
         name="expand_back",
     )
-    expand_own, project_own, lanes_own, bias_own, square, input_own, packed = call(
+    expand_pair = [expand_grad, swap(expand_grad, 1)]
+    keep_pair = [lanes_grad, lanes_other, sums, sums_other]
+    input_pair = [input_part, swap(input_part, 1)]
+    square, packed = call(
         settle_kernel,
+        [((16, 128), f32), ((PACKED_ROWS + 16, C_IN), bf16)],
+        [index, *expand_pair, *keep_pair, three_grad, two_grad, one_grad, *input_pair],
+        name="settle",
+    )
+    expand_own, project_own, lanes_own, bias_own, input_own, block_output = call(
+        own_kernel,
         [
             ((channels, C_IN), f32),
             ((channels, C_IN), f32),
             ((STACK_ROWS, channels), f32),
             ((1, HIDDEN_ROWS), f32),
-            ((16, 128), f32),
             ((POSITIONS, segments, narrow), f32),
-            ((PACKED_ROWS, C_IN), bf16),
+            ((POSITIONS, segments, narrow), bf16, False),
         ],
-        [
-            index, expand_grad, swap(expand_grad, 1), keep, swap(keep, 1), three_grad, two_grad,
-            one_grad, input_part, swap(input_part, 1),
-        ],
-        name="settle",
-    )
-    (block_output,) = call(
-        output_kernel,
-        [((POSITIONS, segments, narrow), bf16)],
-        [index, output, swap(output, 1)],
-        name="output",
-        keep=False,
+        [index, *expand_pair, *keep_pair, two_grad, one_grad, *input_pair, output, output_other],
+        name="own",
     )
     updated = call(
         adam_kernel,
@@ -1169,7 +1285,7 @@
         + [(value.shape, f32) for value in params]
         + [((1, 1), f32)],
         [
-            index, square, swap(square, 2), expand_own, project_own, lanes_own, bias_own, three_grad,
+            index, square, expand_own, project_own, lanes_own, bias_own, three_grad,
             input_own, swap(packed, 2), cot_rows, *params,
         ],
         name="adam",

time: 69 us -> 62 us (0.90)
  waiting for transfers between devices: 18.9 us -> 14.4 us
  Pallas kernels: 31.2 us -> 29 us
  starting transfers between devices: 17.2 us -> 16.2 us
    all_to_all x1, waiting for transfers between devices: 8.82 us -> 4.24 us  [on_device_paired(): x = lax.all_to_all(copies, 'dp', 0, 0)]
    pallas_call x13, Pallas kernels: 31.2 us -> 29 us  [call(): pl.pallas_call(kernel, out_shape=[(jax.ShapeDtypeStruct if out[2:] else m...]
    ppermute x20 -> x19, starting transfers between devices: 9.88 us -> 8.89 us  [swap(): return lax.ppermute(values, 'chan', [(at, at ^ mask) for at in range(4)])]
    ppermute x20 -> x19, waiting for transfers between devices: 10 us -> 10.2 us  [swap(): return lax.ppermute(values, 'chan', [(at, at ^ mask) for at in range(4)])]
  transfers between devices with their start and end apart: 21 -> 20, of which waited for: 10 -> 10; matrix products, arithmetic and copies ran while one was open for 0% -> 0% of each run, Pallas kernels for 20% -> 24%
where the time goes in v4:
time: 62 us; the launch traced here: 61.7 us
  Pallas kernels  29 us (47%)
  starting transfers between devices  16.2 us (26%)
  waiting for transfers between devices  14.4 us (23%)
  between operations  1.27 us (2%)
  local copies, waits for them, and re-layouts  0.76 us (1%)
    pallas_call x13, Pallas kernels, call(): pl.pallas_call(kernel, out_shape=[(jax.ShapeDtypeStruct if out[2:] else m...  29 us
    ppermute x19, waiting for transfers between devices, swap(): return lax.ppermute(values, 'chan', [(at, at ^ mask) for at in range(4)])  10.2 us
    ppermute x19, starting transfers between devices, swap(): return lax.ppermute(values, 'chan', [(at, at ^ mask) for at in range(4)])  8.89 us
    all_to_all x1, starting transfers between devices, on_device_paired(): x = lax.all_to_all(copies, 'dp', 0, 0)  7.28 us
    all_to_all x1, waiting for transfers between devices, on_device_paired(): x = lax.all_to_all(copies, 'dp', 0, 0)  4.24 us
  transfers between devices with their start and end apart: 20, of which 10 were waited for; matrix products, arithmetic and copies ran while one was open for 0% of the time, Pallas kernels for 24%

profile of v4, /device:TPU:0, one launch (start us, length us, event | category | flops | bytes accessed | tf_op | source)
XLA Modules:
  0.0 61.7 jit_solution(11154435696984735875)
XLA Ops:
  0.8 2.1 %copies.1 = bf16[8,256,128]{2,1,0:T(8,128)(2,1)} custom-call(s32[2]{0:T(128)S(1)} %pad_add_fusion.index_ref, bf16[24,16,112]{2,1,0:T(8,128)(2,1)} %bitcast.47, bf16[24,16,28]{2,1,0:T(8,128)(2,1)} %bitcast.33), custom_call_target="tpu_custom_call" | custom-call | tf_op jit(solution)/shard_map/copies/pallas_call | solution.py:1094
  2.9 7.3 %all-to-all-start = ((bf16[8,256,128]{2,1,0:T(8,128)(2,1)}), bf16[8,256,128]{2,1,0:T(8,128)(2,1)S(1)}, u32[]{:S(2)}, u32[]{:S(2)}) async-start(bf16[8,256,128]{2,1,0:T(8,128)(2,1)} %copies.1), calls=%async_computation | async-start | bytes 1048576 | tf_op jit(solution)/shard_map/all_to_all | solution.py:1142
  10.2 1.0 %pack.1 = (f32[104,168]{1,0:T(8,128)S(1)}, bf16[336,112]{1,0:T(8,128)(2,1)S(1)}) custom-call(f32[168,112]{1,0:T(8,128)} %refs_0_.1, f32[168,112]{1,0:T(8,128)} %bitcast.35, f32[25,168]{1,0:T(8,128)} %refs_6_.1, f32[28,168]{1,0:T(8,128)} %refs_12_.1, f32[28,168]{1,0:T(8,128)} %refs_18_.1, f32[1,168]{1,0:T(1,128)} %bitcast.39, f32[2,168]{1,0:T(2,128)} %refs_3_.1, ...), custom_call_target="tpu_custom_call" | custom-call | tf_op jit(solution)/shard_map/pack/pallas_call | solution.py:1094
  11.2 1.6 %collective-permute-start.1 = (bf16[336,112]{1,0:T(8,128)(2,1)S(1)}, bf16[336,112]{1,0:T(8,128)(2,1)S(1)}, u32[]{:S(2)}, u32[]{:S(2)}) collective-permute-start(bf16[336,112]{1,0:T(8,128)(2,1)S(1)} %get-tuple-element.105.matrix_0), channel_id=1, source_target_pairs={{0,2},{1,3},{2,0},{3,1},{4,6},{5,7},{6,4},{7,5},{8,10},{9,11},{10,... | collective-permute-start | bytes 225800 | tf_op jit(solution)/shard_map/ppermute | solution.py:1130
  13.3 3.4 %collective-permute-done.1.matrix_2 = bf16[336,112]{1,0:T(8,128)(2,1)S(1)} collective-permute-done((bf16[336,112]{1,0:T(8,128)(2,1)S(1)}, bf16[336,112]{1,0:T(8,128)(2,1)S(1)}, u32[]{:S(2)}, u32[]{:S(2)}) %collective-permute-start.1) | collective-permute-done | bytes 75296 | tf_op jit(solution)/shard_map/ppermute | solution.py:1130
  18.2 1.0 %collective-permute-done.5.stack_3 = f32[104,168]{1,0:T(8,128)S(1)} collective-permute-done((f32[104,168]{1,0:T(8,128)S(1)}, f32[104,168]{1,0:T(8,128)S(1)}, u32[]{:S(2)}, u32[]{:S(2)}) %collective-permute-start.5) | collective-permute-done | bytes 69920 | tf_op jit(solution)/shard_map/ppermute | solution.py:1130
  20.4 4.2 %all-to-all-done.x_ref = bf16[8,256,128]{2,1,0:T(8,128)(2,1)S(1)} async-done(((bf16[8,256,128]{2,1,0:T(8,128)(2,1)}), bf16[8,256,128]{2,1,0:T(8,128)(2,1)S(1)}, u32[]{:S(2)}, u32[]{:S(2)}) %all-to-all-start) | async-done | bytes 524320 | tf_op jit(solution)/shard_map/all_to_all | solution.py:1142
  24.7 1.5 %first.1 = (f32[8,192,768]{2,1,0:T(8,128)S(1)}, f32[16,768]{1,0:T(8,128)S(1)}, bf16[768,112]{1,0:T(8,128)(2,1)S(1)}, bf16[8,48,112]{2,1,0:T(8,128)(2,1)S(1)}, bf16[8,48,112]{2,1,0:T(8,128)(2,1)S(1)}) custom-call(s32[2]{0:T(128)S(1)} %pad_add_fusion.index_ref, bf16[336,112]{1,0:T(8,128)(2,1)S(1)} %get-tuple-element.105.matrix_0, ...), custom_call_target="tpu_custom_call" | custom-call | tf_op jit(solution)/shard_map/first/pallas_call | solution.py:1094
  26.3 1.6 %collective-permute-start.9 = (bf16[8,48,112]{2,1,0:T(8,128)(2,1)S(1)}, bf16[8,48,112]{2,1,0:T(8,128)(2,1)S(1)}, u32[]{:S(2)}, u32[]{:S(2)}) collective-permute-start(bf16[8,48,112]{2,1,0:T(8,128)(2,1)S(1)} %get-tuple-element.114.own_ref), channel_id=1, source_target_pairs={{0,2},{1,3},{2,0},{3,1},{4,6},{5,7},{6,4},{7,5},{8,10},{9,11},{10,... | collective-permute-start | bytes 258056 | tf_op jit(solution)/shard_map/ppermute | solution.py:1130
  28.5 4.5 %expand.1 = (f32[8,192,768]{2,1,0:T(8,128)S(1)}, f32[16,768]{1,0:T(8,128)S(1)}, f32[32,768]{1,0:T(8,128)S(1)}) custom-call(f32[8,192,768]{2,1,0:T(8,128)S(1)} %get-tuple-element.108.expanded_ref, f32[16,768]{1,0:T(8,128)S(1)} %get-tuple-element.109.sums_own, f32[16,768]{1,0:T(8,128)S(1)} %collective-permute-done.6.sums_other, ...), custom_call_target="tpu_custom_call" | custom-call | tf_op jit(solution)/shard_map/expand/pallas_call | solution.py:1094
  33.3 1.1 %cot.1.cot_ref = bf16[8,192,112]{2,1,0:T(8,128)(2,1)S(1)} custom-call(s32[2]{0:T(128)S(1)} %pad_add_fusion.index_ref, bf16[8,48,112]{2,1,0:T(8,128)(2,1)S(1)} %get-tuple-element.114.own_ref, bf16[8,48,112]{2,1,0:T(8,128)(2,1)S(1)} %collective-permute-done.8.near_ref, bf16[8,48,112]{2,1,0:T(8,128)(2,1)S(1)} %collective-permute-done.9.far_ref, ...), custom_call_target="tpu_custom_call" | custom-call | tf_op jit(solution)/shard_map/cot/pallas_call | solution.py:1094
  34.4 2.7 %squeeze.29 = (f32[8,192,112]{2,1,0:T(8,128)S(1)}, bf16[8,192,768]{2,1,0:T(8,128)(2,1)S(1)}, f32[32,112]{1,0:T(8,128)S(1)}, f32[64,768]{1,0:T(8,128)S(1)}, f32[6...) custom-call(f32[8,192,768]{2,1,0:T(8,128)S(1)} %get-tuple-element.111.depth_ref, ...), custom_call_target="tpu_custom_call" | custom-call | tf_op jit(solution)/shard_map/squeeze/pallas_call | solution.py:1094
  37.5 0.8 %collective-permute-done.11.sums_other = f32[32,112]{1,0:T(8,128)S(1)} collective-permute-done((f32[32,112]{1,0:T(8,128)S(1)}, f32[32,112]{1,0:T(8,128)S(1)}, u32[]{:S(2)}, u32[]{:S(2)}) %collective-permute-start.11) | collective-permute-done | bytes 14368 | tf_op jit(solution)/shard_map/ppermute | solution.py:1130
  38.4 3.9 %gate_back.1 = (f32[8,192,384]{2,1,0:T(8,128)S(1)}, f32[16,384]{1,0:T(8,128)S(1)}, f32[192,384]{1,0:T(8,128)S(1)}, f32[2,112]{1,0:T(2,128)S(1)}, bf16[192,112]{1,0:T(8,128)(2,1)S(1)}) custom-call(s32[2]{0:T(128)S(1)} %pad_add_fusion.index_ref, f32[8,192,112]{2,1,0:T(8,128)S(1)} %get-tuple-element.116.projected_ref, bf16[8,192,112]{2,1,0:T(8,128)(2,1)S(1)} %cot.1.cot_ref, ...), custom_call_target="tpu_custom_call" | custom-call | tf_op jit(solution)/shard_map/gate_back/pallas_call | solution.py:1094
  42.8 1.1 %collective-permute-done.12.sums_other = f32[16,384]{1,0:T(8,128)S(1)} collective-permute-done((f32[16,384]{1,0:T(8,128)S(1)}, f32[16,384]{1,0:T(8,128)S(1)}, u32[]{:S(2)}, u32[]{:S(2)}) %collective-permute-start.12) | collective-permute-done | bytes 24608 | tf_op jit(solution)/shard_map/ppermute | solution.py:1130
  43.9 5.9 %depth_back.1 = (f32[8,192,384]{2,1,0:T(8,128)S(1)}, f32[48,384]{1,0:T(8,128)S(1)}, f32[2,384]{1,0:T(2,128)S(1)}) custom-call(s32[2]{0:T(128)S(1)} %pad_add_fusion.index_ref, f32[16,384]{1,0:T(8,128)S(1)} %get-tuple-element.124.sums_own, f32[16,384]{1,0:T(8,128)S(1)} %collective-permute-done.12.sums_other, f32[8,192,384]{2,1,0:T(8,128)S(1)} %get-tuple-element.125.two_ref, ...), custom_call_target="tpu_custom_call" | custom-call | tf_op jit(solution)/shard_map/depth_back/pallas_call | solution.py:1094
  50.4 1.1 %collective-permute-done.14._output_ref.output_other = bf16[192,112]{1,0:T(8,128)(2,1)S(1)} collective-permute-done((bf16[192,112]{1,0:T(8,128)(2,1)S(1)}, bf16[192,112]{1,0:T(8,128)(2,1)S(1)}, u32[]{:S(2)}, u32[]{:S(2)}) %collective-permute-start.14) | collective-permute-done | bytes 43040 | tf_op jit(solution)/shard_map/ppermute | solution.py:1130
  51.8 1.4 %expand_back.1 = (f32[112,384]{1,0:T(8,128)S(1)}, f32[192,112]{1,0:T(8,128)S(1)}, f32[2,384]{1,0:T(2,128)S(1)}) custom-call(s32[2]{0:T(128)S(1)} %pad_add_fusion.index_ref, f32[48,384]{1,0:T(8,128)S(1)} %get-tuple-element.127.sums_own, f32[48,384]{1,0:T(8,128)S(1)} %collective-permute-done.13.sums_other, f32[8,192,384]{2,1,0:T(8,128)S(1)} %get-tuple-element.128.one_ref, ...), custom_call_target="tpu_custom_call" | custom-call | tf_op jit(solution)/shard_map/expand_back/pallas_call | solution.py:1094
  53.8 1.0 %collective-permute-done.17.input_other = f32[192,112]{1,0:T(8,128)S(1)} collective-permute-done((f32[192,112]{1,0:T(8,128)S(1)}, f32[192,112]{1,0:T(8,128)S(1)}, u32[]{:S(2)}, u32[]{:S(2)}) %collective-permute-start.17) | collective-permute-done | bytes 86048 | tf_op jit(solution)/shard_map/ppermute | solution.py:1130
  54.8 0.8 %settle.1 = (f32[16,128]{1,0:T(8,128)S(1)}, bf16[112,112]{1,0:T(8,128)(2,1)S(1)}) custom-call(s32[2]{0:T(128)S(1)} %pad_add_fusion.index_ref, f32[112,384]{1,0:T(8,128)S(1)} %get-tuple-element.132.expand_own, f32[112,384]{1,0:T(8,128)S(1)} %collective-permute-done.16.expand_other, f32[192,384]{1,0:T(8,128)S(1)} %get-tuple-element.131.keep_own, ...), custom_call_target="tpu_custom_call" | custom-call | tf_op jit(solution)/shard_map/settle/pallas_call | solution.py:1094
  55.6 1.6 %collective-permute-start.18 = (bf16[112,112]{1,0:T(8,128)(2,1)S(1)}, bf16[112,112]{1,0:T(8,128)(2,1)S(1)}, u32[]{:S(2)}, u32[]{:S(2)}) collective-permute-start(bf16[112,112]{1,0:T(8,128)(2,1)S(1)} %get-tuple-element.144), channel_id=1, source_target_pairs={{0,2},{1,3},{2,0},{3,1},{4,6},{5,7},{6,4},{7,5},{8,10},{9,11},{10,... | collective-permute-start | bytes 75272 | tf_op jit(solution)/shard_map/ppermute | solution.py:1130
  57.2 1.5 %own.1 = (f32[168,112]{1,0:T(8,128)S(1)}, f32[168,112]{1,0:T(8,128)S(1)}, f32[104,168]{1,0:T(8,128)S(1)}, f32[1,32]{1,0:T(1,128)S(1)}, f32[24,16,28]{2,1,0:T(8,128)S(1)}, /*index=5*/bf16[24,16,28]{2,1,0:T(8,128)(2,1)}) custom-call(s32[2]{0:T(128)S(1)} %pad_add_fusion.index_ref, f32[112,384]{1,0:T(8,128)S(1)} %get-tuple-element.132.expand_own, ...), custom_call_target="tpu_custom_call" | custom-call | tf_op jit(solution)/shard_map/own/pallas_call | solution.py:1094
  58.8 0.8 %collective-permute-done.18.packed_other = bf16[112,112]{1,0:T(8,128)(2,1)S(1)} collective-permute-done((bf16[112,112]{1,0:T(8,128)(2,1)S(1)}, bf16[112,112]{1,0:T(8,128)(2,1)S(1)}, u32[]{:S(2)}, u32[]{:S(2)}) %collective-permute-start.18) | collective-permute-done | bytes 25120 | tf_op jit(solution)/shard_map/ppermute | solution.py:1130
  59.8 1.9 %adam.1 = (f32[24,16,28]{2,1,0:T(8,128)}, f32[168,112]{1,0:T(8,128)}, f32[168,112]{1,0:T(8,128)}, f32[168,112]{1,0:T(8,128)}, f32[2,168]{1,0:T(2,128)}, /*index=...) custom-call(s32[2]{0:T(128)S(1)} %pad_add_fusion.index_ref, ...), custom_call_target="tpu_custom_call" | custom-call | tf_op jit(solution)/shard_map/adam/pallas_call | solution.py:1094
  (97 shorter events, 6.7 us)
Async XLA Ops:
  0.7 32.6 %copy-start.30 = (f32[28]{0:T(128)S(1)}, f32[28]{0:T(128)}, u32[]{:S(2)}) copy-start(f32[28]{0:T(128)} %param.49) | copy-start | bytes 340
  2.9 21.8 %all-to-all-start = ((bf16[8,256,128]{2,1,0:T(8,128)(2,1)}), bf16[8,256,128]{2,1,0:T(8,128)(2,1)S(1)}, u32[]{:S(2)}, u32[]{:S(2)}) async-start(bf16[8,256,128]{2,1,0:T(8,128)(2,1)} %copies.1), calls=%async_computation | async-start | bytes 1048576 | tf_op jit(solution)/shard_map/all_to_all | solution.py:1142
  11.2 5.5 %collective-permute-start.1 = (bf16[336,112]{1,0:T(8,128)(2,1)S(1)}, bf16[336,112]{1,0:T(8,128)(2,1)S(1)}, u32[]{:S(2)}, u32[]{:S(2)}) collective-permute-start(bf16[336,112]{1,0:T(8,128)(2,1)S(1)} %get-tuple-element.105.matrix_0), channel_id=1, source_target_pairs={{0,2},{1,3},{2,0},{3,1},{4,6},{5,7},{6,4},{7,5},{8,10},{9,11},{10,... | collective-permute-start | bytes 225800 | tf_op jit(solution)/shard_map/ppermute | solution.py:1130
  12.8 5.1 %collective-permute-start.4 = (f32[104,168]{1,0:T(8,128)S(1)}, f32[104,168]{1,0:T(8,128)S(1)}, u32[]{:S(2)}, u32[]{:S(2)}) collective-permute-start(f32[104,168]{1,0:T(8,128)S(1)} %get-tuple-element.106.stack_0), channel_id=1, source_target_pairs={{0,2},{1,3},{2,0},{3,1},{4,6},{5,7},{6,4},{7,5},{8,10},{9,11},{10,... | collective-permute-start | bytes 209672 | tf_op jit(solution)/shard_map/ppermute | solution.py:1130
  13.3 4.8 %collective-permute-start = (bf16[336,112]{1,0:T(8,128)(2,1)S(1)}, bf16[336,112]{1,0:T(8,128)(2,1)S(1)}, u32[]{:S(2)}, u32[]{:S(2)}) collective-permute-start(bf16[336,112]{1,0:T(8,128)(2,1)S(1)} %get-tuple-element.105.matrix_0), channel_id=1, source_target_pairs={{0,1},{1,0},{2,3},{3,2},{4,5},{5,4},{6,7},{7,6},{8,9},{9,8},{10,11... | collective-permute-start | bytes 225800 | tf_op jit(solution)/shard_map/ppermute | solution.py:1130
  16.7 2.5 %collective-permute-start.2 = (bf16[336,112]{1,0:T(8,128)(2,1)S(1)}, bf16[336,112]{1,0:T(8,128)(2,1)S(1)}, u32[]{:S(2)}, u32[]{:S(2)}) collective-permute-start(bf16[336,112]{1,0:T(8,128)(2,1)S(1)} %collective-permute-done.1.matrix_2), channel_id=1, source_target_pairs={{0,1},{1,0},{2,3},{3,2},{4,5},{5,4},{6,7},{7,6},{8,9},{9,8},{10,11... | collective-permute-start | bytes 225800 | tf_op jit(solution)/shard_map/ppermute | solution.py:1130
  16.7 1.5 %collective-permute-start.3 = (f32[104,168]{1,0:T(8,128)S(1)}, f32[104,168]{1,0:T(8,128)S(1)}, u32[]{:S(2)}, u32[]{:S(2)}) collective-permute-start(f32[104,168]{1,0:T(8,128)S(1)} %get-tuple-element.106.stack_0), channel_id=1, source_target_pairs={{0,1},{1,0},{2,3},{3,2},{4,5},{5,4},{6,7},{7,6},{8,9},{9,8},{10,11... | collective-permute-start | bytes 209672 | tf_op jit(solution)/shard_map/ppermute | solution.py:1130
  17.8 1.3 %collective-permute-start.5 = (f32[104,168]{1,0:T(8,128)S(1)}, f32[104,168]{1,0:T(8,128)S(1)}, u32[]{:S(2)}, u32[]{:S(2)}) collective-permute-start(f32[104,168]{1,0:T(8,128)S(1)} %collective-permute-done.4.stack_2), channel_id=1, source_target_pairs={{0,1},{1,0},{2,3},{3,2},{4,5},{5,4},{6,7},{7,6},{8,9},{9,8},{10,11... | collective-permute-start | bytes 209672 | tf_op jit(solution)/shard_map/ppermute | solution.py:1130
  26.2 2.3 %collective-permute-start.6 = (f32[16,768]{1,0:T(8,128)S(1)}, f32[16,768]{1,0:T(8,128)S(1)}, u32[]{:S(2)}, u32[]{:S(2)}) collective-permute-start(f32[16,768]{1,0:T(8,128)S(1)} %get-tuple-element.109.sums_own), channel_id=1, source_target_pairs={{0,1},{1,0},{2,3},{3,2},{4,5},{5,4},{6,7},{7,6},{8,9},{9,8},{10,11... | collective-permute-start | bytes 147464 | tf_op jit(solution)/shard_map/ppermute | solution.py:1130
  26.3 7.0 %collective-permute-start.9 = (bf16[8,48,112]{2,1,0:T(8,128)(2,1)S(1)}, bf16[8,48,112]{2,1,0:T(8,128)(2,1)S(1)}, u32[]{:S(2)}, u32[]{:S(2)}) collective-permute-start(bf16[8,48,112]{2,1,0:T(8,128)(2,1)S(1)} %get-tuple-element.114.own_ref), channel_id=1, source_target_pairs={{0,2},{1,3},{2,0},{3,1},{4,6},{5,7},{6,4},{7,5},{8,10},{9,11},{10,... | collective-permute-start | bytes 258056 | tf_op jit(solution)/shard_map/ppermute | solution.py:1130
  27.8 5.4 %collective-permute-start.10 = (bf16[8,48,112]{2,1,0:T(8,128)(2,1)S(1)}, bf16[8,48,112]{2,1,0:T(8,128)(2,1)S(1)}, u32[]{:S(2)}, u32[]{:S(2)}) collective-permute-start(bf16[8,48,112]{2,1,0:T(8,128)(2,1)S(1)} %get-tuple-element.115), channel_id=1, source_target_pairs={{0,3},{1,2},{2,1},{3,0},{4,7},{5,6},{6,5},{7,4},{8,11},{9,10},{10,... | collective-permute-start | bytes 258056 | tf_op jit(solution)/shard_map/ppermute | solution.py:1130
  28.1 5.2 %collective-permute-start.8 = (bf16[8,48,112]{2,1,0:T(8,128)(2,1)S(1)}, bf16[8,48,112]{2,1,0:T(8,128)(2,1)S(1)}, u32[]{:S(2)}, u32[]{:S(2)}) collective-permute-start(bf16[8,48,112]{2,1,0:T(8,128)(2,1)S(1)} %get-tuple-element.115), channel_id=1, source_target_pairs={{0,1},{1,0},{2,3},{3,2},{4,5},{5,4},{6,7},{7,6},{8,9},{9,8},{10,11... | collective-permute-start | bytes 258056 | tf_op jit(solution)/shard_map/ppermute | solution.py:1130
  28.5 9.9 %copy-start.21 = (f32[2,112]{1,0:T(2,128)S(1)}, f32[2,112]{1,0:T(2,128)}, u32[]{:S(2)}) copy-start(f32[2,112]{1,0:T(2,128)} %copy-done.20) | copy-start | bytes 2692
  33.0 1.4 %collective-permute-start.7 = (f32[16,768]{1,0:T(8,128)S(1)}, f32[16,768]{1,0:T(8,128)S(1)}, u32[]{:S(2)}, u32[]{:S(2)}) collective-permute-start(f32[16,768]{1,0:T(8,128)S(1)} %get-tuple-element.112.sums_own), channel_id=1, source_target_pairs={{0,1},{1,0},{2,3},{3,2},{4,5},{5,4},{6,7},{7,6},{8,9},{9,8},{10,11... | collective-permute-start | bytes 147464 | tf_op jit(solution)/shard_map/ppermute | solution.py:1130
  37.1 1.3 %collective-permute-start.11 = (f32[32,112]{1,0:T(8,128)S(1)}, f32[32,112]{1,0:T(8,128)S(1)}, u32[]{:S(2)}, u32[]{:S(2)}) collective-permute-start(f32[32,112]{1,0:T(8,128)S(1)} %get-tuple-element.117.sums_own), channel_id=1, source_target_pairs={{0,1},{1,0},{2,3},{3,2},{4,5},{5,4},{6,7},{7,6},{8,9},{9,8},{10,11... | collective-permute-start | bytes 43016 | tf_op jit(solution)/shard_map/ppermute | solution.py:1130
  42.2 9.2 %collective-permute-start.15 = (f32[192,384]{1,0:T(8,128)S(1)}, f32[192,384]{1,0:T(8,128)S(1)}, u32[]{:S(2)}, u32[]{:S(2)}) collective-permute-start(f32[192,384]{1,0:T(8,128)S(1)} %get-tuple-element.131.keep_own), channel_id=1, source_target_pairs={{0,1},{1,0},{2,3},{3,2},{4,5},{5,4},{6,7},{7,6},{8,9},{9,8},{10,11... | collective-permute-start | bytes 884744 | tf_op jit(solution)/shard_map/ppermute | solution.py:1130
  42.6 1.3 %collective-permute-start.12 = (f32[16,384]{1,0:T(8,128)S(1)}, f32[16,384]{1,0:T(8,128)S(1)}, u32[]{:S(2)}, u32[]{:S(2)}) collective-permute-start(f32[16,384]{1,0:T(8,128)S(1)} %get-tuple-element.124.sums_own), channel_id=1, source_target_pairs={{0,1},{1,0},{2,3},{3,2},{4,5},{5,4},{6,7},{7,6},{8,9},{9,8},{10,11... | collective-permute-start | bytes 73736 | tf_op jit(solution)/shard_map/ppermute | solution.py:1130
  49.8 1.6 %collective-permute-start.13 = (f32[48,384]{1,0:T(8,128)S(1)}, f32[48,384]{1,0:T(8,128)S(1)}, u32[]{:S(2)}, u32[]{:S(2)}) collective-permute-start(f32[48,384]{1,0:T(8,128)S(1)} %get-tuple-element.127.sums_own), channel_id=1, source_target_pairs={{0,1},{1,0},{2,3},{3,2},{4,5},{5,4},{6,7},{7,6},{8,9},{9,8},{10,11... | collective-permute-start | bytes 221192 | tf_op jit(solution)/shard_map/ppermute | solution.py:1130
  50.2 1.2 %collective-permute-start.14 = (bf16[192,112]{1,0:T(8,128)(2,1)S(1)}, bf16[192,112]{1,0:T(8,128)(2,1)S(1)}, u32[]{:S(2)}, u32[]{:S(2)}) collective-permute-start(bf16[192,112]{1,0:T(8,128)(2,1)S(1)} %get-tuple-element.130.output_own), channel_id=1, source_target_pairs={{0,1},{1,0},{2,3},{3,2},{4,5},{5,4},{6,7},{7,6},{8,9},{9,8},{10,11... | collective-permute-start | bytes 129032 | tf_op jit(solution)/shard_map/ppermute | solution.py:1130
  51.4 8.1 %copy-start = (bf16[28,6,4,16]{0,3,2,1:T(8,128)(2,1)S(1)}, bf16[28,6,4,16]{0,3,2,1:T(8,128)(2,1)}, u32[]{:S(2)}) copy-start(bf16[28,6,4,16]{0,3,2,1:T(8,128)(2,1)} %param.33) | copy-start | bytes 64516
  51.4 8.1 %copy-start.1 = (f32[168,112]{1,0:T(8,128)S(1)}, f32[168,112]{1,0:T(8,128)}, u32[]{:S(2)}) copy-start(f32[168,112]{1,0:T(8,128)} %refs_0_.1) | copy-start | bytes 225796
  53.2 1.6 %collective-permute-start.16 = (f32[112,384]{1,0:T(8,128)S(1)}, f32[112,384]{1,0:T(8,128)S(1)}, u32[]{:S(2)}, u32[]{:S(2)}) collective-permute-start(f32[112,384]{1,0:T(8,128)S(1)} %get-tuple-element.132.expand_own), channel_id=1, source_target_pairs={{0,1},{1,0},{2,3},{3,2},{4,5},{5,4},{6,7},{7,6},{8,9},{9,8},{10,11... | collective-permute-start | bytes 516104 | tf_op jit(solution)/shard_map/ppermute | solution.py:1130
  53.4 1.4 %collective-permute-start.17 = (f32[192,112]{1,0:T(8,128)S(1)}, f32[192,112]{1,0:T(8,128)S(1)}, u32[]{:S(2)}, u32[]{:S(2)}) collective-permute-start(f32[192,112]{1,0:T(8,128)S(1)} %get-tuple-element.135.input_own), channel_id=1, source_target_pairs={{0,1},{1,0},{2,3},{3,2},{4,5},{5,4},{6,7},{7,6},{8,9},{9,8},{10,11... | collective-permute-start | bytes 258056 | tf_op jit(solution)/shard_map/ppermute | solution.py:1130
  55.6 3.9 %collective-permute-start.18 = (bf16[112,112]{1,0:T(8,128)(2,1)S(1)}, bf16[112,112]{1,0:T(8,128)(2,1)S(1)}, u32[]{:S(2)}, u32[]{:S(2)}) collective-permute-start(bf16[112,112]{1,0:T(8,128)(2,1)S(1)} %get-tuple-element.144), channel_id=1, source_target_pairs={{0,2},{1,3},{2,0},{3,1},{4,6},{5,7},{6,4},{7,5},{8,10},{9,11},{10,... | collective-permute-start | bytes 75272 | tf_op jit(solution)/shard_map/ppermute | solution.py:1130
  (29 other events, 225.7 us)

commit v5 on v4

--- a/solution.py
+++ b/solution.py
@@ -378,6 +378,7 @@
 KEEP_BIASES = 64
 KEEP_PROJECT = 80
 KEEP_ROWS = 192
+LATE_ROWS = 48
 PACKED_ROWS = 96
 BLOCK_ROWS = POSITIONS * 8
 SENT_ROWS = 256
@@ -395,6 +396,14 @@
 
 def dot(left, right, numbers):
     return lax.dot_general(left, right, numbers, preferred_element_type=f32)
+
+
+def split_dot(left, right, numbers):
+    left_high, right_high = left.astype(bf16), right.astype(bf16)
+    left_low = (left - left_high.astype(f32)).astype(bf16)
+    right_low = (right - right_high.astype(f32)).astype(bf16)
+    mixed = dot(left_high, right_low, numbers) + dot(left_low, right_high, numbers)
+    return dot(left_high, right_high, numbers) + mixed
 
 
 def rows_sum(values):
@@ -604,7 +613,7 @@
         stack_ref[ROW_DEPTH_GAINS + 1 : ROW_DEPTH_GAINS + 2, :], norm_ref,
     )
 
-    def pool_block(block, carry):
+    def pool_block(block):
         for tile in range(width // 128):
             lanes = lane_tile(tile)
             gain_half = norm_ref[0:8, lanes]
@@ -616,16 +625,16 @@
                 )
                 active_ref[block, 8 * at : 8 * at + 8, lanes] = value
                 total = total + value
-            pooled_ref[pl.ds(pl.multiple_of(block * 8, 8), 8), lanes] = total / POSITIONS
-        return carry
-
-    lax.fori_loop(0, blocks, pool_block, 0)
+            pooled_ref[slice(8 * block, 8 * block + 8), lanes] = total / POSITIONS
+
+    for block in range(blocks):
+        pool_block(block)
     squeeze = stack_ref[ROW_SQUEEZE : ROW_SQUEEZE + HIDDEN_ROWS, :]
     excite = stack_ref[ROW_EXCITE : ROW_EXCITE + HIDDEN_ROWS, :]
-    before = highest(pooled_ref[...], squeeze, contract_lanes) + bias_ref[...]
+    before = split_dot(pooled_ref[...], squeeze, contract_lanes) + bias_ref[...]
     before_ref[...] = before
     hidden = swish_of_half(0.5 * before)
-    raised = highest(hidden, excite, contract_plain)
+    raised = split_dot(hidden, excite, contract_plain)
     raised = raised + stack_ref[ROW_EXCITE_BIAS : ROW_EXCITE_BIAS + 1, :]
     gate_ref[...] = 0.5 + 0.5 * jnp.tanh(0.5 * raised)
     totals = [jnp.zeros((8, C_IN), f32)] * 4
@@ -648,7 +657,7 @@
 def gate_back_kernel(
     total_rows, index_ref, projected_ref, cot_ref, sums_own, sums_other, gains_ref, depth_ref,
     norm_ref, stack_ref, wp_ref, gate_ref, before_ref, pooled_ref, scaled_ref, active_ref, x_ref,
-    two_ref, sums_ref, lanes_ref, gains_grad_ref, output_ref,
+    two_ref, sums_ref, lanes_ref, gains_grad_ref,
     delta_scr, grad_scr, gate_grad_scr, pooled_scr,
 ):
     blocks = depth_ref.shape[0]
@@ -665,9 +674,9 @@
     gain = gains_ref[0:1, :]
     shift = gains_ref[1:2, :]
     mine = index_ref[0]
-    output_ref[...] = (
-        x_ref[mine, 0:BLOCK_ROWS, 0:C_IN].astype(f32) + (projected_ref[mine] - average) * spread * gain + shift
-    ).astype(output_ref.dtype)
+    output = x_ref[mine, 0:BLOCK_ROWS, 0:C_IN].astype(f32)
+    output = output + ((projected_ref[mine] - average) * spread * gain + shift)
+    lanes_ref[:, PAIR_LANES : PAIR_LANES + C_IN] = output
     outer = gain * spread
 
     for block in range(blocks):
@@ -687,19 +696,19 @@
     gate_grad_scr[...] = gate_grad_scr[...] * gate * (1.0 - gate)
     half = 0.5 * before_ref[...]
     hidden = swish_of_half(half)
-    squeeze_delta = highest(gate_grad_scr[...], excite, contract_lanes) * slope_of_half(half)
+    squeeze_delta = split_dot(gate_grad_scr[...], excite, contract_lanes) * slope_of_half(half)
     own_delta = gate_grad_scr[:, own_lanes]
-    lanes_ref[0:HIDDEN_ROWS, :] = highest(squeeze_delta, pooled_ref[:, own_lanes], contract_rows)
-    lanes_ref[HIDDEN_ROWS : 2 * HIDDEN_ROWS, :] = highest(hidden, own_delta, contract_rows)
-    lanes_ref[KEEP_BIASES : KEEP_BIASES + 8, :] = rows_sum(own_delta)
-    lanes_ref[KEEP_BIASES + 8 : KEEP_BIASES + 16, :] = jnp.zeros((8, PAIR_LANES), f32)
+    lanes_ref[0:HIDDEN_ROWS, 0:PAIR_LANES] = split_dot(squeeze_delta, pooled_ref[:, own_lanes], contract_rows)
+    lanes_ref[HIDDEN_ROWS : 2 * HIDDEN_ROWS, 0:PAIR_LANES] = split_dot(hidden, own_delta, contract_rows)
+    lanes_ref[KEEP_BIASES : KEEP_BIASES + 8, 0:PAIR_LANES] = rows_sum(own_delta)
+    lanes_ref[KEEP_BIASES + 8 : KEEP_BIASES + 16, 0:PAIR_LANES] = jnp.zeros((8, PAIR_LANES), f32)
     lanes_ref[KEEP_BIASES + 8 : KEEP_BIASES + 16, 0:HIDDEN_ROWS] = rows_sum(squeeze_delta)
     squeeze = stack_ref[ROW_SQUEEZE : ROW_SQUEEZE + HIDDEN_ROWS, own_lanes]
-    pooled_scr[...] = highest(squeeze_delta, squeeze, contract_plain) / POSITIONS
+    pooled_scr[...] = split_dot(squeeze_delta, squeeze, contract_plain) / POSITIONS
     sums_ref[...] = jnp.zeros_like(sums_ref)
 
-    def two_block(block, carry):
-        rows = pl.ds(pl.multiple_of(block * 8, 8), 8)
+    def two_block(block):
+        rows = slice(8 * block, 8 * block + 8)
         for tile in range(PAIR_LANES // 128):
             lanes = lane_tile(tile)
             whole = lane_tile(tile, own)
@@ -721,11 +730,11 @@
                 product = product + value * (depth - average)
             sums_ref[0:8, lanes] += total
             sums_ref[8:16, lanes] += product
-        return carry
-
-    lax.fori_loop(0, blocks, two_block, 0)
+
+    for block in range(blocks):
+        two_block(block)
     rows = blocks * POSITIONS * 8
-    lanes_ref[KEEP_PROJECT : KEEP_PROJECT + C_IN, :] = dot(
+    lanes_ref[KEEP_PROJECT : KEEP_PROJECT + C_IN, 0:PAIR_LANES] = dot(
         delta_scr[...].reshape(rows, C_IN), scaled_ref[:, :, own_lanes].reshape(rows, PAIR_LANES), contract_rows
     )
 
@@ -748,9 +757,9 @@
     slope = outer * spread * gamma / total_rows
     factors_scr[0:8, :] = outer
     factors_scr[8:16, :] = slope
-    factors_scr[16:24, :] = outer * (beta / total_rows)
+    factors_scr[16:24, :] = outer * (beta / total_rows) - slope * average
     product_filters(
-        lambda i, j: stack_ref[TAPS - 1 - i * KS - j : TAPS - i * KS - j, own_lanes], taps_scr
+        lambda i, j: 0.5 * stack_ref[TAPS - 1 - i * KS - j : TAPS - i * KS - j, own_lanes], taps_scr
     )
     sums_ref[...] = jnp.zeros_like(sums_ref)
     kernel_scr[...] = jnp.zeros_like(kernel_scr)
@@ -762,20 +771,22 @@
             gain_half = norm_one_ref[0:8, whole]
             shift_half = norm_one_ref[8:16, whole]
             average_one = norm_one_ref[16:24, whole]
-            average_two = norm_two_ref[16:24, whole]
             outer = factors_scr[0:8, lanes]
             slope = factors_scr[8:16, lanes]
             level = factors_scr[16:24, lanes]
             grads = []
             active = []
+            bents = []
             for at in range(POSITIONS):
                 spot = slice(8 * at, 8 * at + 8)
                 grads.append(
                     outer * two_ref[block, spot, lanes]
                     - level
-                    - slope * (depth_ref[block, spot, whole] - average_two)
+                    - slope * depth_ref[block, spot, whole]
                 )
-                active.append(swish_of_half(expanded_ref[block, spot, whole] * gain_half + shift_half))
+                half = expanded_ref[block, spot, whole] * gain_half + shift_half
+                bents.append(jnp.tanh(half))
+                active.append(half * bents[at] + half)
             sources = product_inputs(active)
             inputs = product_inputs(grads)
             targets = product_targets(inputs)
@@ -795,7 +806,7 @@
                     at = row * WD + col
                     spot = slice(8 * at, 8 * at + 8)
                     expanded = expanded_ref[block, spot, whole]
-                    value = value * slope_of_half(expanded * gain_half + shift_half)
+                    value = value * ((1.0 + bents[at]) + active[at] * (1.0 - bents[at]))
                     one_ref[block, spot, lanes] = value
                     total = total + value
                     product = product + value * (expanded - average_one)
@@ -818,8 +829,8 @@
 
 def expand_back_kernel(
     total_rows, index_ref, sums_own, sums_other, one_ref, expanded_ref, x_ref, we_ref, stack_ref, norm_ref,
-    _output_ref, _lanes_ref,
-    expand_ref, input_ref, gains_grad_ref, delta_scr,
+    _lanes_ref,
+    late_ref, gains_grad_ref, delta_scr,
 ):
     blocks = x_ref.shape[0]
     own = pl.multiple_of(index_ref[1] // 2 * PAIR_LANES, 128)
@@ -840,10 +851,14 @@
         delta = outer * one_ref[block] - level - slope * centred
         delta_scr[block] = delta.astype(bf16)
     rows = blocks * POSITIONS * 8
-    expand_ref[...] = dot(
+    late_ref[0:C_IN, 0:PAIR_LANES] = dot(
         x_ref[:, 0:BLOCK_ROWS, 0:C_IN].reshape(rows, C_IN), delta_scr[...].reshape(rows, PAIR_LANES), contract_rows
     )
-    input_ref[...] = dot(delta_scr[index_ref[0]], own_weights, contract_plain)
+    part = dot(delta_scr[index_ref[0]], own_weights, contract_plain)
+    for group in range(4):
+        late_ref[C_IN : C_IN + LATE_ROWS, group * 128 : group * 128 + C_IN] = part[
+            group * LATE_ROWS : (group + 1) * LATE_ROWS
+        ]
 
 
 def one_hot(rows, columns, matches):
@@ -943,13 +958,27 @@
 
 def kept_sums(keep_own, keep_other, sums_own, sums_other):
     def both(start, stop):
-        return keep_own[start:stop, :] + keep_other[start:stop, :]
+        return keep_own[start:stop, 0:PAIR_LANES] + keep_other[start:stop, 0:PAIR_LANES]
 
     return (
         both(KEEP_PROJECT, KEEP_PROJECT + C_IN), both(0, 2 * HIDDEN_ROWS),
         sums_own[16 : 16 + TAPS, :] + sums_other[16 : 16 + TAPS, :],
         both(KEEP_BIASES, KEEP_BIASES + 1), both(KEEP_BIASES + 8, KEEP_BIASES + 9)[:, 0:HIDDEN_ROWS],
     )
+
+
+def input_rows(late_ref):
+    return jnp.concatenate(
+        [
+            late_ref[C_IN : C_IN + LATE_ROWS, group * 128 : group * 128 + C_IN]
+            for group in range(4)
+        ],
+        axis=0,
+    )
+
+
+def expand_sum(late_own, late_other):
+    return late_own[0:C_IN, 0:PAIR_LANES] + late_other[0:C_IN, 0:PAIR_LANES]
 
 
 def both_halves(first, own, other):
@@ -961,8 +990,8 @@
 
 
 def settle_kernel(
-    index_ref, expand_own, expand_other, keep_own, keep_other, sums_own, sums_other, three_ref, two_ref, one_ref,
-    input_own, input_other, square_ref, packed_ref,
+    index_ref, late_own, late_other, keep_own, keep_other, sums_own, sums_other, three_ref, two_ref, one_ref,
+    square_ref, packed_ref,
 ):
     position = index_ref[1]
     narrow = C_IN // 4
@@ -971,12 +1000,12 @@
         return jnp.sum(jnp.sum(values * values, axis=0, keepdims=True), axis=1, keepdims=True)
 
     project, hidden, kernel, excite_bias, bias = kept_sums(keep_own, keep_other, sums_own, sums_other)
-    total = squared(expand_own[...] + expand_other[...]) + squared(project) + squared(hidden)
+    total = squared(expand_sum(late_own, late_other)) + squared(project) + squared(hidden)
     total = total + squared(kernel) + squared(excite_bias)
     total = total + squared(one_ref[...]) + squared(two_ref[...])
     square_ref[0:8, :] = jnp.broadcast_to(total, (8, 128))
     square_ref[8:16, :] = jnp.broadcast_to(squared(bias) + squared(three_ref[...]), (8, 128))
-    whole = both_halves(position % 2 == 0, input_own[...], input_other[...])
+    whole = both_halves(position % 2 == 0, input_rows(late_own), input_rows(late_other))
     whole = whole.reshape(4 * PACKED_ROWS, C_IN).astype(bf16)
     across = position + 2 - position // 2 * 4
     packed = None
@@ -1001,10 +1030,14 @@
 
 
 def own_kernel(
-    index_ref, expand_own, expand_other, keep_own, keep_other, sums_own, sums_other, two_ref, one_ref,
-    input_own, input_other, output_own, output_other,
-    expand_ref, project_ref, lanes_ref, bias_ref, input_ref, output_ref,
+    index_ref, late_own, late_other, keep_own, keep_other, sums_own, sums_other, two_ref, one_ref, *refs
 ):
+    params, outs = refs[:30], refs[36:]
+    expand_ref, project_ref, lanes_ref, bias_ref, input_ref, output_ref = refs[30:36]
+    for entry in range(10):
+        shrink = 1.0 - step_rates[entry] * decay_flags[entry] * decay_rate
+        for part, scale in enumerate((shrink, beta_first, beta_second)):
+            outs[3 * entry + part][...] = scale * params[3 * entry + part][...]
     position = index_ref[1]
     first = position % 2 == 0
     channels = expand_ref.shape[0]
@@ -1015,7 +1048,7 @@
 
     project, hidden, kernel, excite_bias, bias = kept_sums(keep_own, keep_other, sums_own, sums_other)
     bias_ref[...] = bias
-    expand_ref[...] = jnp.transpose(mine(expand_own[...] + expand_other[...]))
+    expand_ref[...] = jnp.transpose(mine(expand_sum(late_own, late_other)))
     project_ref[...] = jnp.transpose(mine(project))
     lanes_ref[0:TAPS, :] = mine(kernel)
     lanes_ref[ROW_SQUEEZE : ROW_SQUEEZE + 2 * HIDDEN_ROWS, :] = mine(hidden)
@@ -1024,10 +1057,13 @@
     lanes_ref[ROW_DEPTH_GAINS : ROW_DEPTH_GAINS + 2, :] = mine(two_ref[...])
     pick = one_hot(C_IN, narrow, lambda r, c: r == c + position * narrow)
     halves = [
-        highest(ref[...], pick.astype(f32), contract_plain) for ref in (input_own, input_other)
+        highest(input_rows(ref), pick.astype(f32), contract_plain) for ref in (late_own, late_other)
     ]
     input_ref[...] = both_halves(first, *halves)
-    halves = [dot(ref[...], pick.astype(bf16), contract_plain) for ref in (output_own, output_other)]
+    halves = [
+        dot(ref[:, PAIR_LANES : PAIR_LANES + C_IN].astype(bf16), pick.astype(bf16), contract_plain)
+        for ref in (keep_own, keep_other)
+    ]
     output_ref[...] = both_halves(first, *halves).astype(bf16)
 
 
@@ -1063,32 +1099,32 @@
         highest(three_grad[0:2, :], pick, contract_plain),
     )
     for entry in range(10):
-        updated = adam_step(
-            params[3 * entry][...],
-            params[3 * entry + 1][...],
-            params[3 * entry + 2][...],
-            gradients[entry] * factor,
-            step_rates[entry],
-            decay_flags[entry],
-        )
+        gradient = gradients[entry] * factor
+        first_new = params[3 * entry + 1][...] + (1.0 - beta_first) * gradient
+        second_new = params[3 * entry + 2][...] + (1.0 - beta_second) * gradient * gradient
+        first_hat = first_new / (1.0 - beta_first**STEP)
+        second_hat = second_new / (1.0 - beta_second**STEP)
+        step = first_hat / (jnp.sqrt(second_hat) + adam_epsilon)
+        updated = (params[3 * entry][...] - step_rates[entry] * step, first_new, second_new)
         for part in range(3):
             outs[1 + 3 * entry + part][...] = updated[part]
 
 
-def call(kernel, outs, operands, scratch=(), name=None, keep=True, place=True, after=()):
+def call(kernel, outs, operands, scratch=(), name=None, keep=True, place=True, after=(), plain=()):
     spaces = [
         pl.BlockSpec(memory_space=pltpu.SMEM)
         if operand.dtype == jnp.int32
         else pl.BlockSpec(memory_space=pltpu.VMEM)
         for operand in operands
     ]
+    spaces += [pl.BlockSpec(memory_space=pltpu.VMEM)] * len(plain)
     spaces += [pl.BlockSpec(memory_space=pl.ANY)] * len(after)
     operands = [
         operand
         if operand.dtype == jnp.int32
         else pltpu.with_memory_space_constraint(operand, pltpu.VMEM if place else pltpu.HBM)
         for operand in operands
-    ] + [pltpu.with_memory_space_constraint(operand, pltpu.HBM) for operand in after]
+    ] + [pltpu.with_memory_space_constraint(operand, pltpu.HBM) for operand in (*plain, *after)]
     limit = 4 * 1024 * 1024 + sum(4 * math.prod(shape) for shape, _ in scratch)
     made = pltpu.VMEM if keep else jax.ShapeDtypeStruct
     return pl.pallas_call(
@@ -1206,14 +1242,13 @@
         [depth, sums, swap(sums, 1), stack_all, project_all, cot, bias_row],
         name="squeeze",
     )
-    two, sums, lanes_grad, three_grad, output = call(
+    two, sums, lanes_grad, three_grad = call(
         functools.partial(gate_back_kernel, total_rows),
         [
             ((shards, rows, PAIR_LANES), f32),
             ((16, PAIR_LANES), f32),
-            ((KEEP_ROWS, PAIR_LANES), f32),
+            ((KEEP_ROWS, PAIR_LANES + 128), f32),
             ((2, C_IN), f32),
-            ((rows, C_IN), bf16),
         ],
         [
             index, projected, cot, sums, swap(sums, 1), gains_all, depth, norm_two, stack_all,
@@ -1227,7 +1262,6 @@
         ],
         name="gate_back",
     )
-    output_other = swap(output, 1)
     lanes_other = swap(lanes_grad, 1)
     one, sums, two_grad = call(
         functools.partial(depth_back_kernel, total_rows),
@@ -1247,26 +1281,25 @@
         name="depth_back",
     )
     sums_other = swap(sums, 1)
-    expand_grad, input_part, one_grad = call(
+    late, one_grad = call(
         functools.partial(expand_back_kernel, total_rows),
-        [((C_IN, PAIR_LANES), f32), ((rows, C_IN), f32), ((2, PAIR_LANES), f32)],
+        [((C_IN + LATE_ROWS, 512), f32), ((2, PAIR_LANES), f32)],
         [
             index, sums, sums_other, one, expanded, x, expand_all, stack_all, norm_one,
-            output_other, lanes_other,
+            lanes_other,
         ],
         [((shards, rows, PAIR_LANES), bf16)],
         name="expand_back",
     )
-    expand_pair = [expand_grad, swap(expand_grad, 1)]
+    late_pair = [late, swap(late, 1)]
     keep_pair = [lanes_grad, lanes_other, sums, sums_other]
-    input_pair = [input_part, swap(input_part, 1)]
     square, packed = call(
         settle_kernel,
         [((16, 128), f32), ((PACKED_ROWS + 16, C_IN), bf16)],
-        [index, *expand_pair, *keep_pair, three_grad, two_grad, one_grad, *input_pair],
+        [index, *late_pair, *keep_pair, three_grad, two_grad, one_grad],
         name="settle",
     )
-    expand_own, project_own, lanes_own, bias_own, input_own, block_output = call(
+    expand_own, project_own, lanes_own, bias_own, input_own, block_output, *scaled_params = call(
         own_kernel,
         [
             ((channels, C_IN), f32),
@@ -1275,9 +1308,11 @@
             ((1, HIDDEN_ROWS), f32),
             ((POSITIONS, segments, narrow), f32),
             ((POSITIONS, segments, narrow), bf16, False),
+            *[(value.shape, f32) for value in params],
         ],
-        [index, *expand_pair, *keep_pair, two_grad, one_grad, *input_pair, output, output_other],
+        [index, *late_pair, *keep_pair, two_grad, one_grad],
         name="own",
+        plain=params,
     )
     updated = call(
         adam_kernel,
@@ -1286,7 +1321,7 @@
         + [((1, 1), f32)],
         [
             index, square, expand_own, project_own, lanes_own, bias_own, three_grad,
-            input_own, swap(packed, 2), cot_rows, *params,
+            input_own, swap(packed, 2), cot_rows, *scaled_params,
         ],
         name="adam",
         keep=False,

time: 62 us -> 60.1 us (0.969)
    ppermute x19 -> x17, waiting for transfers between devices: 10.2 us -> 9.63 us  [swap(): return lax.ppermute(values, 'chan', [(at, at ^ mask) for at in range(4)])]
    ppermute x19 -> x17, starting transfers between devices: 8.89 us -> 8.53 us  [swap(): return lax.ppermute(values, 'chan', [(at, at ^ mask) for at in range(4)])]
  transfers between devices with their start and end apart: 20 -> 18, of which waited for: 10 -> 9; matrix products, arithmetic and copies ran while one was open for 0% -> 0% of each run, Pallas kernels for 24% -> 25%
where the time goes in v5:
time: 60.1 us; the launch traced here: 59.8 us
  Pallas kernels  28.6 us (48%)
  starting transfers between devices  15.8 us (26%)
  waiting for transfers between devices  13.9 us (23%)
  between operations  0.84 us (1%)
    pallas_call x13, Pallas kernels, call(): pl.pallas_call(kernel, out_shape=[(jax.ShapeDtypeStruct if out[2:] else m...  28.6 us
    ppermute x17, waiting for transfers between devices, swap(): return lax.ppermute(values, 'chan', [(at, at ^ mask) for at in range(4)])  9.63 us
    ppermute x17, starting transfers between devices, swap(): return lax.ppermute(values, 'chan', [(at, at ^ mask) for at in range(4)])  8.53 us
    all_to_all x1, starting transfers between devices, on_device_paired(): x = lax.all_to_all(copies, 'dp', 0, 0)  7.28 us
    all_to_all x1, waiting for transfers between devices, on_device_paired(): x = lax.all_to_all(copies, 'dp', 0, 0)  4.24 us
  transfers between devices with their start and end apart: 18, of which 9 were waited for; matrix products, arithmetic and copies ran while one was open for 0% of the time, Pallas kernels for 25%

profile of v5, /device:TPU:0, one launch (start us, length us, event | category | flops | bytes accessed | tf_op | source)
XLA Modules:
  0.0 59.8 jit_solution(10973855579003273827)
XLA Ops:
  0.8 2.1 %copies.1 = bf16[8,256,128]{2,1,0:T(8,128)(2,1)} custom-call(s32[2]{0:T(128)S(1)} %pad_add_fusion.index_ref, bf16[24,16,112]{2,1,0:T(8,128)(2,1)} %bitcast.37, bf16[24,16,28]{2,1,0:T(8,128)(2,1)} %bitcast.33), custom_call_target="tpu_custom_call" | custom-call | tf_op jit(solution)/shard_map/copies/pallas_call | solution.py:1130
  2.9 7.3 %all-to-all-start = ((bf16[8,256,128]{2,1,0:T(8,128)(2,1)}), bf16[8,256,128]{2,1,0:T(8,128)(2,1)S(1)}, u32[]{:S(2)}, u32[]{:S(2)}) async-start(bf16[8,256,128]{2,1,0:T(8,128)(2,1)} %copies.1), calls=%async_computation | async-start | bytes 1048576 | tf_op jit(solution)/shard_map/all_to_all | solution.py:1178
  10.2 1.0 %pack.1 = (f32[104,168]{1,0:T(8,128)S(1)}, bf16[336,112]{1,0:T(8,128)(2,1)S(1)}) custom-call(f32[168,112]{1,0:T(8,128)} %refs_0_.1, f32[168,112]{1,0:T(8,128)} %bitcast.35, f32[25,168]{1,0:T(8,128)} %refs_6_.1, f32[28,168]{1,0:T(8,128)} %refs_12_.1, f32[28,168]{1,0:T(8,128)} %refs_18_.1, f32[1,168]{1,0:T(1,128)} %bitcast.40, f32[2,168]{1,0:T(2,128)} %refs_3_.1, ...), custom_call_target="tpu_custom_call" | custom-call | tf_op jit(solution)/shard_map/pack/pallas_call | solution.py:1130
  11.2 1.6 %collective-permute-start.1 = (bf16[336,112]{1,0:T(8,128)(2,1)S(1)}, bf16[336,112]{1,0:T(8,128)(2,1)S(1)}, u32[]{:S(2)}, u32[]{:S(2)}) collective-permute-start(bf16[336,112]{1,0:T(8,128)(2,1)S(1)} %get-tuple-element.133.matrix_0), channel_id=1, source_target_pairs={{0,2},{1,3},{2,0},{3,1},{4,6},{5,7},{6,4},{7,5},{8,10},{9,11},{10,... | collective-permute-start | bytes 225800 | tf_op jit(solution)/shard_map/ppermute | solution.py:1166
  13.3 3.4 %collective-permute-done.1.matrix_2 = bf16[336,112]{1,0:T(8,128)(2,1)S(1)} collective-permute-done((bf16[336,112]{1,0:T(8,128)(2,1)S(1)}, bf16[336,112]{1,0:T(8,128)(2,1)S(1)}, u32[]{:S(2)}, u32[]{:S(2)}) %collective-permute-start.1) | collective-permute-done | bytes 75296 | tf_op jit(solution)/shard_map/ppermute | solution.py:1166
  18.1 1.0 %collective-permute-done.5.stack_3 = f32[104,168]{1,0:T(8,128)S(1)} collective-permute-done((f32[104,168]{1,0:T(8,128)S(1)}, f32[104,168]{1,0:T(8,128)S(1)}, u32[]{:S(2)}, u32[]{:S(2)}) %collective-permute-start.5) | collective-permute-done | bytes 69920 | tf_op jit(solution)/shard_map/ppermute | solution.py:1166
  19.1 0.7 %assemble.1 = (f32[104,768]{1,0:T(8,128)S(1)}, bf16[768,112]{1,0:T(8,128)(2,1)S(1)}, f32[2,112]{1,0:T(2,128)S(1)}) custom-call(s32[2]{0:T(128)S(1)} %pad_add_fusion.index_ref, f32[104,168]{1,0:T(8,128)S(1)} %get-tuple-element.134.stack_0, f32[104,168]{1,0:T(8,128)S(1)} %collective-permute-done.3.stack_1, f32[104,168]{1,0:T(8,128)S(1)} %collective-permute-done.4.stack_2, ...), custom_call_target="tpu_custom_call" | custom-call | tf_op jit(solution)/shard_map/assemble/pallas_call | solution.py:1130
  20.4 4.2 %all-to-all-done.x_ref = bf16[8,256,128]{2,1,0:T(8,128)(2,1)S(1)} async-done(((bf16[8,256,128]{2,1,0:T(8,128)(2,1)}), bf16[8,256,128]{2,1,0:T(8,128)(2,1)S(1)}, u32[]{:S(2)}, u32[]{:S(2)}) %all-to-all-start) | async-done | bytes 524320 | tf_op jit(solution)/shard_map/all_to_all | solution.py:1178
  24.7 1.5 %first.1 = (f32[8,192,768]{2,1,0:T(8,128)S(1)}, f32[16,768]{1,0:T(8,128)S(1)}, bf16[768,112]{1,0:T(8,128)(2,1)S(1)}, bf16[8,48,112]{2,1,0:T(8,128)(2,1)S(1)}, bf16[8,48,112]{2,1,0:T(8,128)(2,1)S(1)}) custom-call(s32[2]{0:T(128)S(1)} %pad_add_fusion.index_ref, bf16[336,112]{1,0:T(8,128)(2,1)S(1)} %get-tuple-element.133.matrix_0, ...), custom_call_target="tpu_custom_call" | custom-call | tf_op jit(solution)/shard_map/first/pallas_call | solution.py:1130
  26.2 1.6 %collective-permute-start.9 = (bf16[8,48,112]{2,1,0:T(8,128)(2,1)S(1)}, bf16[8,48,112]{2,1,0:T(8,128)(2,1)S(1)}, u32[]{:S(2)}, u32[]{:S(2)}) collective-permute-start(bf16[8,48,112]{2,1,0:T(8,128)(2,1)S(1)} %get-tuple-element.142.own_ref), channel_id=1, source_target_pairs={{0,2},{1,3},{2,0},{3,1},{4,6},{5,7},{6,4},{7,5},{8,10},{9,11},{10,... | collective-permute-start | bytes 258056 | tf_op jit(solution)/shard_map/ppermute | solution.py:1166
  28.4 4.5 %expand.1 = (f32[8,192,768]{2,1,0:T(8,128)S(1)}, f32[16,768]{1,0:T(8,128)S(1)}, f32[32,768]{1,0:T(8,128)S(1)}) custom-call(f32[8,192,768]{2,1,0:T(8,128)S(1)} %get-tuple-element.136.expanded_ref, f32[16,768]{1,0:T(8,128)S(1)} %get-tuple-element.137.sums_own, f32[16,768]{1,0:T(8,128)S(1)} %collective-permute-done.6.sums_other, ...), custom_call_target="tpu_custom_call" | custom-call | tf_op jit(solution)/shard_map/expand/pallas_call | solution.py:1130
  33.3 1.1 %cot.1.cot_ref = bf16[8,192,112]{2,1,0:T(8,128)(2,1)S(1)} custom-call(s32[2]{0:T(128)S(1)} %pad_add_fusion.index_ref, bf16[8,48,112]{2,1,0:T(8,128)(2,1)S(1)} %get-tuple-element.142.own_ref, bf16[8,48,112]{2,1,0:T(8,128)(2,1)S(1)} %collective-permute-done.8.near_ref, bf16[8,48,112]{2,1,0:T(8,128)(2,1)S(1)} %collective-permute-done.9.far_ref, ...), custom_call_target="tpu_custom_call" | custom-call | tf_op jit(solution)/shard_map/cot/pallas_call | solution.py:1130
  34.4 2.4 %squeeze.29 = (f32[8,192,112]{2,1,0:T(8,128)S(1)}, bf16[8,192,768]{2,1,0:T(8,128)(2,1)S(1)}, f32[32,112]{1,0:T(8,128)S(1)}, f32[64,768]{1,0:T(8,128)S(1)}, f32[6...) custom-call(f32[8,192,768]{2,1,0:T(8,128)S(1)} %get-tuple-element.139.depth_ref, ...), custom_call_target="tpu_custom_call" | custom-call | tf_op jit(solution)/shard_map/squeeze/pallas_call | solution.py:1130
  37.2 0.8 %collective-permute-done.11.sums_other = f32[32,112]{1,0:T(8,128)S(1)} collective-permute-done((f32[32,112]{1,0:T(8,128)S(1)}, f32[32,112]{1,0:T(8,128)S(1)}, u32[]{:S(2)}, u32[]{:S(2)}) %collective-permute-start.11) | collective-permute-done | bytes 14368 | tf_op jit(solution)/shard_map/ppermute | solution.py:1166
  38.1 3.3 %gate_back.1 = (f32[8,192,384]{2,1,0:T(8,128)S(1)}, f32[16,384]{1,0:T(8,128)S(1)}, f32[192,512]{1,0:T(8,128)S(1)}, f32[2,112]{1,0:T(2,128)S(1)}) custom-call(s32[2]{0:T(128)S(1)} %pad_add_fusion.index_ref, f32[8,192,112]{2,1,0:T(8,128)S(1)} %get-tuple-element.144.projected_ref, bf16[8,192,112]{2,1,0:T(8,128)(2,1)S(1)} %cot.1.cot_ref, ...), custom_call_target="tpu_custom_call" | custom-call | tf_op jit(solution)/shard_map/gate_back/pallas_call | solution.py:1130
  41.9 1.2 %collective-permute-done.12.sums_other = f32[16,384]{1,0:T(8,128)S(1)} collective-permute-done((f32[16,384]{1,0:T(8,128)S(1)}, f32[16,384]{1,0:T(8,128)S(1)}, u32[]{:S(2)}, u32[]{:S(2)}) %collective-permute-start.12) | collective-permute-done | bytes 24608 | tf_op jit(solution)/shard_map/ppermute | solution.py:1166
  43.2 5.5 %depth_back.1 = (f32[8,192,384]{2,1,0:T(8,128)S(1)}, f32[48,384]{1,0:T(8,128)S(1)}, f32[2,384]{1,0:T(2,128)S(1)}) custom-call(s32[2]{0:T(128)S(1)} %pad_add_fusion.index_ref, f32[16,384]{1,0:T(8,128)S(1)} %get-tuple-element.152.sums_own, f32[16,384]{1,0:T(8,128)S(1)} %collective-permute-done.12.sums_other, f32[8,192,384]{2,1,0:T(8,128)S(1)} %get-tuple-element.153.two_ref, ...), custom_call_target="tpu_custom_call" | custom-call | tf_op jit(solution)/shard_map/depth_back/pallas_call | solution.py:1130
  49.1 0.9 %collective-permute-done.13.sums_other = f32[48,384]{1,0:T(8,128)S(1)} collective-permute-done((f32[48,384]{1,0:T(8,128)S(1)}, f32[48,384]{1,0:T(8,128)S(1)}, u32[]{:S(2)}, u32[]{:S(2)}) %collective-permute-start.13) | collective-permute-done | bytes 73760 | tf_op jit(solution)/shard_map/ppermute | solution.py:1166
  50.0 1.4 %expand_back.1 = (f32[160,512]{1,0:T(8,128)S(1)}, f32[2,384]{1,0:T(2,128)S(1)}) custom-call(s32[2]{0:T(128)S(1)} %pad_add_fusion.index_ref, f32[48,384]{1,0:T(8,128)S(1)} %get-tuple-element.155.sums_own, f32[48,384]{1,0:T(8,128)S(1)} %collective-permute-done.13.sums_other, f32[8,192,384]{2,1,0:T(8,128)S(1)} %get-tuple-element.156.one_ref, ...), custom_call_target="tpu_custom_call" | custom-call | tf_op jit(solution)/shard_map/expand_back/pallas_call | solution.py:1130
  51.8 1.3 %collective-permute-done.15.late_other = f32[160,512]{1,0:T(8,128)S(1)} collective-permute-done((f32[160,512]{1,0:T(8,128)S(1)}, f32[160,512]{1,0:T(8,128)S(1)}, u32[]{:S(2)}, u32[]{:S(2)}) %collective-permute-start.15) | collective-permute-done | bytes 327712 | tf_op jit(solution)/shard_map/ppermute | solution.py:1166
  53.1 0.8 %settle.1 = (f32[16,128]{1,0:T(8,128)S(1)}, bf16[112,112]{1,0:T(8,128)(2,1)S(1)}) custom-call(s32[2]{0:T(128)S(1)} %pad_add_fusion.index_ref, f32[160,512]{1,0:T(8,128)S(1)} %get-tuple-element.159.late_own, f32[160,512]{1,0:T(8,128)S(1)} %collective-permute-done.15.late_other, f32[192,512]{1,0:T(8,128)S(1)} %get-tuple-element.158.keep_own, ...), custom_call_target="tpu_custom_call" | custom-call | tf_op jit(solution)/shard_map/settle/pallas_call | solution.py:1130
  53.9 1.6 %collective-permute-start.16 = (bf16[112,112]{1,0:T(8,128)(2,1)S(1)}, bf16[112,112]{1,0:T(8,128)(2,1)S(1)}, u32[]{:S(2)}, u32[]{:S(2)}) collective-permute-start(bf16[112,112]{1,0:T(8,128)(2,1)S(1)} %get-tuple-element.170), channel_id=1, source_target_pairs={{0,2},{1,3},{2,0},{3,1},{4,6},{5,7},{6,4},{7,5},{8,10},{9,11},{10,... | collective-permute-start | bytes 75272 | tf_op jit(solution)/shard_map/ppermute | solution.py:1166
  55.5 2.4 %own.1 = (f32[168,112]{1,0:T(8,128)S(1)}, f32[168,112]{1,0:T(8,128)S(1)}, f32[104,168]{1,0:T(8,128)S(1)}, f32[1,32]{1,0:T(1,128)S(1)}, f32[24,16,28]{2,1,0:T(8,1...) custom-call(s32[2]{0:T(128)S(1)} %pad_add_fusion.index_ref, ...), custom_call_target="tpu_custom_call" | custom-call | tf_op jit(solution)/shard_map/own/pallas_call | solution.py:1130
  57.9 1.8 %adam.1 = (f32[24,16,28]{2,1,0:T(8,128)}, f32[168,112]{1,0:T(8,128)}, f32[168,112]{1,0:T(8,128)}, f32[168,112]{1,0:T(8,128)}, f32[2,168]{1,0:T(2,128)}, /*index=...) custom-call(s32[2]{0:T(128)S(1)} %pad_add_fusion.index_ref, ...), custom_call_target="tpu_custom_call" | custom-call | tf_op jit(solution)/shard_map/adam/pallas_call | solution.py:1130
  (35 shorter events, 5.4 us)
Async XLA Ops:
  0.7 32.5 %copy-start.3 = (f32[28]{0:T(128)S(1)}, f32[28]{0:T(128)}, u32[]{:S(2)}) copy-start(f32[28]{0:T(128)} %param.49) | copy-start | bytes 340
  2.9 21.8 %all-to-all-start = ((bf16[8,256,128]{2,1,0:T(8,128)(2,1)}), bf16[8,256,128]{2,1,0:T(8,128)(2,1)S(1)}, u32[]{:S(2)}, u32[]{:S(2)}) async-start(bf16[8,256,128]{2,1,0:T(8,128)(2,1)} %copies.1), calls=%async_computation | async-start | bytes 1048576 | tf_op jit(solution)/shard_map/all_to_all | solution.py:1178
  11.2 5.5 %collective-permute-start.1 = (bf16[336,112]{1,0:T(8,128)(2,1)S(1)}, bf16[336,112]{1,0:T(8,128)(2,1)S(1)}, u32[]{:S(2)}, u32[]{:S(2)}) collective-permute-start(bf16[336,112]{1,0:T(8,128)(2,1)S(1)} %get-tuple-element.133.matrix_0), channel_id=1, source_target_pairs={{0,2},{1,3},{2,0},{3,1},{4,6},{5,7},{6,4},{7,5},{8,10},{9,11},{10,... | collective-permute-start | bytes 225800 | tf_op jit(solution)/shard_map/ppermute | solution.py:1166
  12.8 5.1 %collective-permute-start.4 = (f32[104,168]{1,0:T(8,128)S(1)}, f32[104,168]{1,0:T(8,128)S(1)}, u32[]{:S(2)}, u32[]{:S(2)}) collective-permute-start(f32[104,168]{1,0:T(8,128)S(1)} %get-tuple-element.134.stack_0), channel_id=1, source_target_pairs={{0,2},{1,3},{2,0},{3,1},{4,6},{5,7},{6,4},{7,5},{8,10},{9,11},{10,... | collective-permute-start | bytes 209672 | tf_op jit(solution)/shard_map/ppermute | solution.py:1166
  13.3 4.8 %collective-permute-start = (bf16[336,112]{1,0:T(8,128)(2,1)S(1)}, bf16[336,112]{1,0:T(8,128)(2,1)S(1)}, u32[]{:S(2)}, u32[]{:S(2)}) collective-permute-start(bf16[336,112]{1,0:T(8,128)(2,1)S(1)} %get-tuple-element.133.matrix_0), channel_id=1, source_target_pairs={{0,1},{1,0},{2,3},{3,2},{4,5},{5,4},{6,7},{7,6},{8,9},{9,8},{10,11... | collective-permute-start | bytes 225800 | tf_op jit(solution)/shard_map/ppermute | solution.py:1166
  16.7 2.5 %collective-permute-start.2 = (bf16[336,112]{1,0:T(8,128)(2,1)S(1)}, bf16[336,112]{1,0:T(8,128)(2,1)S(1)}, u32[]{:S(2)}, u32[]{:S(2)}) collective-permute-start(bf16[336,112]{1,0:T(8,128)(2,1)S(1)} %collective-permute-done.1.matrix_2), channel_id=1, source_target_pairs={{0,1},{1,0},{2,3},{3,2},{4,5},{5,4},{6,7},{7,6},{8,9},{9,8},{10,11... | collective-permute-start | bytes 225800 | tf_op jit(solution)/shard_map/ppermute | solution.py:1166
  16.7 1.5 %collective-permute-start.3 = (f32[104,168]{1,0:T(8,128)S(1)}, f32[104,168]{1,0:T(8,128)S(1)}, u32[]{:S(2)}, u32[]{:S(2)}) collective-permute-start(f32[104,168]{1,0:T(8,128)S(1)} %get-tuple-element.134.stack_0), channel_id=1, source_target_pairs={{0,1},{1,0},{2,3},{3,2},{4,5},{5,4},{6,7},{7,6},{8,9},{9,8},{10,11... | collective-permute-start | bytes 209672 | tf_op jit(solution)/shard_map/ppermute | solution.py:1166
  17.8 1.3 %collective-permute-start.5 = (f32[104,168]{1,0:T(8,128)S(1)}, f32[104,168]{1,0:T(8,128)S(1)}, u32[]{:S(2)}, u32[]{:S(2)}) collective-permute-start(f32[104,168]{1,0:T(8,128)S(1)} %collective-permute-done.4.stack_2), channel_id=1, source_target_pairs={{0,1},{1,0},{2,3},{3,2},{4,5},{5,4},{6,7},{7,6},{8,9},{9,8},{10,11... | collective-permute-start | bytes 209672 | tf_op jit(solution)/shard_map/ppermute | solution.py:1166
  19.9 0.6 copy-start.1
  26.2 2.3 %collective-permute-start.6 = (f32[16,768]{1,0:T(8,128)S(1)}, f32[16,768]{1,0:T(8,128)S(1)}, u32[]{:S(2)}, u32[]{:S(2)}) collective-permute-start(f32[16,768]{1,0:T(8,128)S(1)} %get-tuple-element.137.sums_own), channel_id=1, source_target_pairs={{0,1},{1,0},{2,3},{3,2},{4,5},{5,4},{6,7},{7,6},{8,9},{9,8},{10,11... | collective-permute-start | bytes 147464 | tf_op jit(solution)/shard_map/ppermute | solution.py:1166
  26.2 7.0 %collective-permute-start.9 = (bf16[8,48,112]{2,1,0:T(8,128)(2,1)S(1)}, bf16[8,48,112]{2,1,0:T(8,128)(2,1)S(1)}, u32[]{:S(2)}, u32[]{:S(2)}) collective-permute-start(bf16[8,48,112]{2,1,0:T(8,128)(2,1)S(1)} %get-tuple-element.142.own_ref), channel_id=1, source_target_pairs={{0,2},{1,3},{2,0},{3,1},{4,6},{5,7},{6,4},{7,5},{8,10},{9,11},{10,... | collective-permute-start | bytes 258056 | tf_op jit(solution)/shard_map/ppermute | solution.py:1166
  27.8 5.4 %collective-permute-start.10 = (bf16[8,48,112]{2,1,0:T(8,128)(2,1)S(1)}, bf16[8,48,112]{2,1,0:T(8,128)(2,1)S(1)}, u32[]{:S(2)}, u32[]{:S(2)}) collective-permute-start(bf16[8,48,112]{2,1,0:T(8,128)(2,1)S(1)} %get-tuple-element.143), channel_id=1, source_target_pairs={{0,3},{1,2},{2,1},{3,0},{4,7},{5,6},{6,5},{7,4},{8,11},{9,10},{10,... | collective-permute-start | bytes 258056 | tf_op jit(solution)/shard_map/ppermute | solution.py:1166
  28.1 5.2 %collective-permute-start.8 = (bf16[8,48,112]{2,1,0:T(8,128)(2,1)S(1)}, bf16[8,48,112]{2,1,0:T(8,128)(2,1)S(1)}, u32[]{:S(2)}, u32[]{:S(2)}) collective-permute-start(bf16[8,48,112]{2,1,0:T(8,128)(2,1)S(1)} %get-tuple-element.143), channel_id=1, source_target_pairs={{0,1},{1,0},{2,3},{3,2},{4,5},{5,4},{6,7},{7,6},{8,9},{9,8},{10,11... | collective-permute-start | bytes 258056 | tf_op jit(solution)/shard_map/ppermute | solution.py:1166
  28.4 9.6 %copy-start.2 = (f32[2,112]{1,0:T(2,128)S(1)}, f32[2,112]{1,0:T(2,128)}, u32[]{:S(2)}) copy-start(f32[2,112]{1,0:T(2,128)} %copy-done.1) | copy-start | bytes 2692
  33.0 1.4 %collective-permute-start.7 = (f32[16,768]{1,0:T(8,128)S(1)}, f32[16,768]{1,0:T(8,128)S(1)}, u32[]{:S(2)}, u32[]{:S(2)}) collective-permute-start(f32[16,768]{1,0:T(8,128)S(1)} %get-tuple-element.140.sums_own), channel_id=1, source_target_pairs={{0,1},{1,0},{2,3},{3,2},{4,5},{5,4},{6,7},{7,6},{8,9},{9,8},{10,11... | collective-permute-start | bytes 147464 | tf_op jit(solution)/shard_map/ppermute | solution.py:1166
  36.8 1.2 %collective-permute-start.11 = (f32[32,112]{1,0:T(8,128)S(1)}, f32[32,112]{1,0:T(8,128)S(1)}, u32[]{:S(2)}, u32[]{:S(2)}) collective-permute-start(f32[32,112]{1,0:T(8,128)S(1)} %get-tuple-element.145.sums_own), channel_id=1, source_target_pairs={{0,1},{1,0},{2,3},{3,2},{4,5},{5,4},{6,7},{7,6},{8,9},{9,8},{10,11... | collective-permute-start | bytes 43016 | tf_op jit(solution)/shard_map/ppermute | solution.py:1166
  41.4 8.6 %collective-permute-start.14 = (f32[192,512]{1,0:T(8,128)S(1)}, f32[192,512]{1,0:T(8,128)S(1)}, u32[]{:S(2)}, u32[]{:S(2)}) collective-permute-start(f32[192,512]{1,0:T(8,128)S(1)} %get-tuple-element.158.keep_own), channel_id=1, source_target_pairs={{0,1},{1,0},{2,3},{3,2},{4,5},{5,4},{6,7},{7,6},{8,9},{9,8},{10,11... | collective-permute-start | bytes 1179656 | tf_op jit(solution)/shard_map/ppermute | solution.py:1166
  41.8 1.4 %collective-permute-start.12 = (f32[16,384]{1,0:T(8,128)S(1)}, f32[16,384]{1,0:T(8,128)S(1)}, u32[]{:S(2)}, u32[]{:S(2)}) collective-permute-start(f32[16,384]{1,0:T(8,128)S(1)} %get-tuple-element.152.sums_own), channel_id=1, source_target_pairs={{0,1},{1,0},{2,3},{3,2},{4,5},{5,4},{6,7},{7,6},{8,9},{9,8},{10,11... | collective-permute-start | bytes 73736 | tf_op jit(solution)/shard_map/ppermute | solution.py:1166
  48.7 1.3 %collective-permute-start.13 = (f32[48,384]{1,0:T(8,128)S(1)}, f32[48,384]{1,0:T(8,128)S(1)}, u32[]{:S(2)}, u32[]{:S(2)}) collective-permute-start(f32[48,384]{1,0:T(8,128)S(1)} %get-tuple-element.155.sums_own), channel_id=1, source_target_pairs={{0,1},{1,0},{2,3},{3,2},{4,5},{5,4},{6,7},{7,6},{8,9},{9,8},{10,11... | collective-permute-start | bytes 221192 | tf_op jit(solution)/shard_map/ppermute | solution.py:1166
  50.0 7.9 %copy-start = (bf16[28,6,4,16]{0,3,2,1:T(8,128)(2,1)S(1)}, bf16[28,6,4,16]{0,3,2,1:T(8,128)(2,1)}, u32[]{:S(2)}) copy-start(bf16[28,6,4,16]{0,3,2,1:T(8,128)(2,1)} %param.33) | copy-start | bytes 64516
  51.4 1.7 %collective-permute-start.15 = (f32[160,512]{1,0:T(8,128)S(1)}, f32[160,512]{1,0:T(8,128)S(1)}, u32[]{:S(2)}, u32[]{:S(2)}) collective-permute-start(f32[160,512]{1,0:T(8,128)S(1)} %get-tuple-element.159.late_own), channel_id=1, source_target_pairs={{0,1},{1,0},{2,3},{3,2},{4,5},{5,4},{6,7},{7,6},{8,9},{9,8},{10,11... | collective-permute-start | bytes 983048 | tf_op jit(solution)/shard_map/ppermute | solution.py:1166
  53.9 4.0 %collective-permute-start.16 = (bf16[112,112]{1,0:T(8,128)(2,1)S(1)}, bf16[112,112]{1,0:T(8,128)(2,1)S(1)}, u32[]{:S(2)}, u32[]{:S(2)}) collective-permute-start(bf16[112,112]{1,0:T(8,128)(2,1)S(1)} %get-tuple-element.170), channel_id=1, source_target_pairs={{0,2},{1,3},{2,0},{3,1},{4,6},{5,7},{6,4},{7,5},{8,10},{9,11},{10,... | collective-permute-start | bytes 75272 | tf_op jit(solution)/shard_map/ppermute | solution.py:1166

commit v6 on v5

--- a/solution.py
+++ b/solution.py
@@ -956,15 +956,43 @@
     project_ref[...] = matrix_in_order(index_ref[1], refs, channels, channels)
 
 
-def kept_sums(keep_own, keep_other, sums_own, sums_other):
+def squared(values):
+    return jnp.sum(jnp.sum(values * values, axis=0, keepdims=True), axis=1, keepdims=True)
+
+
+def own_block(position, values, channels):
+    return jnp.where(
+        position % 2 == 0, values[:, 0:channels], values[:, channels : 2 * channels]
+    )
+
+
+def early_kernel(
+    index_ref, keep_own, keep_other, project_ref, lanes_ref, bias_ref, output_ref, square_ref
+):
+    position = index_ref[1]
+    channels = project_ref.shape[0]
+    narrow = output_ref.shape[2]
+
     def both(start, stop):
         return keep_own[start:stop, 0:PAIR_LANES] + keep_other[start:stop, 0:PAIR_LANES]
 
-    return (
-        both(KEEP_PROJECT, KEEP_PROJECT + C_IN), both(0, 2 * HIDDEN_ROWS),
-        sums_own[16 : 16 + TAPS, :] + sums_other[16 : 16 + TAPS, :],
-        both(KEEP_BIASES, KEEP_BIASES + 1), both(KEEP_BIASES + 8, KEEP_BIASES + 9)[:, 0:HIDDEN_ROWS],
-    )
+    project = both(KEEP_PROJECT, KEEP_PROJECT + C_IN)
+    hidden = both(0, 2 * HIDDEN_ROWS)
+    excite_bias = both(KEEP_BIASES, KEEP_BIASES + 1)
+    bias = both(KEEP_BIASES + 8, KEEP_BIASES + 9)[:, 0:HIDDEN_ROWS]
+    total = squared(project) + squared(hidden) + squared(excite_bias)
+    square_ref[0:8, :] = jnp.broadcast_to(total, (8, 128))
+    square_ref[8:16, :] = jnp.broadcast_to(squared(bias), (8, 128))
+    bias_ref[...] = bias
+    project_ref[...] = jnp.transpose(own_block(position, project, channels))
+    lanes_ref[0 : 2 * HIDDEN_ROWS, :] = own_block(position, hidden, channels)
+    lanes_ref[2 * HIDDEN_ROWS : 2 * HIDDEN_ROWS + 1, :] = own_block(position, excite_bias, channels)
+    pick = one_hot(C_IN, narrow, lambda r, c: r == c + position * narrow).astype(bf16)
+    halves = [
+        dot(ref[:, PAIR_LANES : PAIR_LANES + C_IN].astype(bf16), pick, contract_plain)
+        for ref in (keep_own, keep_other)
+    ]
+    output_ref[...] = both_halves(position % 2 == 0, *halves).astype(bf16)
 
 
 def input_rows(late_ref):
@@ -990,21 +1018,17 @@
 
 
 def settle_kernel(
-    index_ref, late_own, late_other, keep_own, keep_other, sums_own, sums_other, three_ref, two_ref, one_ref,
+    index_ref, late_own, late_other, early_ref, sums_own, sums_other, three_ref, two_ref, one_ref,
     square_ref, packed_ref,
 ):
     position = index_ref[1]
     narrow = C_IN // 4
 
-    def squared(values):
-        return jnp.sum(jnp.sum(values * values, axis=0, keepdims=True), axis=1, keepdims=True)
-
-    project, hidden, kernel, excite_bias, bias = kept_sums(keep_own, keep_other, sums_own, sums_other)
-    total = squared(expand_sum(late_own, late_other)) + squared(project) + squared(hidden)
-    total = total + squared(kernel) + squared(excite_bias)
+    kernel = sums_own[16 : 16 + TAPS, :] + sums_other[16 : 16 + TAPS, :]
+    total = early_ref[0:1, 0:1] + squared(expand_sum(late_own, late_other)) + squared(kernel)
     total = total + squared(one_ref[...]) + squared(two_ref[...])
     square_ref[0:8, :] = jnp.broadcast_to(total, (8, 128))
-    square_ref[8:16, :] = jnp.broadcast_to(squared(bias) + squared(three_ref[...]), (8, 128))
+    square_ref[8:16, :] = jnp.broadcast_to(early_ref[8:9, 0:1] + squared(three_ref[...]), (8, 128))
     whole = both_halves(position % 2 == 0, input_rows(late_own), input_rows(late_other))
     whole = whole.reshape(4 * PACKED_ROWS, C_IN).astype(bf16)
     across = position + 2 - position // 2 * 4
@@ -1030,10 +1054,10 @@
 
 
 def own_kernel(
-    index_ref, late_own, late_other, keep_own, keep_other, sums_own, sums_other, two_ref, one_ref, *refs
+    index_ref, late_own, late_other, sums_own, sums_other, two_ref, one_ref, *refs
 ):
-    params, outs = refs[:30], refs[36:]
-    expand_ref, project_ref, lanes_ref, bias_ref, input_ref, output_ref = refs[30:36]
+    params, outs = refs[:30], refs[33:]
+    expand_ref, lanes_ref, input_ref = refs[30:33]
     for entry in range(10):
         shrink = 1.0 - step_rates[entry] * decay_flags[entry] * decay_rate
         for part, scale in enumerate((shrink, beta_first, beta_second)):
@@ -1044,31 +1068,19 @@
     narrow = C_IN // 4
 
     def mine(values):
-        return jnp.where(first, values[:, 0:channels], values[:, channels : 2 * channels])
-
-    project, hidden, kernel, excite_bias, bias = kept_sums(keep_own, keep_other, sums_own, sums_other)
-    bias_ref[...] = bias
+        return own_block(position, values, channels)
+
     expand_ref[...] = jnp.transpose(mine(expand_sum(late_own, late_other)))
-    project_ref[...] = jnp.transpose(mine(project))
-    lanes_ref[0:TAPS, :] = mine(kernel)
-    lanes_ref[ROW_SQUEEZE : ROW_SQUEEZE + 2 * HIDDEN_ROWS, :] = mine(hidden)
-    lanes_ref[ROW_EXCITE_BIAS : ROW_EXCITE_BIAS + 1, :] = mine(excite_bias)
-    lanes_ref[ROW_EXPAND_GAINS : ROW_EXPAND_GAINS + 2, :] = mine(one_ref[...])
-    lanes_ref[ROW_DEPTH_GAINS : ROW_DEPTH_GAINS + 2, :] = mine(two_ref[...])
-    pick = one_hot(C_IN, narrow, lambda r, c: r == c + position * narrow)
-    halves = [
-        highest(input_rows(ref), pick.astype(f32), contract_plain) for ref in (late_own, late_other)
-    ]
+    lanes_ref[0:TAPS, :] = mine(sums_own[16 : 16 + TAPS, :] + sums_other[16 : 16 + TAPS, :])
+    lanes_ref[32:34, :] = mine(one_ref[...])
+    lanes_ref[34:36, :] = mine(two_ref[...])
+    pick = one_hot(C_IN, narrow, lambda r, c: r == c + position * narrow).astype(f32)
+    halves = [highest(input_rows(ref), pick, contract_plain) for ref in (late_own, late_other)]
     input_ref[...] = both_halves(first, *halves)
-    halves = [
-        dot(ref[:, PAIR_LANES : PAIR_LANES + C_IN].astype(bf16), pick.astype(bf16), contract_plain)
-        for ref in (keep_own, keep_other)
-    ]
-    output_ref[...] = both_halves(first, *halves).astype(bf16)
 
 
 def adam_kernel(
-    index_ref, square_ref, expand_grad, project_grad, lanes_grad, bias_grad, three_grad,
+    index_ref, square_ref, expand_grad, project_grad, lanes_grad, early_grad, bias_grad, three_grad,
     input_own, packed_other, cot_ref, *refs,
 ):
     params, outs = refs[:30], refs[30:]
@@ -1088,13 +1100,13 @@
     pick = one_hot(C_IN, narrow, lambda r, c: r == c + index_ref[1] * narrow).astype(f32)
     gradients = (
         expand_grad[...],
-        lanes_grad[ROW_EXPAND_GAINS : ROW_EXPAND_GAINS + 2, :],
+        lanes_grad[32:34, :],
         lanes_grad[0:TAPS, :],
-        lanes_grad[ROW_DEPTH_GAINS : ROW_DEPTH_GAINS + 2, :],
-        lanes_grad[ROW_SQUEEZE : ROW_SQUEEZE + params[12].shape[0], :],
+        lanes_grad[34:36, :],
+        early_grad[0 : params[12].shape[0], :],
         bias_grad[:, 0 : params[15].shape[1]],
-        lanes_grad[ROW_EXCITE : ROW_EXCITE + params[18].shape[0], :],
-        lanes_grad[ROW_EXCITE_BIAS : ROW_EXCITE_BIAS + 1, :],
+        early_grad[HIDDEN_ROWS : HIDDEN_ROWS + params[18].shape[0], :],
+        early_grad[2 * HIDDEN_ROWS : 2 * HIDDEN_ROWS + 1, :],
         project_grad[...],
         highest(three_grad[0:2, :], pick, contract_plain),
     )
@@ -1262,7 +1274,8 @@
         ],
         name="gate_back",
     )
-    lanes_other = swap(lanes_grad, 1)
+    two_other, lanes_late = lax.optimization_barrier((swap(sums, 1), lanes_grad))
+    lanes_other = swap(lanes_late, 1)
     one, sums, two_grad = call(
         functools.partial(depth_back_kernel, total_rows),
         [
@@ -1271,7 +1284,7 @@
             ((2, PAIR_LANES), f32),
         ],
         [
-            index, sums, swap(sums, 1), two, depth, expanded, stack_all, norm_one, norm_two,
+            index, sums, two_other, two, depth, expanded, stack_all, norm_one, norm_two,
         ],
         [
             ((KS * PRODUCTS, 8, PAIR_LANES), f32),
@@ -1292,25 +1305,34 @@
         name="expand_back",
     )
     late_pair = [late, swap(late, 1)]
-    keep_pair = [lanes_grad, lanes_other, sums, sums_other]
+    kernel_pair = [sums, sums_other]
+    project_own, lanes_early, bias_own, block_output, square_early = call(
+        early_kernel,
+        [
+            ((channels, C_IN), f32),
+            ((2 * HIDDEN_ROWS + 8, channels), f32),
+            ((1, HIDDEN_ROWS), f32),
+            ((POSITIONS, segments, narrow), bf16, False),
+            ((16, 128), f32),
+        ],
+        [index, lanes_late, lanes_other],
+        name="early",
+    )
     square, packed = call(
         settle_kernel,
         [((16, 128), f32), ((PACKED_ROWS + 16, C_IN), bf16)],
-        [index, *late_pair, *keep_pair, three_grad, two_grad, one_grad],
+        [index, *late_pair, square_early, *kernel_pair, three_grad, two_grad, one_grad],
         name="settle",
     )
-    expand_own, project_own, lanes_own, bias_own, input_own, block_output, *scaled_params = call(
+    expand_own, lanes_own, input_own, *scaled_params = call(
         own_kernel,
         [
             ((channels, C_IN), f32),
-            ((channels, C_IN), f32),
-            ((STACK_ROWS, channels), f32),
-            ((1, HIDDEN_ROWS), f32),
+            ((40, channels), f32),
             ((POSITIONS, segments, narrow), f32),
-            ((POSITIONS, segments, narrow), bf16, False),
             *[(value.shape, f32) for value in params],
         ],
-        [index, *late_pair, *keep_pair, two_grad, one_grad],
+        [index, *late_pair, *kernel_pair, two_grad, one_grad],
         name="own",
         plain=params,
     )
@@ -1320,7 +1342,7 @@
         + [(value.shape, f32) for value in params]
         + [((1, 1), f32)],
         [
-            index, square, expand_own, project_own, lanes_own, bias_own, three_grad,
+            index, square, expand_own, project_own, lanes_own, lanes_early, bias_own, three_grad,
             input_own, swap(packed, 2), cot_rows, *scaled_params,
         ],
         name="adam",

time: 60.1 us -> 59.6 us (level)
  waiting for transfers between devices: 13.9 us -> 13.1 us
    ppermute x17, waiting for transfers between devices: 9.63 us -> 8.83 us  [swap(): return lax.ppermute(values, 'chan', [(at, at ^ mask) for at in range(4)])]
    pallas_call x13 -> x14, Pallas kernels: 28.6 us -> 29.2 us  [call(): pl.pallas_call(kernel, out_shape=[(jax.ShapeDtypeStruct if out[2:] else m...]
  transfers between devices with their start and end apart: 18 -> 18, of which waited for: 9 -> 10; matrix products, arithmetic and copies ran while one was open for 0% -> 0% of each run, Pallas kernels for 25% -> 27%
where the time goes in v6:
time: 59.6 us; the launch traced here: 59.3 us
  Pallas kernels  29.2 us (49%)
  starting transfers between devices  15.6 us (26%)
  waiting for transfers between devices  13.1 us (22%)
  between operations  0.83 us (1%)
    pallas_call x14, Pallas kernels, call(): pl.pallas_call(kernel, out_shape=[(jax.ShapeDtypeStruct if out[2:] else m...  29.2 us
    ppermute x17, waiting for transfers between devices, swap(): return lax.ppermute(values, 'chan', [(at, at ^ mask) for at in range(4)])  8.83 us
    ppermute x17, starting transfers between devices, swap(): return lax.ppermute(values, 'chan', [(at, at ^ mask) for at in range(4)])  8.3 us
    all_to_all x1, starting transfers between devices, on_device_paired(): x = lax.all_to_all(copies, 'dp', 0, 0)  7.28 us
    all_to_all x1, waiting for transfers between devices, on_device_paired(): x = lax.all_to_all(copies, 'dp', 0, 0)  4.24 us
  transfers between devices with their start and end apart: 18, of which 10 were waited for; matrix products, arithmetic and copies ran while one was open for 0% of the time, Pallas kernels for 27%

profile of v6, /device:TPU:0, one launch (start us, length us, event | category | flops | bytes accessed | tf_op | source)
XLA Modules:
  0.0 59.3 jit_solution(17326769171753500254)
XLA Ops:
  0.8 2.1 %copies.1 = bf16[8,256,128]{2,1,0:T(8,128)(2,1)} custom-call(s32[2]{0:T(128)S(1)} %pad_add_fusion.index_ref, bf16[24,16,112]{2,1,0:T(8,128)(2,1)} %bitcast.37, bf16[24,16,28]{2,1,0:T(8,128)(2,1)} %bitcast.33), custom_call_target="tpu_custom_call" | custom-call | tf_op jit(solution)/shard_map/copies/pallas_call | solution.py:1142
  2.9 7.3 %all-to-all-start = ((bf16[8,256,128]{2,1,0:T(8,128)(2,1)}), bf16[8,256,128]{2,1,0:T(8,128)(2,1)S(1)}, u32[]{:S(2)}, u32[]{:S(2)}) async-start(bf16[8,256,128]{2,1,0:T(8,128)(2,1)} %copies.1), calls=%async_computation | async-start | bytes 1048576 | tf_op jit(solution)/shard_map/all_to_all | solution.py:1190
  10.2 1.0 %pack.1 = (f32[104,168]{1,0:T(8,128)S(1)}, bf16[336,112]{1,0:T(8,128)(2,1)S(1)}) custom-call(f32[168,112]{1,0:T(8,128)} %refs_0_.1, f32[168,112]{1,0:T(8,128)} %bitcast.35, f32[25,168]{1,0:T(8,128)} %refs_6_.1, f32[28,168]{1,0:T(8,128)} %refs_12_.1, f32[28,168]{1,0:T(8,128)} %refs_18_.1, f32[1,168]{1,0:T(1,128)} %bitcast.40, f32[2,168]{1,0:T(2,128)} %refs_3_.1, ...), custom_call_target="tpu_custom_call" | custom-call | tf_op jit(solution)/shard_map/pack/pallas_call | solution.py:1142
  11.2 1.6 %collective-permute-start.1 = (bf16[336,112]{1,0:T(8,128)(2,1)S(1)}, bf16[336,112]{1,0:T(8,128)(2,1)S(1)}, u32[]{:S(2)}, u32[]{:S(2)}) collective-permute-start(bf16[336,112]{1,0:T(8,128)(2,1)S(1)} %get-tuple-element.137.matrix_0), channel_id=1, source_target_pairs={{0,2},{1,3},{2,0},{3,1},{4,6},{5,7},{6,4},{7,5},{8,10},{9,11},{10,... | collective-permute-start | bytes 225800 | tf_op jit(solution)/shard_map/ppermute | solution.py:1178
  13.3 3.4 %collective-permute-done.1.matrix_2 = bf16[336,112]{1,0:T(8,128)(2,1)S(1)} collective-permute-done((bf16[336,112]{1,0:T(8,128)(2,1)S(1)}, bf16[336,112]{1,0:T(8,128)(2,1)S(1)}, u32[]{:S(2)}, u32[]{:S(2)}) %collective-permute-start.1) | collective-permute-done | bytes 75296 | tf_op jit(solution)/shard_map/ppermute | solution.py:1178
  18.1 1.0 %collective-permute-done.5.stack_3 = f32[104,168]{1,0:T(8,128)S(1)} collective-permute-done((f32[104,168]{1,0:T(8,128)S(1)}, f32[104,168]{1,0:T(8,128)S(1)}, u32[]{:S(2)}, u32[]{:S(2)}) %collective-permute-start.5) | collective-permute-done | bytes 69920 | tf_op jit(solution)/shard_map/ppermute | solution.py:1178
  19.1 0.7 %assemble.1 = (f32[104,768]{1,0:T(8,128)S(1)}, bf16[768,112]{1,0:T(8,128)(2,1)S(1)}, f32[2,112]{1,0:T(2,128)S(1)}) custom-call(s32[2]{0:T(128)S(1)} %pad_add_fusion.index_ref, f32[104,168]{1,0:T(8,128)S(1)} %get-tuple-element.138.stack_0, f32[104,168]{1,0:T(8,128)S(1)} %collective-permute-done.3.stack_1, f32[104,168]{1,0:T(8,128)S(1)} %collective-permute-done.4.stack_2, ...), custom_call_target="tpu_custom_call" | custom-call | tf_op jit(solution)/shard_map/assemble/pallas_call | solution.py:1142
  20.4 4.2 %all-to-all-done.x_ref = bf16[8,256,128]{2,1,0:T(8,128)(2,1)S(1)} async-done(((bf16[8,256,128]{2,1,0:T(8,128)(2,1)}), bf16[8,256,128]{2,1,0:T(8,128)(2,1)S(1)}, u32[]{:S(2)}, u32[]{:S(2)}) %all-to-all-start) | async-done | bytes 524320 | tf_op jit(solution)/shard_map/all_to_all | solution.py:1190
  24.7 1.5 %first.1 = (f32[8,192,768]{2,1,0:T(8,128)S(1)}, f32[16,768]{1,0:T(8,128)S(1)}, bf16[768,112]{1,0:T(8,128)(2,1)S(1)}, bf16[8,48,112]{2,1,0:T(8,128)(2,1)S(1)}, bf16[8,48,112]{2,1,0:T(8,128)(2,1)S(1)}) custom-call(s32[2]{0:T(128)S(1)} %pad_add_fusion.index_ref, bf16[336,112]{1,0:T(8,128)(2,1)S(1)} %get-tuple-element.137.matrix_0, ...), custom_call_target="tpu_custom_call" | custom-call | tf_op jit(solution)/shard_map/first/pallas_call | solution.py:1142
  26.2 1.6 %collective-permute-start.9 = (bf16[8,48,112]{2,1,0:T(8,128)(2,1)S(1)}, bf16[8,48,112]{2,1,0:T(8,128)(2,1)S(1)}, u32[]{:S(2)}, u32[]{:S(2)}) collective-permute-start(bf16[8,48,112]{2,1,0:T(8,128)(2,1)S(1)} %get-tuple-element.146.own_ref), channel_id=1, source_target_pairs={{0,2},{1,3},{2,0},{3,1},{4,6},{5,7},{6,4},{7,5},{8,10},{9,11},{10,... | collective-permute-start | bytes 258056 | tf_op jit(solution)/shard_map/ppermute | solution.py:1178
  28.5 4.5 %expand.1 = (f32[8,192,768]{2,1,0:T(8,128)S(1)}, f32[16,768]{1,0:T(8,128)S(1)}, f32[32,768]{1,0:T(8,128)S(1)}) custom-call(f32[8,192,768]{2,1,0:T(8,128)S(1)} %get-tuple-element.140.expanded_ref, f32[16,768]{1,0:T(8,128)S(1)} %get-tuple-element.141.sums_own, f32[16,768]{1,0:T(8,128)S(1)} %collective-permute-done.6.sums_other, ...), custom_call_target="tpu_custom_call" | custom-call | tf_op jit(solution)/shard_map/expand/pallas_call | solution.py:1142
  33.3 1.1 %cot.1.cot_ref = bf16[8,192,112]{2,1,0:T(8,128)(2,1)S(1)} custom-call(s32[2]{0:T(128)S(1)} %pad_add_fusion.index_ref, bf16[8,48,112]{2,1,0:T(8,128)(2,1)S(1)} %get-tuple-element.146.own_ref, bf16[8,48,112]{2,1,0:T(8,128)(2,1)S(1)} %collective-permute-done.8.near_ref, bf16[8,48,112]{2,1,0:T(8,128)(2,1)S(1)} %collective-permute-done.9.far_ref, ...), custom_call_target="tpu_custom_call" | custom-call | tf_op jit(solution)/shard_map/cot/pallas_call | solution.py:1142
  34.4 2.4 %squeeze.29 = (f32[8,192,112]{2,1,0:T(8,128)S(1)}, bf16[8,192,768]{2,1,0:T(8,128)(2,1)S(1)}, f32[32,112]{1,0:T(8,128)S(1)}, f32[64,768]{1,0:T(8,128)S(1)}, f32[6...) custom-call(f32[8,192,768]{2,1,0:T(8,128)S(1)} %get-tuple-element.143.depth_ref, ...), custom_call_target="tpu_custom_call" | custom-call | tf_op jit(solution)/shard_map/squeeze/pallas_call | solution.py:1142
  37.2 0.8 %collective-permute-done.11.sums_other = f32[32,112]{1,0:T(8,128)S(1)} collective-permute-done((f32[32,112]{1,0:T(8,128)S(1)}, f32[32,112]{1,0:T(8,128)S(1)}, u32[]{:S(2)}, u32[]{:S(2)}) %collective-permute-start.11) | collective-permute-done | bytes 14368 | tf_op jit(solution)/shard_map/ppermute | solution.py:1178
  38.0 3.3 %gate_back.1 = (f32[8,192,384]{2,1,0:T(8,128)S(1)}, f32[16,384]{1,0:T(8,128)S(1)}, f32[192,512]{1,0:T(8,128)S(1)}, f32[2,112]{1,0:T(2,128)S(1)}) custom-call(s32[2]{0:T(128)S(1)} %pad_add_fusion.index_ref, f32[8,192,112]{2,1,0:T(8,128)S(1)} %get-tuple-element.148.projected_ref, bf16[8,192,112]{2,1,0:T(8,128)(2,1)S(1)} %cot.1.cot_ref, ...), custom_call_target="tpu_custom_call" | custom-call | tf_op jit(solution)/shard_map/gate_back/pallas_call | solution.py:1142
  41.8 0.9 %collective-permute-done.12.sums_other = f32[16,384]{1,0:T(8,128)S(1)} collective-permute-done((f32[16,384]{1,0:T(8,128)S(1)}, f32[16,384]{1,0:T(8,128)S(1)}, u32[]{:S(2)}, u32[]{:S(2)}) %collective-permute-start.12) | collective-permute-done | bytes 24608 | tf_op jit(solution)/shard_map/ppermute | solution.py:1178
  43.0 5.5 %depth_back.1 = (f32[8,192,384]{2,1,0:T(8,128)S(1)}, f32[48,384]{1,0:T(8,128)S(1)}, f32[2,384]{1,0:T(2,128)S(1)}) custom-call(s32[2]{0:T(128)S(1)} %pad_add_fusion.index_ref, f32[16,384]{1,0:T(8,128)S(1)} %get-tuple-element.156.sums_own, f32[16,384]{1,0:T(8,128)S(1)} %collective-permute-done.12.sums_other, f32[8,192,384]{2,1,0:T(8,128)S(1)} %get-tuple-element.161.two_ref, ...), custom_call_target="tpu_custom_call" | custom-call | tf_op jit(solution)/shard_map/depth_back/pallas_call | solution.py:1142
  48.7 1.1 %collective-permute-done.14.sums_other = f32[48,384]{1,0:T(8,128)S(1)} collective-permute-done((f32[48,384]{1,0:T(8,128)S(1)}, f32[48,384]{1,0:T(8,128)S(1)}, u32[]{:S(2)}, u32[]{:S(2)}) %collective-permute-start.14) | collective-permute-done | bytes 73760 | tf_op jit(solution)/shard_map/ppermute | solution.py:1178
  49.8 1.4 %expand_back.1 = (f32[160,512]{1,0:T(8,128)S(1)}, f32[2,384]{1,0:T(2,128)S(1)}) custom-call(s32[2]{0:T(128)S(1)} %pad_add_fusion.index_ref, f32[48,384]{1,0:T(8,128)S(1)} %get-tuple-element.163.sums_own, f32[48,384]{1,0:T(8,128)S(1)} %collective-permute-done.14.sums_other, f32[8,192,384]{2,1,0:T(8,128)S(1)} %get-tuple-element.164.one_ref, ...), custom_call_target="tpu_custom_call" | custom-call | tf_op jit(solution)/shard_map/expand_back/pallas_call | solution.py:1142
  51.4 1.4 %early.1 = (f32[168,112]{1,0:T(8,128)S(1)}, f32[72,168]{1,0:T(8,128)S(1)}, f32[1,32]{1,0:T(1,128)S(1)}, bf16[24,16,28]{2,1,0:T(8,128)(2,1)}, f32[16,128]{1,0:T(8,128)S(1)}) custom-call(s32[2]{0:T(128)S(1)} %pad_add_fusion.index_ref, f32[192,512]{1,0:T(8,128)S(1)} %get-tuple-element.158.keep_own, f32[192,512]{1,0:T(8,128)S(1)} %collective-permute-done.13.keep_other._lanes_ref), custom_call_target="tpu_custom_call" | custom-call | tf_op jit(solution)/shard_map/early/pallas_call | solution.py:1142
  52.9 0.8 %settle.1 = (f32[16,128]{1,0:T(8,128)S(1)}, bf16[112,112]{1,0:T(8,128)(2,1)S(1)}) custom-call(s32[2]{0:T(128)S(1)} %pad_add_fusion.index_ref, f32[160,512]{1,0:T(8,128)S(1)} %get-tuple-element.166.late_own, f32[160,512]{1,0:T(8,128)S(1)} %collective-permute-done.15.late_other, f32[16,128]{1,0:T(8,128)S(1)} %get-tuple-element.167.early_ref, ...), custom_call_target="tpu_custom_call" | custom-call | tf_op jit(solution)/shard_map/settle/pallas_call | solution.py:1142
  53.6 1.6 %collective-permute-start.16 = (bf16[112,112]{1,0:T(8,128)(2,1)S(1)}, bf16[112,112]{1,0:T(8,128)(2,1)S(1)}, u32[]{:S(2)}, u32[]{:S(2)}) collective-permute-start(bf16[112,112]{1,0:T(8,128)(2,1)S(1)} %get-tuple-element.178), channel_id=1, source_target_pairs={{0,2},{1,3},{2,0},{3,1},{4,6},{5,7},{6,4},{7,5},{8,10},{9,11},{10,... | collective-permute-start | bytes 75272 | tf_op jit(solution)/shard_map/ppermute | solution.py:1178
  55.2 1.7 %own.1 = (f32[168,112]{1,0:T(8,128)S(1)}, f32[40,168]{1,0:T(8,128)S(1)}, f32[24,16,28]{2,1,0:T(8,128)S(1)}, f32[168,112]{1,0:T(8,128)S(1)}, f32[168,112]{1,0:T(8...) custom-call(s32[2]{0:T(128)S(1)} %pad_add_fusion.index_ref, ...), custom_call_target="tpu_custom_call" | custom-call | tf_op jit(solution)/shard_map/own/pallas_call | solution.py:1142
  57.6 1.7 %adam.1 = (f32[24,16,28]{2,1,0:T(8,128)}, f32[168,112]{1,0:T(8,128)}, f32[168,112]{1,0:T(8,128)}, f32[168,112]{1,0:T(8,128)}, f32[2,168]{1,0:T(2,128)}, /*index=...) custom-call(s32[2]{0:T(128)S(1)} %pad_add_fusion.index_ref, ...), custom_call_target="tpu_custom_call" | custom-call | tf_op jit(solution)/shard_map/adam/pallas_call | solution.py:1142
  (36 shorter events, 5.9 us)
Async XLA Ops:
  0.7 32.5 %copy-start.3 = (f32[28]{0:T(128)S(1)}, f32[28]{0:T(128)}, u32[]{:S(2)}) copy-start(f32[28]{0:T(128)} %param.49) | copy-start | bytes 340
  2.9 21.8 %all-to-all-start = ((bf16[8,256,128]{2,1,0:T(8,128)(2,1)}), bf16[8,256,128]{2,1,0:T(8,128)(2,1)S(1)}, u32[]{:S(2)}, u32[]{:S(2)}) async-start(bf16[8,256,128]{2,1,0:T(8,128)(2,1)} %copies.1), calls=%async_computation | async-start | bytes 1048576 | tf_op jit(solution)/shard_map/all_to_all | solution.py:1190
  11.2 5.5 %collective-permute-start.1 = (bf16[336,112]{1,0:T(8,128)(2,1)S(1)}, bf16[336,112]{1,0:T(8,128)(2,1)S(1)}, u32[]{:S(2)}, u32[]{:S(2)}) collective-permute-start(bf16[336,112]{1,0:T(8,128)(2,1)S(1)} %get-tuple-element.137.matrix_0), channel_id=1, source_target_pairs={{0,2},{1,3},{2,0},{3,1},{4,6},{5,7},{6,4},{7,5},{8,10},{9,11},{10,... | collective-permute-start | bytes 225800 | tf_op jit(solution)/shard_map/ppermute | solution.py:1178
  12.8 5.1 %collective-permute-start.4 = (f32[104,168]{1,0:T(8,128)S(1)}, f32[104,168]{1,0:T(8,128)S(1)}, u32[]{:S(2)}, u32[]{:S(2)}) collective-permute-start(f32[104,168]{1,0:T(8,128)S(1)} %get-tuple-element.138.stack_0), channel_id=1, source_target_pairs={{0,2},{1,3},{2,0},{3,1},{4,6},{5,7},{6,4},{7,5},{8,10},{9,11},{10,... | collective-permute-start | bytes 209672 | tf_op jit(solution)/shard_map/ppermute | solution.py:1178
  13.3 4.8 %collective-permute-start = (bf16[336,112]{1,0:T(8,128)(2,1)S(1)}, bf16[336,112]{1,0:T(8,128)(2,1)S(1)}, u32[]{:S(2)}, u32[]{:S(2)}) collective-permute-start(bf16[336,112]{1,0:T(8,128)(2,1)S(1)} %get-tuple-element.137.matrix_0), channel_id=1, source_target_pairs={{0,1},{1,0},{2,3},{3,2},{4,5},{5,4},{6,7},{7,6},{8,9},{9,8},{10,11... | collective-permute-start | bytes 225800 | tf_op jit(solution)/shard_map/ppermute | solution.py:1178
  16.7 2.5 %collective-permute-start.2 = (bf16[336,112]{1,0:T(8,128)(2,1)S(1)}, bf16[336,112]{1,0:T(8,128)(2,1)S(1)}, u32[]{:S(2)}, u32[]{:S(2)}) collective-permute-start(bf16[336,112]{1,0:T(8,128)(2,1)S(1)} %collective-permute-done.1.matrix_2), channel_id=1, source_target_pairs={{0,1},{1,0},{2,3},{3,2},{4,5},{5,4},{6,7},{7,6},{8,9},{9,8},{10,11... | collective-permute-start | bytes 225800 | tf_op jit(solution)/shard_map/ppermute | solution.py:1178
  16.7 1.5 %collective-permute-start.3 = (f32[104,168]{1,0:T(8,128)S(1)}, f32[104,168]{1,0:T(8,128)S(1)}, u32[]{:S(2)}, u32[]{:S(2)}) collective-permute-start(f32[104,168]{1,0:T(8,128)S(1)} %get-tuple-element.138.stack_0), channel_id=1, source_target_pairs={{0,1},{1,0},{2,3},{3,2},{4,5},{5,4},{6,7},{7,6},{8,9},{9,8},{10,11... | collective-permute-start | bytes 209672 | tf_op jit(solution)/shard_map/ppermute | solution.py:1178
  17.8 1.3 %collective-permute-start.5 = (f32[104,168]{1,0:T(8,128)S(1)}, f32[104,168]{1,0:T(8,128)S(1)}, u32[]{:S(2)}, u32[]{:S(2)}) collective-permute-start(f32[104,168]{1,0:T(8,128)S(1)} %collective-permute-done.4.stack_2), channel_id=1, source_target_pairs={{0,1},{1,0},{2,3},{3,2},{4,5},{5,4},{6,7},{7,6},{8,9},{9,8},{10,11... | collective-permute-start | bytes 209672 | tf_op jit(solution)/shard_map/ppermute | solution.py:1178
  19.9 0.6 copy-start.1
  26.2 2.3 %collective-permute-start.6 = (f32[16,768]{1,0:T(8,128)S(1)}, f32[16,768]{1,0:T(8,128)S(1)}, u32[]{:S(2)}, u32[]{:S(2)}) collective-permute-start(f32[16,768]{1,0:T(8,128)S(1)} %get-tuple-element.141.sums_own), channel_id=1, source_target_pairs={{0,1},{1,0},{2,3},{3,2},{4,5},{5,4},{6,7},{7,6},{8,9},{9,8},{10,11... | collective-permute-start | bytes 147464 | tf_op jit(solution)/shard_map/ppermute | solution.py:1178
  26.2 7.0 %collective-permute-start.9 = (bf16[8,48,112]{2,1,0:T(8,128)(2,1)S(1)}, bf16[8,48,112]{2,1,0:T(8,128)(2,1)S(1)}, u32[]{:S(2)}, u32[]{:S(2)}) collective-permute-start(bf16[8,48,112]{2,1,0:T(8,128)(2,1)S(1)} %get-tuple-element.146.own_ref), channel_id=1, source_target_pairs={{0,2},{1,3},{2,0},{3,1},{4,6},{5,7},{6,4},{7,5},{8,10},{9,11},{10,... | collective-permute-start | bytes 258056 | tf_op jit(solution)/shard_map/ppermute | solution.py:1178
  27.8 5.4 %collective-permute-start.10 = (bf16[8,48,112]{2,1,0:T(8,128)(2,1)S(1)}, bf16[8,48,112]{2,1,0:T(8,128)(2,1)S(1)}, u32[]{:S(2)}, u32[]{:S(2)}) collective-permute-start(bf16[8,48,112]{2,1,0:T(8,128)(2,1)S(1)} %get-tuple-element.147), channel_id=1, source_target_pairs={{0,3},{1,2},{2,1},{3,0},{4,7},{5,6},{6,5},{7,4},{8,11},{9,10},{10,... | collective-permute-start | bytes 258056 | tf_op jit(solution)/shard_map/ppermute | solution.py:1178
  28.1 5.1 %collective-permute-start.8 = (bf16[8,48,112]{2,1,0:T(8,128)(2,1)S(1)}, bf16[8,48,112]{2,1,0:T(8,128)(2,1)S(1)}, u32[]{:S(2)}, u32[]{:S(2)}) collective-permute-start(bf16[8,48,112]{2,1,0:T(8,128)(2,1)S(1)} %get-tuple-element.147), channel_id=1, source_target_pairs={{0,1},{1,0},{2,3},{3,2},{4,5},{5,4},{6,7},{7,6},{8,9},{9,8},{10,11... | collective-permute-start | bytes 258056 | tf_op jit(solution)/shard_map/ppermute | solution.py:1178
  28.5 9.6 %copy-start.2 = (f32[2,112]{1,0:T(2,128)S(1)}, f32[2,112]{1,0:T(2,128)}, u32[]{:S(2)}) copy-start(f32[2,112]{1,0:T(2,128)} %copy-done.1) | copy-start | bytes 2692
  33.0 1.4 %collective-permute-start.7 = (f32[16,768]{1,0:T(8,128)S(1)}, f32[16,768]{1,0:T(8,128)S(1)}, u32[]{:S(2)}, u32[]{:S(2)}) collective-permute-start(f32[16,768]{1,0:T(8,128)S(1)} %get-tuple-element.144.sums_own), channel_id=1, source_target_pairs={{0,1},{1,0},{2,3},{3,2},{4,5},{5,4},{6,7},{7,6},{8,9},{9,8},{10,11... | collective-permute-start | bytes 147464 | tf_op jit(solution)/shard_map/ppermute | solution.py:1178
  36.8 1.3 %collective-permute-start.11 = (f32[32,112]{1,0:T(8,128)S(1)}, f32[32,112]{1,0:T(8,128)S(1)}, u32[]{:S(2)}, u32[]{:S(2)}) collective-permute-start(f32[32,112]{1,0:T(8,128)S(1)} %get-tuple-element.149.sums_own), channel_id=1, source_target_pairs={{0,1},{1,0},{2,3},{3,2},{4,5},{5,4},{6,7},{7,6},{8,9},{9,8},{10,11... | collective-permute-start | bytes 43016 | tf_op jit(solution)/shard_map/ppermute | solution.py:1178
  41.4 1.3 %collective-permute-start.12 = (f32[16,384]{1,0:T(8,128)S(1)}, f32[16,384]{1,0:T(8,128)S(1)}, u32[]{:S(2)}, u32[]{:S(2)}) collective-permute-start(f32[16,384]{1,0:T(8,128)S(1)} %get-tuple-element.156.sums_own), channel_id=1, source_target_pairs={{0,1},{1,0},{2,3},{3,2},{4,5},{5,4},{6,7},{7,6},{8,9},{9,8},{10,11... | collective-permute-start | bytes 73736 | tf_op jit(solution)/shard_map/ppermute | solution.py:1178
  42.6 7.1 %collective-permute-start.13 = (f32[192,512]{1,0:T(8,128)S(1)}, f32[192,512]{1,0:T(8,128)S(1)}, u32[]{:S(2)}, u32[]{:S(2)}) collective-permute-start(f32[192,512]{1,0:T(8,128)S(1)} %get-tuple-element.158.keep_own), channel_id=1, source_target_pairs={{0,1},{1,0},{2,3},{3,2},{4,5},{5,4},{6,7},{7,6},{8,9},{9,8},{10,11... | collective-permute-start | bytes 1179656 | tf_op jit(solution)/shard_map/ppermute | solution.py:1178
  48.4 1.3 %collective-permute-start.14 = (f32[48,384]{1,0:T(8,128)S(1)}, f32[48,384]{1,0:T(8,128)S(1)}, u32[]{:S(2)}, u32[]{:S(2)}) collective-permute-start(f32[48,384]{1,0:T(8,128)S(1)} %get-tuple-element.163.sums_own), channel_id=1, source_target_pairs={{0,1},{1,0},{2,3},{3,2},{4,5},{5,4},{6,7},{7,6},{8,9},{9,8},{10,11... | collective-permute-start | bytes 221192 | tf_op jit(solution)/shard_map/ppermute | solution.py:1178
  49.8 7.8 %copy-start = (bf16[28,6,4,16]{0,3,2,1:T(8,128)(2,1)S(1)}, bf16[28,6,4,16]{0,3,2,1:T(8,128)(2,1)}, u32[]{:S(2)}) copy-start(bf16[28,6,4,16]{0,3,2,1:T(8,128)(2,1)} %param.33) | copy-start | bytes 64516
  51.2 1.7 %collective-permute-start.15 = (f32[160,512]{1,0:T(8,128)S(1)}, f32[160,512]{1,0:T(8,128)S(1)}, u32[]{:S(2)}, u32[]{:S(2)}) collective-permute-start(f32[160,512]{1,0:T(8,128)S(1)} %get-tuple-element.166.late_own), channel_id=1, source_target_pairs={{0,1},{1,0},{2,3},{3,2},{4,5},{5,4},{6,7},{7,6},{8,9},{9,8},{10,11... | collective-permute-start | bytes 983048 | tf_op jit(solution)/shard_map/ppermute | solution.py:1178
  53.6 3.9 %collective-permute-start.16 = (bf16[112,112]{1,0:T(8,128)(2,1)S(1)}, bf16[112,112]{1,0:T(8,128)(2,1)S(1)}, u32[]{:S(2)}, u32[]{:S(2)}) collective-permute-start(bf16[112,112]{1,0:T(8,128)(2,1)S(1)} %get-tuple-element.178), channel_id=1, source_target_pairs={{0,2},{1,3},{2,0},{3,1},{4,6},{5,7},{6,4},{7,5},{8,10},{9,11},{10,... | collective-permute-start | bytes 75272 | tf_op jit(solution)/shard_map/ppermute | solution.py:1178
